TPU v7x, 32 devices: a whole 2x2x4 slice. The times are simulated.
32 devices in a mesh: dp: 8 (over z, x), tensor: 4 (over y, core).
Axes of the slice: x: 2, y: 2, z: 4, core: 2. Of those that a mesh axis runs over, the one named last changes fastest.
Arguments:
- tokens: bfloat16 [8192, 2048], P('dp'), may hold values from -12 to 12, as said below
- attention_gain: bfloat16 [2048], P('dp'), may hold values from 0.5 to 1.5
- query_matrix: bfloat16 [2048, 2048], P('dp', 'tensor'), may hold values from -2 to 2, as said below
- key_matrix: bfloat16 [2048, 512], P('dp', 'tensor'), may hold values from -2 to 2, as said below
- value_matrix: bfloat16 [2048, 512], P('dp', 'tensor'), may hold values from -0.125 to 0.125
- output_weight: bfloat16 [2048, 2048], P('tensor', 'dp'), may hold values from -0.5 to 0.5
- feed_gain: bfloat16 [2048], P('dp'), may hold values from 0.5 to 1.5
- gate_weight: bfloat16 [2048, 8192], P('dp', 'tensor'), may hold values from -0.125 to 0.125
- up_weight: bfloat16 [2048, 8192], P('dp', 'tensor'), may hold values from -0.125 to 0.125
- down_weight: bfloat16 [8192, 2048], P('tensor', 'dp'), may hold values from -0.0625 to 0.0625
- sequence_lengths: int32 [8, 8], P('dp'), may hold values from 0 to 1024, as said below
- block_mask: int32 [64, 8], P('dp'), may hold values from 0 to 1, as said below
- cotangent: bfloat16 [8192, 2048], P('dp'), may hold values from -6 to 6
Outputs:
- block_output: bfloat16 [8192, 2048], P('dp')
- input_grad: float32 [8192, 2048], P('dp')
- attention_gain_grad: float32 [2048], P('dp')
- query_grad: float32 [2048, 2048], P('dp', 'tensor')
- key_grad: float32 [2048, 512], P('dp', 'tensor')
- value_grad: float32 [2048, 512], P('dp', 'tensor')
- output_grad: float32 [2048, 2048], P('tensor', 'dp')
- feed_gain_grad: float32 [2048], P('dp')
- gate_grad: float32 [2048, 8192], P('dp', 'tensor')
- up_grad: float32 [2048, 8192], P('dp', 'tensor')
- down_grad: float32 [8192, 2048], P('tensor', 'dp')
Inputs may be any that keep to these rules, and one draw needn't show every extreme that they name: `sequence_lengths`: row d lists, in order, the lengths of the sequences packed into the token slots of index d of dp: nonzero lengths of 128 or more come first, zeros fill the rest, and the sequences' whole blocks of 128 slots together are at most 8. `block_mask`: entry (d * 8 + i, j) is 1 exactly where query block i and key block j of index d of dp lie in the same sequence and j <= i. `tokens`: real values of the layer's input. `query_matrix`: real values of the query projection. `key_matrix`: real values of the key projection.
All inputs are finite; a program needn't handle non-finite values.
Results may differ from a plain program's by a relative error of at most 0.024.
Values may be sent and summed in bfloat16 or wider, within the bound.
A program may use at most 256 MiB of HBM per device.

v0:
```python
import jax
import jax.numpy as jnp
from jax import lax
from jax.sharding import PartitionSpec as P

HEAD_SIZE = 64
BLOCK = 128


EPS_NORM = 1e-05
THETA_BASE = 500000.0
NEG_FILL = -1e30


def token_layout(lengths_row, total, block):
    blocks_per = (lengths_row + block - 1) // block
    offsets = jnp.cumsum(blocks_per) - blocks_per
    first_token = offsets * block
    indices = jnp.arange(total, dtype=jnp.int32)
    member = (indices[:, None] >= first_token[None, :]) & (blocks_per[None, :] > 0)
    sequence = jnp.sum(member.astype(jnp.int32), axis=1) - 1
    select = sequence[:, None] == jnp.arange(lengths_row.shape[0], dtype=jnp.int32)[None, :]
    begins = jnp.sum(jnp.where(select, first_token[None, :], 0), axis=1)
    limits = jnp.sum(jnp.where(select, lengths_row[None, :], 0), axis=1)
    position = indices - begins
    return (sequence, position, position < limits)


def allowed_pairs(sequence, position, valid, mask_blocks, begin_row, rows, block):
    total = sequence.shape[0]
    blocks_all = total // block
    query_seq = sequence[begin_row : begin_row + rows]
    query_pos = position[begin_row : begin_row + rows]
    mask_rows = mask_blocks[begin_row // block : (begin_row + rows) // block]
    tiled = jnp.broadcast_to(
        mask_rows[:, None, :, None] > 0, (rows // block, block, blocks_all, block)
    ).reshape(rows, total)
    same = query_seq[:, None] == sequence[None, :]
    causal = position[None, :] <= query_pos[:, None]
    diagonal = (begin_row + jnp.arange(rows, dtype=jnp.int32))[:, None] == jnp.arange(
        total, dtype=jnp.int32
    )[None, :]
    return tiled & same & causal & valid[None, :] | diagonal


def rope_tables(position, head_dim):
    freqs = THETA_BASE ** (-jnp.arange(head_dim // 2, dtype=jnp.float32) * 2.0 / head_dim)
    angles = position.astype(jnp.float32)[:, None] * freqs[None, :]
    return (jnp.cos(angles), jnp.sin(angles))


def rotate(value_vectors, cosine, sine):
    half = value_vectors.shape[-1] // 2
    first = value_vectors[..., :half]
    second = value_vectors[..., half:]
    return jnp.concatenate(
        [first * cosine - second * sine, second * cosine + first * sine], axis=-1
    )


def rotate_back(value_vectors, cosine, sine):
    half = value_vectors.shape[-1] // 2
    first = value_vectors[..., :half]
    second = value_vectors[..., half:]
    return jnp.concatenate(
        [first * cosine + second * sine, second * cosine - first * sine], axis=-1
    )


def contract_rows(left, right):
    return lax.dot_general(
        left, right, (((0,), (0,)), ((), ())), preferred_element_type=jnp.float32
    )


def contract_cols(left, right):
    return lax.dot_general(
        left, right, (((1,), (1,)), ((), ())), preferred_element_type=jnp.float32
    )


def norm_parts(stream):
    inverse = lax.rsqrt(jnp.mean(stream * stream, axis=-1, keepdims=True) + EPS_NORM)
    return (stream * inverse, inverse)


def norm_back(grad_normed, gain, normalized_input, inverse):
    scaled = grad_normed * gain[None, :]
    return inverse * (
        scaled - normalized_input * jnp.mean(scaled * normalized_input, axis=-1, keepdims=True)
    )


def block_rows():
    return 512


def block_scores(query_block, key_vectors, layout, mask_blocks, begin_row, rows):
    sequence, position, valid = layout
    allowed = allowed_pairs(sequence, position, valid, mask_blocks, begin_row, rows, BLOCK)
    scores = jnp.einsum(
        "qkgd,skd->kgqs", query_block, key_vectors, preferred_element_type=jnp.float32
    ) * HEAD_SIZE ** (-0.5)
    return jnp.where(allowed[None, None], scores, NEG_FILL)


def attention_forward(query_vectors, key_vectors, value_vectors, layout, mask_blocks):
    token_positions = query_vectors.shape[0]
    rows = block_rows()
    outputs = []
    totals = []
    for begin_row in range(0, token_positions, rows):
        scores = block_scores(
            query_vectors[begin_row : begin_row + rows],
            key_vectors,
            layout,
            mask_blocks,
            begin_row,
            rows,
        )
        highest = jnp.max(scores, axis=-1, keepdims=True)
        expo = jnp.exp(scores - highest)
        summed = jnp.sum(expo, axis=-1, keepdims=True)
        weights = (expo / summed).astype(jnp.bfloat16)
        outputs.append(
            jnp.einsum("kgqs,skd->qkgd", weights, value_vectors, preferred_element_type=jnp.float32)
        )
        totals.append(highest + jnp.log(summed))
    return (jnp.concatenate(outputs, axis=0), totals)


def attention_backward(
    query_vectors, key_vectors, value_vectors, grad_out, totals, layout, mask_blocks
):
    token_positions = query_vectors.shape[0]
    rows = block_rows()
    grad_queries = []
    grad_keys = jnp.zeros(key_vectors.shape, jnp.float32)
    grad_values = jnp.zeros(value_vectors.shape, jnp.float32)
    for number, begin_row in enumerate(range(0, token_positions, rows)):
        query_block = query_vectors[begin_row : begin_row + rows]
        grad_block = grad_out[begin_row : begin_row + rows]
        scores = block_scores(query_block, key_vectors, layout, mask_blocks, begin_row, rows)
        probs = jnp.exp(scores - totals[number])
        grad_probs = jnp.einsum(
            "qkgd,skd->kgqs", grad_block, value_vectors, preferred_element_type=jnp.float32
        )
        centre = jnp.sum(probs * grad_probs, axis=-1, keepdims=True)
        grad_scores = (probs * (grad_probs - centre)).astype(jnp.bfloat16)
        grad_queries.append(
            jnp.einsum(
                "kgqs,skd->qkgd", grad_scores, key_vectors, preferred_element_type=jnp.float32
            )
            * HEAD_SIZE ** (-0.5)
        )
        grad_keys = grad_keys + jnp.einsum(
            "kgqs,qkgd->skd", grad_scores, query_block, preferred_element_type=jnp.float32
        ) * HEAD_SIZE ** (-0.5)
        grad_values = grad_values + jnp.einsum(
            "kgqs,qkgd->skd",
            probs.astype(jnp.bfloat16),
            grad_block,
            preferred_element_type=jnp.float32,
        )
    return (jnp.concatenate(grad_queries, axis=0), grad_keys, grad_values)


def shards(
    tokens,
    attention_gain,
    query_matrix,
    key_matrix,
    value_matrix,
    output_weight,
    feed_gain,
    gate_weight,
    up_weight,
    down_weight,
    sequence_lengths,
    block_mask,
    cotangent,
):
    token_positions = tokens.shape[0]
    local_heads = query_matrix.shape[1] // HEAD_SIZE
    local_kv = key_matrix.shape[1] // HEAD_SIZE
    head_groups = local_heads // local_kv
    stream = tokens.astype(jnp.float32)
    layout = token_layout(sequence_lengths[0], token_positions, BLOCK)
    cosine, sine = rope_tables(layout[1], HEAD_SIZE)
    cos_query, sin_query = (cosine[:, None, None, :], sine[:, None, None, :])
    cos_key, sin_key = (cosine[:, None, :], sine[:, None, :])
    query_full, key_full, value_full, output_full, gain_one = (
        lax.all_gather(query_matrix, "dp", axis=0, tiled=True),
        lax.all_gather(key_matrix, "dp", axis=0, tiled=True),
        lax.all_gather(value_matrix, "dp", axis=0, tiled=True),
        lax.all_gather(output_weight, "dp", axis=1, tiled=True),
        lax.all_gather(attention_gain, "dp", axis=0, tiled=True),
    )
    gain_first = gain_one.astype(jnp.float32)
    normalized_input, inverse = norm_parts(stream)
    normed_low = (normalized_input * gain_first[None, :]).astype(jnp.bfloat16)
    query_vectors = jnp.dot(normed_low, query_full, preferred_element_type=jnp.float32).reshape(
        token_positions, local_kv, head_groups, HEAD_SIZE
    )
    key_vectors = jnp.dot(normed_low, key_full, preferred_element_type=jnp.float32).reshape(
        token_positions, local_kv, HEAD_SIZE
    )
    value_vectors = (
        jnp.dot(normed_low, value_full, preferred_element_type=jnp.float32)
        .reshape(token_positions, local_kv, HEAD_SIZE)
        .astype(jnp.bfloat16)
    )
    query_vectors = rotate(query_vectors, cos_query, sin_query).astype(jnp.bfloat16)
    key_vectors = rotate(key_vectors, cos_key, sin_key).astype(jnp.bfloat16)
    attended, totals = attention_forward(
        query_vectors, key_vectors, value_vectors, layout, block_mask
    )
    attended = attended.reshape(token_positions, local_heads * HEAD_SIZE).astype(jnp.bfloat16)
    attention_part = jnp.dot(attended, output_full, preferred_element_type=jnp.float32)
    gate_full, up_full, down_full, gain_two = (
        lax.all_gather(gate_weight, "dp", axis=0, tiled=True),
        lax.all_gather(up_weight, "dp", axis=0, tiled=True),
        lax.all_gather(down_weight, "dp", axis=1, tiled=True),
        lax.all_gather(feed_gain, "dp", axis=0, tiled=True),
    )
    gain_second = gain_two.astype(jnp.float32)
    middle = stream + lax.psum(attention_part.astype(jnp.bfloat16), "tensor").astype(jnp.float32)
    normed_two, inverse_two = norm_parts(middle)
    normed_two_low = (normed_two * gain_second[None, :]).astype(jnp.bfloat16)
    gate = jnp.dot(normed_two_low, gate_full, preferred_element_type=jnp.float32)
    upper = jnp.dot(normed_two_low, up_full, preferred_element_type=jnp.float32)
    hidden = (jax.nn.silu(gate) * upper).astype(jnp.bfloat16)
    feed_part = jnp.dot(hidden, down_full, preferred_element_type=jnp.float32)
    block_output = (
        middle + lax.psum(feed_part.astype(jnp.bfloat16), "tensor").astype(jnp.float32)
    ).astype(jnp.bfloat16)
    grad_out = cotangent.astype(jnp.float32)
    down_grad = contract_rows(hidden, cotangent)
    grad_hidden = contract_cols(cotangent, down_full)
    sigmoid = jax.nn.sigmoid(gate)
    grad_gate = (grad_hidden * upper * sigmoid * (1.0 + gate * (1.0 - sigmoid))).astype(
        jnp.bfloat16
    )
    grad_up = (grad_hidden * gate * sigmoid).astype(jnp.bfloat16)
    gate_grad = contract_rows(normed_two_low, grad_gate)
    up_grad = contract_rows(normed_two_low, grad_up)
    feed_partial = contract_cols(grad_gate, gate_full) + contract_cols(grad_up, up_full)
    grad_normed_two = lax.psum(feed_partial.astype(jnp.bfloat16), "tensor").astype(jnp.float32)
    feed_gain_full = jnp.sum(grad_normed_two * normed_two, axis=0)
    grad_middle = grad_out + norm_back(grad_normed_two, gain_second, normed_two, inverse_two)
    gate_grad, up_grad, down_grad, feed_gain_grad = (
        lax.psum_scatter(
            gate_grad.astype(jnp.bfloat16), "dp", scatter_dimension=0, tiled=True
        ).astype(jnp.float32),
        lax.psum_scatter(
            up_grad.astype(jnp.bfloat16), "dp", scatter_dimension=0, tiled=True
        ).astype(jnp.float32),
        lax.psum_scatter(
            down_grad.astype(jnp.bfloat16), "dp", scatter_dimension=1, tiled=True
        ).astype(jnp.float32),
        lax.psum_scatter(
            feed_gain_full.astype(jnp.bfloat16), "dp", scatter_dimension=0, tiled=True
        ).astype(jnp.float32),
    )
    grad_middle_low = grad_middle.astype(jnp.bfloat16)
    output_grad = contract_rows(attended, grad_middle_low)
    grad_attended = (
        contract_cols(grad_middle_low, output_full)
        .astype(jnp.bfloat16)
        .reshape(token_positions, local_kv, head_groups, HEAD_SIZE)
    )
    grad_queries, grad_keys, grad_values = attention_backward(
        query_vectors, key_vectors, value_vectors, grad_attended, totals, layout, block_mask
    )
    grad_queries = (
        rotate_back(grad_queries, cos_query, sin_query)
        .astype(jnp.bfloat16)
        .reshape(token_positions, local_heads * HEAD_SIZE)
    )
    grad_keys = (
        rotate_back(grad_keys, cos_key, sin_key)
        .astype(jnp.bfloat16)
        .reshape(token_positions, local_kv * HEAD_SIZE)
    )
    grad_values = grad_values.astype(jnp.bfloat16).reshape(token_positions, local_kv * HEAD_SIZE)
    query_grad = contract_rows(normed_low, grad_queries)
    key_grad = contract_rows(normed_low, grad_keys)
    value_grad = contract_rows(normed_low, grad_values)
    grad_normed = (
        contract_cols(grad_queries, query_full)
        + contract_cols(grad_keys, key_full)
        + contract_cols(grad_values, value_full)
    )
    grad_normed = lax.psum(grad_normed.astype(jnp.bfloat16), "tensor").astype(jnp.float32)
    attention_gain_full = jnp.sum(grad_normed * normalized_input, axis=0)
    input_grad = grad_middle + norm_back(grad_normed, gain_first, normalized_input, inverse)
    query_grad, key_grad, value_grad, output_grad, attention_gain_grad = (
        lax.psum_scatter(
            query_grad.astype(jnp.bfloat16), "dp", scatter_dimension=0, tiled=True
        ).astype(jnp.float32),
        lax.psum_scatter(
            key_grad.astype(jnp.bfloat16), "dp", scatter_dimension=0, tiled=True
        ).astype(jnp.float32),
        lax.psum_scatter(
            value_grad.astype(jnp.bfloat16), "dp", scatter_dimension=0, tiled=True
        ).astype(jnp.float32),
        lax.psum_scatter(
            output_grad.astype(jnp.bfloat16), "dp", scatter_dimension=1, tiled=True
        ).astype(jnp.float32),
        lax.psum_scatter(
            attention_gain_full.astype(jnp.bfloat16), "dp", scatter_dimension=0, tiled=True
        ).astype(jnp.float32),
    )
    return (
        block_output,
        input_grad,
        attention_gain_grad,
        query_grad,
        key_grad,
        value_grad,
        output_grad,
        feed_gain_grad,
        gate_grad,
        up_grad,
        down_grad,
    )


def solution(mesh):
    in_specs = (
        P("dp", None),
        P("dp"),
        P("dp", "tensor"),
        P("dp", "tensor"),
        P("dp", "tensor"),
        P("tensor", "dp"),
        P("dp"),
        P("dp", "tensor"),
        P("dp", "tensor"),
        P("tensor", "dp"),
        P("dp", None),
        P("dp", None),
        P("dp", None),
    )
    out_specs = (
        P("dp", None),
        P("dp", None),
        P("dp"),
        P("dp", "tensor"),
        P("dp", "tensor"),
        P("dp", "tensor"),
        P("tensor", "dp"),
        P("dp"),
        P("dp", "tensor"),
        P("dp", "tensor"),
        P("tensor", "dp"),
    )
    return jax.shard_map(shards, mesh=mesh, in_specs=in_specs, out_specs=out_specs, check_vma=False)
```

profile of v0, /device:TPU:0, one launch (start us, length us, event | category | flops | bytes accessed | tf_op | source)
XLA Modules:
  0.0 1711.1 jit_solution(3431623023508275635)
XLA Ops:
  14.4 22.6 %all-gather = bf16[8,1,256]{2,1,0:T(2,128)(2,1)S(1)} all-gather(bf16[1,1,256]{2,1,0:T(2,128)(2,1)S(1)} %reshape.442), channel_id=1, replica_groups=mesh['dp'=8,'tensor'=4] {'dp'}, dimensions={0}, use_global_device_ids=true | all-gather | bytes 4608 | tf_op jit(solution)/shard_map/all_gather | solution.py:197
  37.8 33.4 %all_gather.29 = bf16[2048,128]{1,0:T(8,128)(2,1)S(1)} all-gather(bf16[256,128]{1,0:T(8,128)(2,1)} %param.16), channel_id=1, replica_groups=mesh['dp'=8,'tensor'=4] {'dp'}, dimensions={0}, use_global_device_ids=true | all-gather | bytes 589824 | tf_op jit(solution)/shard_map/all_gather | solution.py:194
  71.2 32.4 %all_gather.28 = bf16[2048,128]{1,0:T(8,128)(2,1)S(1)} all-gather(bf16[256,128]{1,0:T(8,128)(2,1)} %param.17), channel_id=1, replica_groups=mesh['dp'=8,'tensor'=4] {'dp'}, dimensions={0}, use_global_device_ids=true | all-gather | bytes 589824 | tf_op jit(solution)/shard_map/all_gather | solution.py:195
  174.6 16.6 all-gather.1
  191.2 64.7 %all-reduce.8.cloned.1.call-done = bf16[1024,2048]{1,0:T(8,128)(2,1)} async-done(((bf16[1024,2048]{1,0:T(8,128)(2,1)}), bf16[1024,2048]{1,0:T(8,128)(2,1)}) %all-reduce.8.cloned.1.call-update) | async-done | bytes 4194320 | tf_op jit(solution)/shard_map/psum | solution.py:227
  266.3 116.2 %all-gather.14.cloned.1.call-done = bf16[2048,2048]{1,0:T(8,128)(2,1)} async-done(((bf16[256,2048]{1,0:T(8,128)(2,1)}), bf16[2048,2048]{1,0:T(8,128)(2,1)}) %all-gather.14.cloned.1.call-update) | async-done | bytes 8388624 | tf_op jit(solution)/shard_map/all_gather | solution.py:222
  382.5 14.6 fusion.86
  397.0 110.1 %all-gather.12.cloned.1.call-done = bf16[2048,2048]{1,0:T(8,128)(2,1)} async-done(((bf16[256,2048]{1,0:T(8,128)(2,1)}), bf16[2048,2048]{1,0:T(8,128)(2,1)}) %all-gather.12.cloned.1.call-update) | async-done | bytes 8388624 | tf_op jit(solution)/shard_map/all_gather | solution.py:221
  507.1 14.5 fusion.85
  521.6 110.6 %all-gather.16.cloned.1.call-done = bf16[2048,2048]{1,0:T(8,128)(2,1)} async-done(((bf16[2048,256]{1,0:T(8,128)(2,1)}), bf16[2048,2048]{1,0:T(8,128)(2,1)}) %all-gather.16.cloned.1.call-update) | async-done | bytes 8388624 | tf_op jit(solution)/shard_map/all_gather | solution.py:223
  632.2 22.0 %multiply_convert_fusion = (bf16[1024,2048]{1,0:T(8,128)(2,1)}, bf16[1024,2048]{1,0:T(8,128)(2,1)}, bf16[1024,2048]{1,0:T(8,128)(2,1)}) fusion(f32[1024,2048]{1,0:T(8,128)} %fusion.85, f32[1024,2048]{1,0:T(8,128)} %fusion.86, bf16[1024,2048]{1,0:T(8,128)(2,1)} %param.25, bf16[2048,2048]{1,0:T(8,128)(2,1)} %all-gather.16.cloned.1.call-done), kind=kOutput, calls=%fused_computation.51 | convolution fusion | flops 8623489024 | bytes 41943040 | tf_op jit(solution)/shard_map/dot_general | solution.py:77
  654.2 12.7 fusion.87
  666.9 12.8 add_convert_fusion.1
  679.8 83.7 %all-reduce.10.cloned.1.call-done = bf16[1024,2048]{1,0:T(8,128)(2,1)} async-done(((bf16[1024,2048]{1,0:T(8,128)(2,1)}), bf16[1024,2048]{1,0:T(8,128)(2,1)}) %all-reduce.10.cloned.1.call-update) | async-done | bytes 4194320 | tf_op jit(solution)/shard_map/psum | solution.py:248
  763.6 8.8 fusion.22
  782.7 9.5 fusion.52
  792.2 13.6 fusion.3
  805.8 8.1 fusion
  822.3 12.1 fusion.2
  841.1 10.4 fusion.5
  881.9 13.9 convolution_convert_fusion.3
  903.4 14.1 convolution_convert_fusion
  917.6 14.1 convolution_convert_fusion.1
  932.0 14.1 convolution_convert_fusion.2
  952.2 70.5 %reduce-scatter.14.cloned.1.call-done = bf16[512,256]{1,0:T(8,128)(2,1)} async-done(((bf16[512,2048]{1,0:T(8,128)(2,1)}), bf16[512,256]{1,0:T(8,128)(2,1)}) %reduce-scatter.14.cloned.1.call-update) | async-done | bytes 262160 | tf_op jit(solution)/shard_map/reduce_scatter | solution.py:307
  1024.4 69.7 %reduce-scatter.8.cloned.1.call-done = bf16[256,512]{1,0:T(8,128)(2,1)} async-done(((bf16[2048,512]{1,0:T(8,128)(2,1)}), bf16[256,512]{1,0:T(8,128)(2,1)}) %reduce-scatter.8.cloned.1.call-update) | async-done | bytes 262160 | tf_op jit(solution)/shard_map/reduce_scatter | solution.py:298
  1096.0 153.2 %all-reduce.12.cloned.1.call-done = (bf16[1024,2048]{1,0:T(8,128)(2,1)}, bf16[1024,2048]{1,0:T(8,128)(2,1)}) async-done(((bf16[1024,2048]{1,0:T(8,128)(2,1)}, bf16[1024,2048]{1,0:T(8,128)(2,1)}), (bf16[1024,2048]{1,0:T(8,128)(2,1)}, bf16[1024,2048]{1,0:T(8,128)(2,1)})) %all-reduce.12.cloned.1.call-update) | async-done | bytes 8388624 | tf_op jit(solution)/shard_map/psum | solution.py:235
  1254.2 22.8 %all-reduce.2 = (bf16[2048]{0:T(1024)(128)(2,1)S(1)}, bf16[2048]{0:T(1024)(128)(2,1)S(1)}) all-reduce(bf16[2048]{0:T(1024)(128)(2,1)S(1)} %get-tuple-element.13, bf16[2048]{0:T(1024)(128)(2,1)S(1)} %copy-done.36), channel_id=2, replica_groups=mesh['dp'=8,'tensor'=4] {'dp'}, use_global_device_ids=true, to_apply=%region_19.20.clone | all-reduce | flops 4096 | bytes 16384
  1278.2 14.0 fusion.18
  1292.3 108.9 %reduce-scatter.20.cloned.1.call-done = bf16[2048,256]{1,0:T(8,128)(2,1)} async-done(((bf16[2048,2048]{1,0:T(8,128)(2,1)}), bf16[2048,256]{1,0:T(8,128)(2,1)}) %reduce-scatter.20.cloned.1.call-update) | async-done | bytes 1048592 | tf_op jit(solution)/shard_map/reduce_scatter | solution.py:258
  1403.9 147.4 %reduce-scatter.18.cloned.1.call-done = bf16[256,2048]{1,0:T(8,128)(2,1)} async-done(((bf16[2048,2048]{1,0:T(8,128)(2,1)}), bf16[256,2048]{1,0:T(8,128)(2,1)}) %reduce-scatter.18.cloned.1.call-update) | async-done | bytes 1048592 | tf_op jit(solution)/shard_map/reduce_scatter | solution.py:255
  1554.1 147.3 %reduce-scatter.16.cloned.1.call-done = bf16[256,2048]{1,0:T(8,128)(2,1)} async-done(((bf16[2048,2048]{1,0:T(8,128)(2,1)}), bf16[256,2048]{1,0:T(8,128)(2,1)}) %reduce-scatter.16.cloned.1.call-update) | async-done | bytes 1048592 | tf_op jit(solution)/shard_map/reduce_scatter | solution.py:252
  (211 shorter events, 176.0 us)
Async XLA Ops:
  7.2 107.4 %all-gather.8.cloned.1.call-start = ((), (), s32[]{:S(2)}) async-start(), calls=%async_computation.7 | async-start | bytes 2359296 | tf_op jit(solution)/shard_map/all_gather | solution.py:193
  7.9 158.4 %all-gather.10.cloned.1.call-start = ((), (), s32[]{:S(2)}) async-start(), calls=%async_computation.8 | async-start | bytes 2359296 | tf_op jit(solution)/shard_map/all_gather | solution.py:196
  8.7 247.2 %all-reduce.8.cloned.1.call-start = ((), (), s32[]{:S(2)}) async-start(), calls=%async_computation.9 | async-start | bytes 8388608 | tf_op jit(solution)/shard_map/psum | solution.py:227
  14.4 96.2 %copy-start.34 = (f32[1024]{0:T(1024)}, f32[1024]{0:T(1024)S(1)}, u32[]{:S(2)}) copy-start(f32[1024]{0:T(1024)S(1)} %add_rsqrt_fusion.1) | copy-start | bytes 12292
  37.0 73.5 %copy-start.31 = (f32[8,1,256]{2,1,0:T(1,128)}, f32[8,1,256]{2,1,0:T(1,128)S(1)}, u32[]{:S(2)}) copy-start(f32[8,1,256]{2,1,0:T(1,128)S(1)} %convert_element_type.223) | copy-start | bytes 24580
  71.2 39.3 %copy-start.18 = (bf16[2048,128]{1,0:T(8,128)(2,1)}, bf16[2048,128]{1,0:T(8,128)(2,1)S(1)}, u32[]{:S(2)}) copy-start(bf16[2048,128]{1,0:T(8,128)(2,1)S(1)} %all_gather.29) | copy-start | bytes 1572868
  111.2 31.9 %copy-start.24 = (bf16[1024,2,32]{0,2,1:T(8,128)(2,1)}, bf16[1024,2,32]{0,2,1:T(8,128)(2,1)S(1)}, u32[]{:S(2)}) copy-start(bf16[1024,2,32]{0,2,1:T(8,128)(2,1)S(1)} %get-tuple-element.36) | copy-start | bytes 393220
  111.2 31.9 %copy-start.26 = (bf16[1024,2,32]{0,2,1:T(8,128)(2,1)}, bf16[1024,2,32]{0,2,1:T(8,128)(2,1)S(1)}, u32[]{:S(2)}) copy-start(bf16[1024,2,32]{0,2,1:T(8,128)(2,1)S(1)} %get-tuple-element.37) | copy-start | bytes 393220
  120.3 22.8 %copy-start.11 = (bf16[1024,2,4,32]{0,3,2,1:T(8,128)(2,1)}, bf16[1024,2,4,32]{0,3,2,1:T(8,128)(2,1)S(1)}, u32[]{:S(2)}) copy-start(bf16[1024,2,4,32]{0,3,2,1:T(8,128)(2,1)S(1)} %get-tuple-element.30) | copy-start | bytes 1572868
  120.3 22.8 %copy-start.13 = (bf16[1024,2,4,32]{0,3,2,1:T(8,128)(2,1)}, bf16[1024,2,4,32]{0,3,2,1:T(8,128)(2,1)S(1)}, u32[]{:S(2)}) copy-start(bf16[1024,2,4,32]{0,3,2,1:T(8,128)(2,1)S(1)} %get-tuple-element.31) | copy-start | bytes 1572868
  172.7 209.7 %all-gather.14.cloned.1.call-start = ((), (), s32[]{:S(2)}) async-start(), calls=%async_computation.11 | async-start | bytes 9437184 | tf_op jit(solution)/shard_map/all_gather | solution.py:222
  173.3 333.8 %all-gather.12.cloned.1.call-start = ((), (), s32[]{:S(2)}) async-start(), calls=%async_computation.10 | async-start | bytes 9437184 | tf_op jit(solution)/shard_map/all_gather | solution.py:221
  173.9 458.3 %all-gather.16.cloned.1.call-start = ((), (), s32[]{:S(2)}) async-start(), calls=%async_computation.12 | async-start | bytes 9437184 | tf_op jit(solution)/shard_map/all_gather | solution.py:223
  174.5 589.1 %all-reduce.10.cloned.1.call-start = ((), (), s32[]{:S(2)}) async-start(), calls=%async_computation.13 | async-start | bytes 8388608 | tf_op jit(solution)/shard_map/psum | solution.py:248
  679.7 268.3 %reduce-scatter.12.cloned.1.call-start = ((), (), s32[]{:S(2)}) async-start(), calls=%async_computation.16 | async-start | bytes 589824 | tf_op jit(solution)/shard_map/reduce_scatter | solution.py:304
  782.6 23.1 %copy-start.15 = (bf16[512,512]{0,1:T(8,128)(2,1)}, bf16[512,512]{0,1:T(8,128)(2,1)S(1)}, u32[]{:S(2)}) copy-start(bf16[512,512]{0,1:T(8,128)(2,1)S(1)} %get-tuple-element.33) | copy-start | bytes 1572868
  782.7 23.1 %slice-start = ((s8[16777216]{0:T(1024)(128)(4,1)}), s8[4194304]{0:T(1024)(128)(4,1)S(1)}, s32[]{:S(2)}) async-start(s8[16777216]{0:T(1024)(128)(4,1)} %bitcast.171), calls=%async_computation.22 | async-start | bytes 8388608
  782.7 23.1 %slice-start.1 = ((s8[16777216]{0:T(1024)(128)(4,1)}), s8[4194304]{0:T(1024)(128)(4,1)S(1)}, s32[]{:S(2)}) async-start(s8[16777216]{0:T(1024)(128)(4,1)} %bitcast.171), calls=%async_computation.23 | async-start | bytes 8388608
  822.1 128.5 %reduce-scatter.10.cloned.1.call-start = ((), (), s32[]{:S(2)}) async-start(), calls=%async_computation.15 | async-start | bytes 589824 | tf_op jit(solution)/shard_map/reduce_scatter | solution.py:301
  822.2 14.8 slice-start.4
  822.2 17.7 %slice-start.6 = ((s8[16777216]{0:T(1024)(128)(4,1)}), s8[4194304]{0:T(1024)(128)(4,1)S(1)}, s32[]{:S(2)}) async-start(s8[16777216]{0:T(1024)(128)(4,1)} %bitcast.173), calls=%async_computation.28 | async-start | bytes 8388608
  822.3 18.8 %slice-start.7 = ((s8[16777216]{0:T(1024)(128)(4,1)}), s8[4194304]{0:T(1024)(128)(4,1)S(1)}, s32[]{:S(2)}) async-start(s8[16777216]{0:T(1024)(128)(4,1)} %bitcast.173), calls=%async_computation.29 | async-start | bytes 8388608
  834.4 17.2 %copy-start.4 = (bf16[2,4,512,1024]{2,3,1,0:T(8,128)(2,1)}, bf16[2,4,512,1024]{2,3,1,0:T(8,128)(2,1)S(1)}, u32[]{:S(2)}) copy-start(bf16[2,4,512,1024]{2,3,1,0:T(8,128)(2,1)S(1)} %fusion.2) | copy-start | bytes 25165828
  860.1 162.6 %reduce-scatter.14.cloned.1.call-start = ((), (), s32[]{:S(2)}) async-start(), calls=%async_computation.17 | async-start | bytes 2359296 | tf_op jit(solution)/shard_map/reduce_scatter | solution.py:307
  867.3 226.9 %reduce-scatter.8.cloned.1.call-start = ((), (), s32[]{:S(2)}) async-start(), calls=%async_computation.14 | async-start | bytes 2359296 | tf_op jit(solution)/shard_map/reduce_scatter | solution.py:298
  881.9 367.3 %all-reduce.12.cloned.1.call-start = ((), (), s32[]{:S(2)}) async-start(), calls=%async_computation.21 | async-start | bytes 16777216 | tf_op jit(solution)/shard_map/psum | solution.py:235
  903.2 498.0 %reduce-scatter.20.cloned.1.call-start = ((), (), s32[]{:S(2)}) async-start(), calls=%async_computation.20 | async-start | bytes 9437184 | tf_op jit(solution)/shard_map/reduce_scatter | solution.py:258
  917.6 633.7 %reduce-scatter.18.cloned.1.call-start = ((), (), s32[]{:S(2)}) async-start(), calls=%async_computation.19 | async-start | bytes 9437184 | tf_op jit(solution)/shard_map/reduce_scatter | solution.py:255
  931.7 769.7 %reduce-scatter.16.cloned.1.call-start = ((), (), s32[]{:S(2)}) async-start(), calls=%async_computation.18 | async-start | bytes 9437184 | tf_op jit(solution)/shard_map/reduce_scatter | solution.py:252
  946.1 303.0 %copy-start.32 = (f32[8,1,256]{2,1,0:T(1,128)S(1)}, f32[8,1,256]{2,1,0:T(1,128)}, u32[]{:S(2)}) copy-start(f32[8,1,256]{2,1,0:T(1,128)} %copy-done.31) | copy-start | bytes 24580
  946.1 303.1 %copy-start.35 = (f32[1024]{0:T(1024)S(1)}, f32[1024]{0:T(1024)}, u32[]{:S(2)}) copy-start(f32[1024]{0:T(1024)} %copy-done.34) | copy-start | bytes 12292
  946.1 308.0 %copy-start.36 = (bf16[2048]{0:T(1024)(128)(2,1)S(1)}, bf16[2048]{0:T(1024)(128)(2,1)}, u32[]{:S(2)}) copy-start(bf16[2048]{0:T(1024)(128)(2,1)} %get-tuple-element.11) | copy-start | bytes 12292
  (33 other events, 249.0 us)
Sparse Core Ops, SparseCore 0:
  10.1 58.0 all-gather.7
  70.2 53.0 all-gather.9
  172.9 82.9 all-reduce.7
  257.8 124.5 all-gather.13
  384.4 122.6 all-gather.11
  509.0 123.1 all-gather.15
  679.9 83.6 all-reduce.9
  822.3 62.7 reduce-scatter.11
  889.0 61.6 reduce-scatter.9
  954.6 67.9 reduce-scatter.13
  1026.8 67.3 reduce-scatter.7
  1097.2 151.9 all-reduce.11
  1252.8 148.3 reduce-scatter.19
  1404.7 146.5 reduce-scatter.17
  1554.8 146.5 reduce-scatter.15
where the time goes:
time: 1720 us; the launch traced here: 1710 us
  waiting for transfers between devices  1190 us (69%)
  matrix products  258 us (15%)
  blocking collectives  128 us (7%)
  other arithmetic  112 us (7%)
    psum x1, waiting for transfers between devices, shards(): lax.psum(feed_part.astype(jnp.bfloat16), 'tensor').astype(jnp.float32)  153 us
    reduce_scatter x1, waiting for transfers between devices, shards(): lax.psum_scatter(up_grad.astype(jnp.bfloat16), 'dp', scatter_dimension=0,...  147 us
    reduce_scatter x1, waiting for transfers between devices, shards(): lax.psum_scatter(gate_grad.astype(jnp.bfloat16), 'dp', scatter_dimension=...  147 us
    all_gather x1, waiting for transfers between devices, shards(): lax.all_gather(up_weight, 'dp', axis=0, tiled=True)  116 us
    all_gather x1, waiting for transfers between devices, shards(): lax.all_gather(down_weight, 'dp', axis=1, tiled=True)  111 us
    all_gather x1, waiting for transfers between devices, shards(): lax.all_gather(gate_weight, 'dp', axis=0, tiled=True)  110 us
    reduce_scatter x1, waiting for transfers between devices, shards(): lax.psum_scatter(down_grad.astype(jnp.bfloat16), 'dp', scatter_dimension=...  109 us
    psum x1, waiting for transfers between devices, shards(): lax.psum(feed_partial.astype(jnp.bfloat16), 'tensor').astype(jnp.float32)  83.7 us
  transfers between devices with their start and end apart: 15, of which 12 were waited for; matrix products, arithmetic and copies ran while one was open for 15% of the time, Pallas kernels for 0%

commit v1 on v0

--- a/solution.py
+++ b/solution.py
@@ -163,6 +163,26 @@
             preferred_element_type=jnp.float32,
         )
     return (jnp.concatenate(grad_queries, axis=0), grad_keys, grad_values)
+
+
+def tensor_sum(partial):
+    rows = partial.shape[0] // 2
+    core = lax.axis_index("tensor") % 2
+    count = lax.axis_size("tensor")
+    flip_core = [(i, i ^ 1) for i in range(count)]
+    flip_y = [(i, i ^ 2) for i in range(count)]
+    mine = lax.dynamic_slice_in_dim(partial, core * rows, rows, axis=0)
+    other = lax.dynamic_slice_in_dim(partial, (1 - core) * rows, rows, axis=0)
+    received = lax.ppermute(other, "tensor", flip_core)
+    chip = (mine.astype(jnp.float32) + received.astype(jnp.float32)).astype(jnp.bfloat16)
+    across = lax.ppermute(chip, "tensor", flip_y)
+    total = (chip.astype(jnp.float32) + across.astype(jnp.float32)).astype(jnp.bfloat16)
+    back = lax.ppermute(total, "tensor", flip_core)
+    return jnp.where(
+        core == 0,
+        jnp.concatenate([total, back], axis=0),
+        jnp.concatenate([back, total], axis=0),
+    )
 
 
 def shards(
@@ -189,10 +209,14 @@
     cosine, sine = rope_tables(layout[1], HEAD_SIZE)
     cos_query, sin_query = (cosine[:, None, None, :], sine[:, None, None, :])
     cos_key, sin_key = (cosine[:, None, :], sine[:, None, :])
-    query_full, key_full, value_full, output_full, gain_one = (
-        lax.all_gather(query_matrix, "dp", axis=0, tiled=True),
-        lax.all_gather(key_matrix, "dp", axis=0, tiled=True),
-        lax.all_gather(value_matrix, "dp", axis=0, tiled=True),
+    wide_q, wide_k = query_matrix.shape[1], key_matrix.shape[1]
+    packed_full = lax.all_gather(
+        jnp.concatenate([query_matrix, key_matrix, value_matrix], axis=1), "dp", axis=0, tiled=True
+    )
+    query_full = packed_full[:, :wide_q]
+    key_full = packed_full[:, wide_q : wide_q + wide_k]
+    value_full = packed_full[:, wide_q + wide_k :]
+    output_full, gain_one = (
         lax.all_gather(output_weight, "dp", axis=1, tiled=True),
         lax.all_gather(attention_gain, "dp", axis=0, tiled=True),
     )
@@ -224,7 +248,7 @@
         lax.all_gather(feed_gain, "dp", axis=0, tiled=True),
     )
     gain_second = gain_two.astype(jnp.float32)
-    middle = stream + lax.psum(attention_part.astype(jnp.bfloat16), "tensor").astype(jnp.float32)
+    middle = stream + tensor_sum(attention_part.astype(jnp.bfloat16)).astype(jnp.float32)
     normed_two, inverse_two = norm_parts(middle)
     normed_two_low = (normed_two * gain_second[None, :]).astype(jnp.bfloat16)
     gate = jnp.dot(normed_two_low, gate_full, preferred_element_type=jnp.float32)
@@ -232,7 +256,7 @@
     hidden = (jax.nn.silu(gate) * upper).astype(jnp.bfloat16)
     feed_part = jnp.dot(hidden, down_full, preferred_element_type=jnp.float32)
     block_output = (
-        middle + lax.psum(feed_part.astype(jnp.bfloat16), "tensor").astype(jnp.float32)
+        middle + tensor_sum(feed_part.astype(jnp.bfloat16)).astype(jnp.float32)
     ).astype(jnp.bfloat16)
     grad_out = cotangent.astype(jnp.float32)
     down_grad = contract_rows(hidden, cotangent)
@@ -245,7 +269,7 @@
     gate_grad = contract_rows(normed_two_low, grad_gate)
     up_grad = contract_rows(normed_two_low, grad_up)
     feed_partial = contract_cols(grad_gate, gate_full) + contract_cols(grad_up, up_full)
-    grad_normed_two = lax.psum(feed_partial.astype(jnp.bfloat16), "tensor").astype(jnp.float32)
+    grad_normed_two = tensor_sum(feed_partial.astype(jnp.bfloat16)).astype(jnp.float32)
     feed_gain_full = jnp.sum(grad_normed_two * normed_two, axis=0)
     grad_middle = grad_out + norm_back(grad_normed_two, gain_second, normed_two, inverse_two)
     gate_grad, up_grad, down_grad, feed_gain_grad = (
@@ -291,19 +315,19 @@
         + contract_cols(grad_keys, key_full)
         + contract_cols(grad_values, value_full)
     )
-    grad_normed = lax.psum(grad_normed.astype(jnp.bfloat16), "tensor").astype(jnp.float32)
+    grad_normed = tensor_sum(grad_normed.astype(jnp.bfloat16)).astype(jnp.float32)
     attention_gain_full = jnp.sum(grad_normed * normalized_input, axis=0)
     input_grad = grad_middle + norm_back(grad_normed, gain_first, normalized_input, inverse)
-    query_grad, key_grad, value_grad, output_grad, attention_gain_grad = (
-        lax.psum_scatter(
-            query_grad.astype(jnp.bfloat16), "dp", scatter_dimension=0, tiled=True
-        ).astype(jnp.float32),
-        lax.psum_scatter(
-            key_grad.astype(jnp.bfloat16), "dp", scatter_dimension=0, tiled=True
-        ).astype(jnp.float32),
-        lax.psum_scatter(
-            value_grad.astype(jnp.bfloat16), "dp", scatter_dimension=0, tiled=True
-        ).astype(jnp.float32),
+    packed_grad = lax.psum_scatter(
+        jnp.concatenate([query_grad, key_grad, value_grad], axis=1).astype(jnp.bfloat16),
+        "dp",
+        scatter_dimension=0,
+        tiled=True,
+    ).astype(jnp.float32)
+    query_grad = packed_grad[:, :wide_q]
+    key_grad = packed_grad[:, wide_q : wide_q + wide_k]
+    value_grad = packed_grad[:, wide_q + wide_k :]
+    output_grad, attention_gain_grad = (
         lax.psum_scatter(
             output_grad.astype(jnp.bfloat16), "dp", scatter_dimension=1, tiled=True
         ).astype(jnp.float32),

time: 1720 us -> 1290 us (0.75)
  waiting for transfers between devices: 1190 us -> 779 us
  blocking collectives: 128 us -> 60.9 us
  other arithmetic: 112 us -> 144 us
    psum x3 -> x0, waiting for transfers between devices: 302 us -> none  [the longest x1 153 us: shards(): lax.psum(feed_part.astype(jnp.bfloat16), 'tensor').astype(jnp.float32)]
    ppermute x0 -> x12, waiting for transfers between devices: none -> 192 us  [the longest x4 179 us: tensor_sum(): across = lax.ppermute(chip, 'tensor', flip_y)]
    reduce_scatter x1, waiting for transfers between devices: 109 us -> 17.2 us  [shards(): lax.psum_scatter(down_grad.astype(jnp.bfloat16), 'dp', scatter_dimension=...]
    all_gather x1, waiting for transfers between devices: 111 us -> 25.9 us  [shards(): lax.all_gather(down_weight, 'dp', axis=1, tiled=True)]
    reduce_scatter x3 -> x1, waiting for transfers between devices: 70.9 us -> 0.01 us  [shards(): lax.psum_scatter(jnp.concatenate([query_grad, key_grad, value_grad], axis...]
    reduce_scatter x1, waiting for transfers between devices: 70.5 us -> 0.02 us  [shards(): lax.psum_scatter(output_grad.astype(jnp.bfloat16), 'dp', scatter_dimensio...]
    all_gather x2 -> x0, blocking collectives: 65.8 us -> none  [the longest x1 33.4 us: shards(): lax.all_gather(key_matrix, 'dp', axis=0, tiled=True)]
    all_gather x1, waiting for transfers between devices: 0.02 us -> 26 us  [shards(): lax.all_gather(jnp.concatenate([query_matrix, key_matrix, value_matrix],...]
  transfers between devices with their start and end apart: 15 -> 22, of which waited for: 12 -> 14; matrix products, arithmetic and copies ran while one was open for 15% -> 22% of each run, Pallas kernels for 0% -> 0%
where the time goes in v1:
time: 1290 us
  waiting for transfers between devices  779 us (60%)
  matrix products  262 us (20%)
  other arithmetic  144 us (11%)
  blocking collectives  60.9 us (5%)
  local copies, waits for them, and re-layouts  18.2 us (1%)
  between operations  16.1 us (1%)
    ppermute x4, waiting for transfers between devices, tensor_sum(): across = lax.ppermute(chip, 'tensor', flip_y)  179 us
    reduce_scatter x1, waiting for transfers between devices, shards(): lax.psum_scatter(up_grad.astype(jnp.bfloat16), 'dp', scatter_dimension=0,...  148 us
    reduce_scatter x1, waiting for transfers between devices, shards(): lax.psum_scatter(gate_grad.astype(jnp.bfloat16), 'dp', scatter_dimension=...  147 us
    all_gather x1, waiting for transfers between devices, shards(): lax.all_gather(gate_weight, 'dp', axis=0, tiled=True)  110 us
    all_gather x1, waiting for transfers between devices, shards(): lax.all_gather(up_weight, 'dp', axis=0, tiled=True)  110 us
    dot_general x7, matrix products, contract_cols(): lax.dot_general(left, right, (((1,), (1,)), ((), ())), preferred_element_...  55.9 us
    dot_general x7, matrix products, contract_rows(): lax.dot_general(left, right, (((0,), (0,)), ((), ())), preferred_element_...  51 us
    dot_general x2, matrix products, attention_backward(): jnp.einsum('qkgd,skd->kgqs', grad_block, value_vectors, preferred_element...  30.9 us
  transfers between devices with their start and end apart: 22, of which 14 were waited for; matrix products, arithmetic and copies ran while one was open for 22% of the time, Pallas kernels for 0%

profile of v1, /device:TPU:0, one launch (start us, length us, event | category | flops | bytes accessed | tf_op | source)
XLA Modules:
  0.0 1287.5 jit_solution(10656139916120193872)
XLA Ops:
  15.5 22.8 %all-gather = bf16[8,1,256]{2,1,0:T(2,128)(2,1)S(1)} all-gather(bf16[1,1,256]{2,1,0:T(2,128)(2,1)S(1)} %reshape.442), channel_id=1, replica_groups=mesh['dp'=8,'tensor'=4] {'dp'}, dimensions={0}, use_global_device_ids=true | all-gather | bytes 4608 | tf_op jit(solution)/shard_map/all_gather | solution.py:221
  47.6 26.0 %all-gather.8.cloned.1.call-done = bf16[2048,768]{1,0:T(8,128)(2,1)} async-done(((bf16[256,768]{1,0:T(8,128)(2,1)}), bf16[2048,768]{1,0:T(8,128)(2,1)}) %all-gather.8.cloned.1.call-update) | async-done | bytes 3145744 | tf_op jit(solution)/shard_map/all_gather | solution.py:213
  147.3 46.3 %collective-permute-done.1 = bf16[512,2048]{1,0:T(8,128)(2,1)S(1)} collective-permute-done((bf16[512,2048]{1,0:T(8,128)(2,1)S(1)}, bf16[512,2048]{1,0:T(8,128)(2,1)S(1)}, u32[]{:S(2)}, u32[]{:S(2)}) %collective-permute-start.1) | collective-permute-done | bytes 2097184 | tf_op jit(solution)/shard_map/ppermute | solution.py:178
  194.6 19.3 %all-gather.1 = bf16[8,1,256]{2,1,0:T(2,128)(2,1)S(1)} all-gather(bf16[1,1,256]{2,1,0:T(2,128)(2,1)S(1)} %reshape.444), channel_id=1, replica_groups=mesh['dp'=8,'tensor'=4] {'dp'}, dimensions={0}, use_global_device_ids=true | all-gather | bytes 4608 | tf_op jit(solution)/shard_map/all_gather | solution.py:248
  224.2 25.9 %all-gather.16.cloned.1.call-done = bf16[2048,2048]{1,0:T(8,128)(2,1)} async-done(((bf16[2048,256]{1,0:T(8,128)(2,1)}), bf16[2048,2048]{1,0:T(8,128)(2,1)}) %all-gather.16.cloned.1.call-update) | async-done | bytes 8388624 | tf_op jit(solution)/shard_map/all_gather | solution.py:247
  250.1 14.5 %fusion.95 = f32[1024,2048]{1,0:T(8,128)} fusion(bf16[1024,2048]{1,0:T(8,128)(2,1)} %param.25, bf16[2048,2048]{1,0:T(8,128)(2,1)} %all-gather.16.cloned.1.call-done), kind=kOutput, calls=%fused_computation.189 | convolution fusion | flops 8589934592 | bytes 20971520 | tf_op jit(solution)/shard_map/dot_general | solution.py:77
  264.6 110.1 %all-gather.14.cloned.1.call-done = bf16[2048,2048]{1,0:T(8,128)(2,1)} async-done(((bf16[256,2048]{1,0:T(8,128)(2,1)}), bf16[2048,2048]{1,0:T(8,128)(2,1)}) %all-gather.14.cloned.1.call-update) | async-done | bytes 8388624 | tf_op jit(solution)/shard_map/all_gather | solution.py:246
  374.7 14.4 %fusion.94 = f32[1024,2048]{1,0:T(8,128)} fusion(bf16[1024,2048]{1,0:T(8,128)(2,1)} %multiply_convert_fusion.3, bf16[2048,2048]{1,0:T(8,128)(2,1)} %all-gather.14.cloned.1.call-done), kind=kOutput, calls=%fused_computation.188 | convolution fusion | flops 8589934592 | bytes 20971520 | tf_op jit(solution)/shard_map/dot_general | solution.py:255
  389.1 110.2 %all-gather.12.cloned.1.call-done = bf16[2048,2048]{1,0:T(8,128)(2,1)} async-done(((bf16[256,2048]{1,0:T(8,128)(2,1)}), bf16[2048,2048]{1,0:T(8,128)(2,1)}) %all-gather.12.cloned.1.call-update) | async-done | bytes 8388624 | tf_op jit(solution)/shard_map/all_gather | solution.py:245
  499.4 21.5 %multiply_convert_fusion = (bf16[1024,2048]{1,0:T(8,128)(2,1)S(1)}, bf16[1024,2048]{1,0:T(8,128)(2,1)}, bf16[1024,2048]{1,0:T(8,128)(2,1)}) fusion(f32[1024,2048]{1,0:T(8,128)} %fusion.95, f32[1024,2048]{1,0:T(8,128)} %fusion.94, bf16[1024,2048]{1,0:T(8,128)(2,1)} %multiply_convert_fusion.3, bf16[2048,2048]{1,0:T(8,128)(2,1)} %all-gather.12.cloned.1.call-done), kind=kOutput, calls=%fused_computation.51 | convolution fusion | flops 8623489024 | bytes 41943040 | tf_op jit(solution)/shard_map/dot_general | solution.py:254
  520.9 16.1 %fusion.96 = f32[1024,2048]{1,0:T(8,128)} fusion(bf16[1024,2048]{1,0:T(8,128)(2,1)} %get-tuple-element.53, bf16[2048,2048]{1,0:T(8,128)(2,1)} %all-gather.12.cloned.1.call-done), kind=kOutput, calls=%fused_computation.190 | convolution fusion | flops 8589934592 | bytes 20971520 | tf_op jit(solution)/shard_map/dot_general | solution.py:77
  537.0 13.0 %add_convert_fusion.1 = bf16[1024,2048]{1,0:T(8,128)(2,1)S(1)} fusion(f32[1024,2048]{1,0:T(8,128)} %fusion.96, bf16[1024,2048]{1,0:T(8,128)(2,1)S(1)} %get-tuple-element.52, bf16[2048,2048]{1,0:T(8,128)(2,1)} %all-gather.14.cloned.1.call-done), kind=kOutput, calls=%fused_computation.50 | convolution fusion | flops 8594128896 | bytes 25165824 | tf_op jit(solution)/shard_map/dot_general | solution.py:77
  556.9 46.2 %collective-permute-done.7 = bf16[512,2048]{1,0:T(8,128)(2,1)S(1)} collective-permute-done((bf16[512,2048]{1,0:T(8,128)(2,1)S(1)}, bf16[512,2048]{1,0:T(8,128)(2,1)S(1)}, u32[]{:S(2)}, u32[]{:S(2)}) %collective-permute-start.7) | collective-permute-done | bytes 2097184 | tf_op jit(solution)/shard_map/ppermute | solution.py:178
  608.3 10.5 fusion.19
  618.9 13.5 %fusion.21 = f32[1024,2048]{1,0:T(8,128)S(1)} fusion(bf16[1024,2048]{1,0:T(8,128)(2,1)S(1)} %copy-done.16, bf16[1024,2048]{1,0:T(8,128)(2,1)S(1)} %copy-done.1, f32[1024]{0:T(1024)S(1)} %broadcast_multiply_fusion.1, f32[2048]{0:T(1024)S(1)} %bitcast.203, f32[1024]{0:T(1024)S(1)} %add_rsqrt_fusion, bf16[512,2048]{1,0:T(8,128)(2,1)S(1)} %add_convert_fusion.5, ...), kind=kLoop, calls=%fused_computation.39 | loop fusion | flops 60817408 | bytes 25182208 | tf_op jit(solution)/shard_map/add | solution.py:274
  646.0 15.4 %fusion = (f32[2,4,512]{2,1,0:T(4,128)S(1)}, f32[2,1024,512,4]{2,1,3,0:T(8,128)}) fusion(f32[2,4,512,1024]{2,3,1,0:T(8,128)} %get-tuple-element.82, f32[2,4,512]{2,1,0:T(4,128)S(1)} %bitcast.191, bf16[1024,2,64,1]{0,2,3,1:T(8,128)(2,1)S(1)} %bitcast.179, bf16[512,2,4,64]{0,3,2,1:T(8,128)(2,1)S(1)} %bitcast.171), kind=kOutput, calls=%fused_computation.2 | convolution fusion | flops 549449728 | bytes 34373632 | tf_op jit(solution)/shard_map/qkgd,skd->kgqs/dot_general | solution.py:145
  662.6 10.6 fusion.2
  681.9 15.5 %fusion.3 = (f32[2,4,512]{2,1,0:T(4,128)S(1)}, f32[2,1024,512,4]{2,1,3,0:T(8,128)}) fusion(f32[2,4,512,1024]{2,3,1,0:T(8,128)} %get-tuple-element.84, f32[2,4,512]{2,1,0:T(4,128)S(1)} %bitcast.194, bf16[1024,2,64,1]{0,2,3,1:T(8,128)(2,1)S(1)} %bitcast.180, bf16[512,2,4,64]{0,3,2,1:T(8,128)(2,1)S(1)} %bitcast.173), kind=kOutput, calls=%fused_computation.7 | convolution fusion | flops 549449728 | bytes 34373632 | tf_op jit(solution)/shard_map/qkgd,skd->kgqs/dot_general | solution.py:145
  698.5 10.6 fusion.5
  719.2 9.5 fusion.56
  740.8 14.0 %convolution_convert_fusion = bf16[2048,2048]{1,0:T(8,128)(2,1)} fusion(bf16[1024,2048]{1,0:T(8,128)(2,1)} %get-tuple-element.54, bf16[1024,2048]{1,0:T(8,128)(2,1)} %param.25), kind=kOutput, calls=%fused_computation.60 | convolution fusion | flops 8594128896 | bytes 16777216 | tf_op jit(solution)/shard_map/dot_general | solution.py:71
  754.9 14.1 %convolution_convert_fusion.1 = bf16[2048,2048]{1,0:T(8,128)(2,1)} fusion(bf16[1024,2048]{1,0:T(8,128)(2,1)} %multiply_convert_fusion.3, bf16[1024,2048]{1,0:T(8,128)(2,1)} %copy-done.46), kind=kOutput, calls=%fused_computation.61 | convolution fusion | flops 8594128896 | bytes 16777216 | tf_op jit(solution)/shard_map/dot_general | solution.py:71
  769.1 14.2 %convolution_convert_fusion.2 = bf16[2048,2048]{1,0:T(8,128)(2,1)} fusion(bf16[1024,2048]{1,0:T(8,128)(2,1)} %multiply_convert_fusion.3, bf16[1024,2048]{1,0:T(8,128)(2,1)} %get-tuple-element.53), kind=kOutput, calls=%fused_computation.62 | convolution fusion | flops 8594128896 | bytes 16777216 | tf_op jit(solution)/shard_map/dot_general | solution.py:71
  783.4 12.7 convolution_convert_fusion.3
  811.9 44.6 %collective-permute-done.4 = bf16[512,2048]{1,0:T(8,128)(2,1)S(1)} collective-permute-done((bf16[512,2048]{1,0:T(8,128)(2,1)S(1)}, bf16[512,2048]{1,0:T(8,128)(2,1)S(1)}, u32[]{:S(2)}, u32[]{:S(2)}) %collective-permute-start.4) | collective-permute-done | bytes 2097184 | tf_op jit(solution)/shard_map/ppermute | solution.py:178
  858.6 42.1 %collective-permute-done.10 = bf16[512,2048]{1,0:T(8,128)(2,1)S(1)} collective-permute-done((bf16[512,2048]{1,0:T(8,128)(2,1)S(1)}, bf16[512,2048]{1,0:T(8,128)(2,1)S(1)}, u32[]{:S(2)}, u32[]{:S(2)}) %collective-permute-start.10) | collective-permute-done | bytes 2097184 | tf_op jit(solution)/shard_map/ppermute | solution.py:178
  904.1 11.7 fusion.22
  924.0 18.7 %all-reduce.2 = (bf16[2048]{0:T(1024)(128)(2,1)S(1)}, bf16[2048]{0:T(1024)(128)(2,1)S(1)}) all-reduce(bf16[2048]{0:T(1024)(128)(2,1)S(1)} %get-tuple-element.44, bf16[2048]{0:T(1024)(128)(2,1)S(1)} %get-tuple-element.55), channel_id=2, replica_groups=mesh['dp'=8,'tensor'=4] {'dp'}, use_global_device_ids=true, to_apply=%region_15.16.clone | all-reduce | flops 4096 | bytes 16384
  944.0 11.8 fusion.18
  960.2 17.2 %reduce-scatter.14.cloned.1.call-done = bf16[2048,256]{1,0:T(8,128)(2,1)} async-done(((bf16[2048,2048]{1,0:T(8,128)(2,1)}), bf16[2048,256]{1,0:T(8,128)(2,1)}) %reduce-scatter.14.cloned.1.call-update) | async-done | bytes 1048592 | tf_op jit(solution)/shard_map/reduce_scatter | solution.py:282
  980.1 147.6 %reduce-scatter.12.cloned.1.call-done = bf16[256,2048]{1,0:T(8,128)(2,1)} async-done(((bf16[2048,2048]{1,0:T(8,128)(2,1)}), bf16[256,2048]{1,0:T(8,128)(2,1)}) %reduce-scatter.12.cloned.1.call-update) | async-done | bytes 1048592 | tf_op jit(solution)/shard_map/reduce_scatter | solution.py:279
  1130.4 147.3 %reduce-scatter.10.cloned.1.call-done = bf16[256,2048]{1,0:T(8,128)(2,1)} async-done(((bf16[2048,2048]{1,0:T(8,128)(2,1)}), bf16[256,2048]{1,0:T(8,128)(2,1)}) %reduce-scatter.10.cloned.1.call-update) | async-done | bytes 1048592 | tf_op jit(solution)/shard_map/reduce_scatter | solution.py:276
  (254 shorter events, 203.3 us)
Async XLA Ops:
  7.2 66.4 %all-gather.8.cloned.1.call-start = ((), (), s32[]{:S(2)}) async-start(), calls=%async_computation.5 | async-start | bytes 3538944 | tf_op jit(solution)/shard_map/all_gather | solution.py:213
  9.1 121.9 %all-gather.10.cloned.1.call-start = ((), (), s32[]{:S(2)}) async-start(), calls=%async_computation.6 | async-start | bytes 2359296 | tf_op jit(solution)/shard_map/all_gather | solution.py:220
  9.8 240.2 %all-gather.16.cloned.1.call-start = ((), (), s32[]{:S(2)}) async-start(), calls=%async_computation.9 | async-start | bytes 9437184 | tf_op jit(solution)/shard_map/all_gather | solution.py:247
  10.6 364.2 %all-gather.14.cloned.1.call-start = ((), (), s32[]{:S(2)}) async-start(), calls=%async_computation.8 | async-start | bytes 9437184 | tf_op jit(solution)/shard_map/all_gather | solution.py:246
  11.2 488.2 %all-gather.12.cloned.1.call-start = ((), (), s32[]{:S(2)}) async-start(), calls=%async_computation.7 | async-start | bytes 9437184 | tf_op jit(solution)/shard_map/all_gather | solution.py:245
  11.7 904.1 %reduce-scatter.8.cloned.1.call-start = ((), (), s32[]{:S(2)}) async-start(), calls=%async_computation.11 | async-start | bytes 2359296 | tf_op jit(solution)/shard_map/reduce_scatter | solution.py:331
  15.5 28.8 %copy-start.39 = (f32[1024]{0:T(1024)}, f32[1024]{0:T(1024)S(1)}, u32[]{:S(2)}) copy-start(f32[1024]{0:T(1024)S(1)} %add_rsqrt_fusion.1) | copy-start | bytes 12292
  38.9 42.8 %copy-start.18 = (f32[1024,32]{0,1:T(8,128)}, f32[1024,32]{0,1:T(8,128)S(1)}, u32[]{:S(2)}) copy-start(f32[1024,32]{0,1:T(8,128)S(1)} %get-tuple-element.71) | copy-start | bytes 393220
  38.9 42.8 %copy-start.20 = (f32[1024,32]{0,1:T(8,128)}, f32[1024,32]{0,1:T(8,128)S(1)}, u32[]{:S(2)}) copy-start(f32[1024,32]{0,1:T(8,128)S(1)} %get-tuple-element.72) | copy-start | bytes 393220
  139.1 4.4 collective-permute-start
  145.8 48.8 %copy-start.44 = (bf16[256]{0:T(256)(128)(2,1)S(1)}, bf16[256]{0:T(256)(128)(2,1)}, u32[]{:S(2)}) copy-start(bf16[256]{0:T(256)(128)(2,1)} %param.19) | copy-start | bytes 1540
  145.8 47.7 %collective-permute-start.1 = (bf16[512,2048]{1,0:T(8,128)(2,1)S(1)}, bf16[512,2048]{1,0:T(8,128)(2,1)S(1)}, u32[]{:S(2)}, u32[]{:S(2)}) collective-permute-start(bf16[512,2048]{1,0:T(8,128)(2,1)S(1)} %add_convert_fusion.10), channel_id=1, source_target_pairs={{0,2},{1,3},{2,0},{3,1},{4,6},{5,7},{6,4},{7,5},{8,10},{9,11},{10,... | collective-permute-start | bytes 6291464 | tf_op jit(solution)/shard_map/ppermute | solution.py:178
  194.5 424.4 %copy-start.6 = (bf16[512,2048]{1,0:T(8,128)(2,1)}, bf16[512,2048]{1,0:T(8,128)(2,1)S(1)}, u32[]{:S(2)}) copy-start(bf16[512,2048]{1,0:T(8,128)(2,1)S(1)} %add_convert_fusion.9) | copy-start | bytes 6291460
  194.5 19.5 %collective-permute-start.2 = (bf16[512,2048]{1,0:T(8,128)(2,1)S(1)}, bf16[512,2048]{1,0:T(8,128)(2,1)}, u32[]{:S(2)}, u32[]{:S(2)}) collective-permute-start(bf16[512,2048]{1,0:T(8,128)(2,1)S(1)} %add_convert_fusion.9), channel_id=1, source_target_pairs={{0,1},{1,0},{2,3},{3,2},{4,5},{5,4},{6,7},{7,6},{8,9},{9,8},{10,11... | collective-permute-start | bytes 6291464 | tf_op jit(solution)/shard_map/ppermute | solution.py:180
  219.0 399.8 %copy-start.37 = (f32[1024]{0:T(1024)}, f32[1024]{0:T(1024)S(1)}, u32[]{:S(2)}) copy-start(f32[1024]{0:T(1024)S(1)} %add_rsqrt_fusion) | copy-start | bytes 12292
  550.2 4.2 collective-permute-start.6
  555.4 52.9 %copy-start.1 = (bf16[1024,2048]{1,0:T(8,128)(2,1)S(1)}, bf16[1024,2048]{1,0:T(8,128)(2,1)}, u32[]{:S(2)}) copy-start(bf16[1024,2048]{1,0:T(8,128)(2,1)} %param.13) | copy-start | bytes 12582916
  555.4 47.7 %collective-permute-start.7 = (bf16[512,2048]{1,0:T(8,128)(2,1)S(1)}, bf16[512,2048]{1,0:T(8,128)(2,1)S(1)}, u32[]{:S(2)}, u32[]{:S(2)}) collective-permute-start(bf16[512,2048]{1,0:T(8,128)(2,1)S(1)} %add_convert_fusion.6), channel_id=1, source_target_pairs={{0,2},{1,3},{2,0},{3,1},{4,6},{5,7},{6,4},{7,5},{8,10},{9,11},{10,... | collective-permute-start | bytes 6291464 | tf_op jit(solution)/shard_map/ppermute | solution.py:178
  604.0 4.2 collective-permute-start.8
  681.8 274.1 %reduce-scatter.6.cloned.1.call-start = ((), (), s32[]{:S(2)}) async-start(), calls=%async_computation.10 | async-start | bytes 3538944 | tf_op jit(solution)/shard_map/reduce_scatter | solution.py:321
  740.4 237.0 %reduce-scatter.14.cloned.1.call-start = ((), (), s32[]{:S(2)}) async-start(), calls=%async_computation.14 | async-start | bytes 9437184 | tf_op jit(solution)/shard_map/reduce_scatter | solution.py:282
  754.9 372.8 %reduce-scatter.12.cloned.1.call-start = ((), (), s32[]{:S(2)}) async-start(), calls=%async_computation.13 | async-start | bytes 9437184 | tf_op jit(solution)/shard_map/reduce_scatter | solution.py:279
  769.1 508.6 %reduce-scatter.10.cloned.1.call-start = ((), (), s32[]{:S(2)}) async-start(), calls=%async_computation.12 | async-start | bytes 9437184 | tf_op jit(solution)/shard_map/reduce_scatter | solution.py:276
  797.6 7.9 collective-permute-start.3
  805.2 4.2 collective-permute-start.9
  807.9 48.6 %collective-permute-start.4 = (bf16[512,2048]{1,0:T(8,128)(2,1)S(1)}, bf16[512,2048]{1,0:T(8,128)(2,1)S(1)}, u32[]{:S(2)}, u32[]{:S(2)}) collective-permute-start(bf16[512,2048]{1,0:T(8,128)(2,1)S(1)} %add_convert_fusion.8), channel_id=1, source_target_pairs={{0,2},{1,3},{2,0},{3,1},{4,6},{5,7},{6,4},{7,5},{8,10},{9,11},{10,... | collective-permute-start | bytes 6291464 | tf_op jit(solution)/shard_map/ppermute | solution.py:178
  810.3 90.4 %collective-permute-start.10 = (bf16[512,2048]{1,0:T(8,128)(2,1)S(1)}, bf16[512,2048]{1,0:T(8,128)(2,1)S(1)}, u32[]{:S(2)}, u32[]{:S(2)}) collective-permute-start(bf16[512,2048]{1,0:T(8,128)(2,1)S(1)} %add_convert_fusion.4), channel_id=1, source_target_pairs={{0,2},{1,3},{2,0},{3,1},{4,6},{5,7},{6,4},{7,5},{8,10},{9,11},{10,... | collective-permute-start | bytes 6291464 | tf_op jit(solution)/shard_map/ppermute | solution.py:178
  858.6 44.3 %copy-start.45 = (u32[32]{0:T(128)S(1)}, u32[32]{0:T(128)}, u32[]{:S(2)}) copy-start(u32[32]{0:T(128)} %constant.89) | copy-start | bytes 388
  858.6 45.5 %copy-start.7 = (bf16[512,2048]{1,0:T(8,128)(2,1)S(1)}, bf16[512,2048]{1,0:T(8,128)(2,1)}, u32[]{:S(2)}) copy-start(bf16[512,2048]{1,0:T(8,128)(2,1)} %copy-done.6) | copy-start | bytes 6291460
  858.6 45.5 %copy-start.38 = (f32[1024]{0:T(1024)S(1)}, f32[1024]{0:T(1024)}, u32[]{:S(2)}) copy-start(f32[1024]{0:T(1024)} %copy-done.37) | copy-start | bytes 12292
  858.6 45.5 %collective-permute-start.5 = (bf16[512,2048]{1,0:T(8,128)(2,1)}, bf16[512,2048]{1,0:T(8,128)(2,1)}, u32[]{:S(2)}, u32[]{:S(2)}) collective-permute-start(bf16[512,2048]{1,0:T(8,128)(2,1)} %add_convert_fusion.7), channel_id=1, source_target_pairs={{0,1},{1,0},{2,3},{3,2},{4,5},{5,4},{6,7},{7,6},{8,9},{9,8},{10,11... | collective-permute-start | bytes 6291464 | tf_op jit(solution)/shard_map/ppermute | solution.py:180
  902.8 14.8 %collective-permute-start.11 = (bf16[512,2048]{1,0:T(8,128)(2,1)}, bf16[512,2048]{1,0:T(8,128)(2,1)}, u32[]{:S(2)}, u32[]{:S(2)}) collective-permute-start(bf16[512,2048]{1,0:T(8,128)(2,1)} %add_convert_fusion.3), channel_id=1, source_target_pairs={{0,1},{1,0},{2,3},{3,2},{4,5},{5,4},{6,7},{7,6},{8,9},{9,8},{10,11... | collective-permute-start | bytes 6291464 | tf_op jit(solution)/shard_map/ppermute | solution.py:180
  (49 other events, 454.8 us)
Sparse Core Ops, SparseCore 0:
  10.8 62.7 all-gather.7
  75.6 49.0 all-gather.9
  126.7 123.2 all-gather.15
  252.0 122.6 all-gather.13
  376.7 122.6 all-gather.11
  681.9 67.2 reduce-scatter.7
  752.7 73.7 reduce-scatter.5
  830.2 147.1 reduce-scatter.13
  981.0 146.5 reduce-scatter.11
  1131.1 146.5 reduce-scatter.9

commit v2 on v0

v2 whole, which is shorter than its diff:
```python
import functools

import jax
import jax.numpy as jnp
from jax import lax
from jax.experimental import pallas as pl
from jax.experimental.pallas import tpu as pltpu
from jax.sharding import PartitionSpec as P

HEAD_SIZE = 64
BLOCK = 128
LANES = 128
EPS_NORM = 1e-05
THETA_BASE = 500000.0
NEG_FILL = -1e30
UNIT = 256
ROWS = 256
FOLD = 2
XFIRST = 6
MESH = pl.DeviceIdType.MESH
VMEM = pltpu.VMEM
DMA = pltpu.SemaphoreType.DMA
HBM_SPEC = pl.BlockSpec(memory_space=pl.ANY)
VMEM_SPEC = pl.BlockSpec(memory_space=pltpu.VMEM)
F32 = jnp.float32
BF16 = jnp.bfloat16


def token_layout(lengths_row, total, block):
    blocks_per = (lengths_row + block - 1) // block
    offsets = jnp.cumsum(blocks_per) - blocks_per
    first_token = offsets * block
    indices = jnp.arange(total, dtype=jnp.int32)
    member = (indices[:, None] >= first_token[None, :]) & (blocks_per[None, :] > 0)
    sequence = jnp.sum(member.astype(jnp.int32), axis=1) - 1
    select = sequence[:, None] == jnp.arange(lengths_row.shape[0], dtype=jnp.int32)[None, :]
    begins = jnp.sum(jnp.where(select, first_token[None, :], 0), axis=1)
    limits = jnp.sum(jnp.where(select, lengths_row[None, :], 0), axis=1)
    position = indices - begins
    return (sequence, position, position < limits)


def allowed_pairs(sequence, position, valid, mask_blocks, block):
    total = sequence.shape[0]
    blocks = total // block
    tiled = jnp.broadcast_to(
        mask_blocks[:, None, :, None] > 0, (blocks, block, blocks, block)
    ).reshape(total, total)
    same = sequence[:, None] == sequence[None, :]
    causal = position[None, :] <= position[:, None]
    row = jnp.arange(total, dtype=jnp.int32)
    diagonal = row[:, None] == row[None, :]
    return tiled & same & causal & valid[None, :] | diagonal


def rope_tables(position, head_dim):
    freqs = THETA_BASE ** (-jnp.arange(head_dim // 2, dtype=F32) * 2.0 / head_dim)
    angles = position.astype(F32)[:, None] * freqs[None, :]
    return (jnp.cos(angles), jnp.sin(angles))


def dot(left, right):
    return jnp.dot(left, right, preferred_element_type=F32)


def dot_nt(left, right):
    return lax.dot_general(left, right, (((1,), (1,)), ((), ())), preferred_element_type=F32)


def dot_tn(left, right):
    return lax.dot_general(left, right, (((0,), (0,)), ((), ())), preferred_element_type=F32)


class Place:
    def __init__(self, depth):
        self.depth = depth
        self.me = lax.axis_index("dp")
        self.z = self.me // FOLD
        self.x = self.me % FOLD
        self.right = self.me + FOLD
        self.left = self.me - FOLD
        self.partner = self.z * FOLD + (1 - self.x)
        member = lax.axis_index("tensor")
        self.core = member % 2
        row = member // 2
        self.other = row * 2 + (1 - self.core)
        self.across = (1 - row) * 2 + self.core

    def enter(self):
        count = self.depth * FOLD
        barrier = pltpu.get_barrier_semaphore()
        for step in range(1, count):
            pl.semaphore_signal(
                barrier,
                1,
                device_id={"dp": lax.rem(self.me + step, count)},
                device_id_type=MESH,
            )
        for peer in (self.other, self.across):
            pl.semaphore_signal(barrier, 1, device_id={"tensor": peer}, device_id_type=MESH)
        pl.semaphore_wait(barrier, count + 1)


class Gather:
    def __init__(self, place, g_ref, rows, units, sems, first=0):
        self.place, self.g, self.rows, self.units, self.first = place, g_ref, rows, units, first
        self.z_send, self.z_recv, self.x_send, self.x_recv = sems

    @staticmethod
    def scratch(units, depth):
        return [
            DMA((units, 2, depth)),
            DMA((units, depth)),
            DMA((units, depth)),
            DMA((units, depth)),
        ]

    def block(self, unit, index, count=1):
        start = pl.multiple_of(index * self.rows, self.rows)
        return self.g.at[unit, pl.ds(start, count * self.rows)]

    def along(self, unit, zz, way, wide):
        p = self.place
        if wide:
            ref = self.block(unit, zz * FOLD, FOLD)
        else:
            ref = self.block(unit, zz * FOLD + p.x)
        return pltpu.make_async_remote_copy(
            ref,
            ref,
            self.z_send.at[unit, way, zz],
            self.z_recv.at[unit, zz],
            device_id={"dp": p.left if way else p.right},
            device_id_type=MESH,
        )

    def over(self, unit, zz, incoming=False):
        p = self.place
        ref = self.block(unit, zz * FOLD + (1 - p.x if incoming else p.x))
        return pltpu.make_async_remote_copy(
            ref,
            ref,
            self.x_send.at[unit, zz],
            self.x_recv.at[unit, zz],
            device_id={"dp": p.partner},
            device_id_type=MESH,
        )

    def send_both(self, unit, zz, wide):
        p, last = self.place, self.place.depth - 1

        @pl.when(p.z < last)
        def _():
            self.along(unit, zz, 0, wide).start()

        @pl.when(p.z > 0)
        def _():
            self.along(unit, zz, 1, wide).start()

    def forward(self, unit, step, wide, across):
        p, last = self.place, self.place.depth - 1

        @pl.when(p.z >= step)
        def _():
            zz = p.z - step
            self.along(unit, zz, 0, wide).wait_recv()

            @pl.when(p.z < last)
            def _():
                self.along(unit, zz, 0, wide).start()

            if across:
                self.over(unit, zz).start()

        @pl.when(p.z + step <= last)
        def _():
            zz = p.z + step
            self.along(unit, zz, 1, wide).wait_recv()

            @pl.when(p.z > 0)
            def _():
                self.along(unit, zz, 1, wide).start()

            if across:
                self.over(unit, zz).start()

    def drain(self, unit, wide):
        p, last = self.place, self.place.depth - 1
        for zz in range(p.depth):

            @pl.when((p.z >= zz) & (p.z < last))
            def _():
                self.along(unit, zz, 0, wide).wait_send()

            @pl.when((p.z <= zz) & (p.z > 0))
            def _():
                self.along(unit, zz, 1, wide).wait_send()

    def stage(self, step, unit):
        p, depth = self.place, self.place.depth

        def slow_first():
            if step == 0:
                self.send_both(unit, p.z, False)
                self.over(unit, p.z).start()
            elif step < depth:
                self.forward(unit, step, False, True)
            else:
                for zz in range(depth):
                    self.over(unit, zz, True).wait_recv()
                for zz in range(depth):
                    self.over(unit, zz).wait_send()
                self.drain(unit, False)

        def fast_first():
            if step == 0:
                self.over(unit, p.z).start()
            elif step == 1:
                self.over(unit, p.z, True).wait_recv()
                self.send_both(unit, p.z, True)
            else:
                self.forward(unit, step - 1, True, False)
                if step == depth:
                    self.over(unit, p.z).wait_send()
                    self.drain(unit, True)

        inside = (unit >= 0) & (unit < self.units)
        fast = lax.rem(unit + self.first, XFIRST) == XFIRST - 1
        pl.when(inside & jnp.logical_not(fast))(slow_first)
        pl.when(inside & fast)(fast_first)

    def latency(self):
        return self.place.depth + 1

    def tick(self, time):
        depth = self.place.depth
        for step in range(depth):
            self.stage(step, time - step)
        self.stage(depth, time - depth - 1)


class TensorSum:
    def __init__(self, place, part, bufs, sems):
        self.place, self.part = place, part
        self.half_in, self.half, self.far_in, self.total, self.back = bufs
        self.sends, self.recvs = sems

    @staticmethod
    def scratch(blocks, half, width):
        return [VMEM((blocks, half, width), BF16)] * 5, [DMA((3, blocks)), DMA((3, blocks))]

    def copy(self, step, src, dst, blk):
        p = self.place
        return pltpu.make_async_remote_copy(
            src,
            dst.at[blk],
            self.sends.at[step, blk],
            self.recvs.at[step, blk],
            device_id={"tensor": p.across if step == 1 else p.other},
            device_id_type=MESH,
        )

    def first(self, blk):
        half = self.half.shape[1]
        start = pl.multiple_of((1 - self.place.core) * half, half)
        return self.copy(0, self.part.at[blk, pl.ds(start, half)], self.half_in, blk)

    def second(self, blk):
        return self.copy(1, self.half.at[blk], self.far_in, blk)

    def third(self, blk):
        return self.copy(2, self.total.at[blk], self.back, blk)

    def begin(self, blk):
        self.first(blk).start()

    def middle(self, blk):
        half = self.half.shape[1]
        self.first(blk).wait_recv()
        start = pl.multiple_of(self.place.core * half, half)
        mine = self.part[blk, pl.ds(start, half), :].astype(F32)
        self.half[blk] = (mine + self.half_in[blk].astype(F32)).astype(BF16)
        self.second(blk).start()

    def late(self, blk):
        self.second(blk).wait_recv()
        self.total[blk] = (self.half[blk].astype(F32) + self.far_in[blk].astype(F32)).astype(BF16)
        self.third(blk).start()

    def end(self, blk):
        half = self.half.shape[1]
        self.third(blk).wait_recv()
        core = self.place.core
        return (
            (pl.multiple_of(blk * 2 * half + core * half, half), self.total),
            (pl.multiple_of(blk * 2 * half + (1 - core) * half, half), self.back),
        )

    def drain(self, blk):
        self.first(blk).wait_send()
        self.second(blk).wait_send()
        self.third(blk).wait_send()


def turn(values, cosine, sine, back=False):
    half = HEAD_SIZE // 2
    lane = lax.broadcasted_iota(jnp.int32, (1, LANES), 1)
    low = lax.rem(lane, HEAD_SIZE) < half
    tiles = []
    for start in range(0, values.shape[1], LANES):
        tile = values[:, start : start + LANES]
        swapped = jnp.where(low, pltpu.roll(tile, LANES - half, 1), pltpu.roll(tile, half, 1))
        if back:
            tiles.append(tile * cosine - swapped * sine)
        else:
            tiles.append(tile * cosine + swapped * sine)
    return tiles[0] if len(tiles) == 1 else jnp.concatenate(tiles, axis=1)


def probabilities(query, keys, allowed):
    scores = dot_nt(query, keys) * HEAD_SIZE ** (-0.5)
    scores = jnp.where(allowed, scores, NEG_FILL)
    expo = jnp.exp(scores - jnp.max(scores, axis=-1, keepdims=True))
    return expo / jnp.sum(expo, axis=-1, keepdims=True)


def normed(stream):
    return stream * lax.rsqrt(jnp.mean(stream * stream, axis=-1, keepdims=True) + EPS_NORM)


def attend_kernel(cfg, *refs):
    (
        x_ref,
        w_ref,
        gain_ref,
        mask_ref,
        cos_ref,
        sin_ref,
        g_ref,
        a_ref,
        q_ref,
        k_ref,
        v_ref,
        att_ref,
        sum_ref,
        b_ref,
        gain_in,
        gains,
        weights,
        part,
        half_in,
        half,
        far_in,
        total,
        back,
        sum_sends,
        sum_recvs,
        z_send,
        z_recv,
        x_send,
        x_recv,
        gain_send,
        gain_recv,
        local_sem,
    ) = refs
    depth, units, q_units, o_units = cfg
    place = Place(depth)
    count = depth * FOLD
    token_count, width = x_ref.shape
    rows = w_ref.shape[1]
    blocks = token_count // ROWS
    fill = pltpu.make_async_copy(
        w_ref, g_ref.at[:, pl.ds(pl.multiple_of(place.me * rows, rows), rows)], local_sem
    )
    fill.start()
    place.enter()
    fill.wait()
    gather = Gather(place, g_ref, rows, units, (z_send, z_recv, x_send, x_recv))
    summer = TensorSum(place, part, (half_in, half, far_in, total, back), (sum_sends, sum_recvs))

    def gain_copy(step):
        return pltpu.make_async_remote_copy(
            gain_ref,
            gain_in.at[place.me],
            gain_send.at[step],
            gain_recv.at[place.me],
            device_id={"dp": lax.rem(place.me + step, count)},
            device_id_type=MESH,
        )

    def gain_arrival(source):
        return pltpu.make_async_remote_copy(
            gain_ref,
            gain_in.at[source],
            gain_send.at[0],
            gain_recv.at[source],
            device_id={"dp": place.partner},
            device_id_type=MESH,
        )

    lane = lax.broadcasted_iota(jnp.int32, (1, LANES), 1)
    low_half = lane < HEAD_SIZE

    def spread_gains():
        gain_in[place.me] = gain_ref[...]
        for step in range(1, count):
            gain_arrival(lax.rem(place.me + step, count)).wait_recv()
        for source in range(count):
            gains[:, source * rows : (source + 1) * rows] = gain_in[source]

    def norm_block(blk):
        rows_at = pl.ds(pl.multiple_of(blk * ROWS, ROWS), ROWS)
        stream = x_ref[rows_at, :].astype(F32)
        a_ref[rows_at, :] = (normed(stream) * gains[0:1, :]).astype(BF16)

    def load(unit):
        copy = pltpu.make_async_copy(g_ref.at[unit], weights.at[unit], local_sem)
        copy.start()
        copy.wait()

    def project(unit):
        load(unit)

        def block(blk, _):
            rows_at = pl.ds(pl.multiple_of(blk * ROWS, ROWS), ROWS)
            cosine, sine = cos_ref[rows_at, :], sin_ref[rows_at, :]
            out = dot(a_ref[rows_at, :], weights[unit])
            if unit < q_units:
                q_ref[rows_at, unit * UNIT : (unit + 1) * UNIT] = turn(out, cosine, sine).astype(
                    BF16
                )
            else:
                kv = k_ref.shape[1]
                k_ref[rows_at, :] = turn(out[:, :kv], cosine, sine).astype(BF16)
                v_ref[rows_at, :] = out[:, kv:].astype(BF16)
            return 0

        lax.fori_loop(0, blocks, block, 0)

    def attend(blk):
        start, stop = blk * ROWS, (blk + 1) * ROWS
        allowed = mask_ref[start:stop, :stop] > 0
        keys, values = k_ref[:stop, :], v_ref[:stop, :]

        def pair(index, _):
            lanes = pl.ds(pl.multiple_of(index * LANES, LANES), LANES)
            query = q_ref[start:stop, lanes]
            outs = []
            for first in (True, False):
                keep = low_half if first else jnp.logical_not(low_half)
                masked = jnp.where(keep, query, jnp.zeros_like(query))
                probs = probabilities(masked, keys, allowed).astype(BF16)
                outs.append(dot(probs, values))
            att_ref[start:stop, lanes] = jnp.where(low_half, outs[0], outs[1]).astype(BF16)
            return 0

        lax.fori_loop(0, q_ref.shape[1] // LANES, pair, 0)

    def emit(blk):
        first = q_units + 1
        out = None
        for number in range(o_units):
            cols = slice(number * UNIT, (number + 1) * UNIT)
            piece = dot_nt(att_ref[blk * ROWS : (blk + 1) * ROWS, cols], weights[first + number])
            out = piece if out is None else out + piece
        part[blk] = out.astype(BF16)
        summer.begin(blk)

    def finish(blk):
        for row, values in summer.end(blk):
            rows_at = pl.ds(row, ROWS // 2)
            added = values[blk]
            sum_ref[rows_at, :] = added
            stream = x_ref[rows_at, :].astype(F32) + added.astype(F32)
            b_ref[rows_at, :] = (normed(stream) * gains[1:2, :]).astype(BF16)

    ready = gather.latency()
    schedule = []
    for unit in range(q_units + 1):
        schedule.append((ready + unit, functools.partial(project, unit)))
    for unit in range(q_units + 1, q_units + 1 + o_units):
        schedule.append((ready + unit, functools.partial(load, unit)))
    base = ready + q_units + 1
    for blk in range(blocks):
        schedule.append((base + blk, functools.partial(attend, blk)))
        schedule.append((base + o_units + blk, functools.partial(emit, blk)))
        schedule.append((base + o_units + blk + 1, functools.partial(summer.middle, blk)))
        schedule.append((base + o_units + blk + 3, functools.partial(summer.late, blk)))
        schedule.append((base + o_units + blk + 4, functools.partial(finish, blk)))
    schedule.sort(key=lambda item: item[0])
    length = max(units + ready, base + o_units + blocks + 4)

    for step in range(1, count):
        gain_copy(step).start()

    def body(time, _):
        gather.tick(time)
        pl.when(time == 0)(spread_gains)

        @pl.when(time < blocks)
        def _():
            norm_block(time)

        for when, work in schedule:
            pl.when(time == when)(work)
        return 0

    lax.fori_loop(0, length, body, 0)
    for blk in range(blocks):
        summer.drain(blk)
    for step in range(1, count):
        gain_copy(step).wait_send()


def attend(tokens, own, gain_rows, mask, cosine, sine, depth, q_units, o_units):
    token_count, width = tokens.shape
    units, rows, cols = own.shape
    blocks, half = token_count // ROWS, ROWS // 2
    q_width = q_units * UNIT
    kv_width = UNIT // 2
    sum_bufs, sum_sems = TensorSum.scratch(blocks, half, width)
    count = depth * FOLD

    def out(*shape):
        return jax.ShapeDtypeStruct(shape, BF16)

    return pl.pallas_call(
        functools.partial(attend_kernel, (depth, units, q_units, o_units)),
        out_shape=(
            out(units, width, cols),
            out(token_count, width),
            out(token_count, q_width),
            out(token_count, kv_width),
            out(token_count, kv_width),
            out(token_count, q_width),
            out(token_count, width),
            out(token_count, width),
        ),
        in_specs=[VMEM_SPEC] * 6,
        out_specs=[HBM_SPEC] + [VMEM_SPEC] * 7,
        scratch_shapes=[
            VMEM((count, 8, rows), F32),
            VMEM((8, width), F32),
            VMEM((q_units + 1 + o_units, width, cols), BF16),
            VMEM((blocks, ROWS, width), BF16),
            *sum_bufs,
            *sum_sems,
            *Gather.scratch(units, depth),
            DMA((count,)),
            DMA((count,)),
            DMA,
        ],
        compiler_params=pltpu.CompilerParams(
            collective_id=0, has_side_effects=True, vmem_limit_bytes=60 << 20
        ),
        name="attend",
    )(tokens, own, gain_rows, mask, cosine, sine)


class Scatter:
    SLOTS = 4

    def __init__(self, place, rows, units, refs, first=0):
        self.place, self.rows, self.units, self.first = place, rows, units, first
        (
            self.grads,
            self.x_in,
            self.z_in,
            self.kept,
            self.mine,
            self.theirs,
            self.summed,
            self.x_send,
            self.x_recv,
            self.z_send,
            self.z_recv,
            self.load_sem,
            self.keep_sem,
        ) = refs

    @staticmethod
    def scratch(units, depth, rows):
        return [
            VMEM((depth, rows, UNIT), BF16),
            VMEM((depth, rows, UNIT), BF16),
            VMEM((Scatter.SLOTS, depth, rows, UNIT), BF16),
            DMA((units, depth)),
            DMA((units, depth)),
            DMA((units, depth)),
            DMA((units, depth)),
            DMA((2, depth)),
            DMA((Scatter.SLOTS,)),
        ]

    @staticmethod
    def outputs(units, depth, rows):
        return (
            jax.ShapeDtypeStruct((units, depth, rows, UNIT), BF16),
            jax.ShapeDtypeStruct((units, depth, rows, UNIT), BF16),
            jax.ShapeDtypeStruct((units, rows, UNIT), BF16),
        )

    def block(self, unit, index):
        start = pl.multiple_of(index * self.rows, self.rows)
        return self.grads.at[unit + self.first, pl.ds(start, self.rows)]

    def over(self, unit, zz):
        p = self.place
        return pltpu.make_async_remote_copy(
            self.block(unit, zz * FOLD + 1 - p.x),
            self.x_in.at[unit, zz],
            self.x_send.at[unit, zz],
            self.x_recv.at[unit, zz],
            device_id={"dp": p.partner},
            device_id_type=MESH,
        )

    def along(self, unit, step):
        p = self.place
        dest = lax.rem(p.z + step, p.depth)
        slot = lax.rem(unit, self.SLOTS)
        return pltpu.make_async_remote_copy(
            self.summed.at[slot, dest],
            self.z_in.at[unit, step],
            self.z_send.at[unit, step],
            self.z_recv.at[unit, step],
            device_id={"dp": dest * FOLD + p.x},
            device_id_type=MESH,
        )

    def keep(self, unit):
        slot = lax.rem(unit, self.SLOTS)
        return pltpu.make_async_copy(
            self.summed.at[slot, self.place.z], self.kept.at[unit], self.keep_sem.at[slot]
        )

    def stage(self, step, unit):
        p = self.place

        @pl.when((unit >= 0) & (unit < self.units))
        def _():
            if step == 0:
                for zz in range(p.depth):
                    self.over(unit, zz).start()
            elif step == 1:
                loads = []
                for zz in range(p.depth):
                    loads.append(
                        pltpu.make_async_copy(
                            self.block(unit, zz * FOLD + p.x),
                            self.mine.at[zz],
                            self.load_sem.at[0, zz],
                        )
                    )
                    loads[-1].start()
                for zz in range(p.depth):
                    self.over(unit, zz).wait_recv()
                    loads.append(
                        pltpu.make_async_copy(
                            self.x_in.at[unit, zz], self.theirs.at[zz], self.load_sem.at[1, zz]
                        )
                    )
                    loads[-1].start()
                for copy in loads:
                    copy.wait()
                slot = lax.rem(unit, self.SLOTS)
                for zz in range(p.depth):
                    self.summed[slot, zz] = (
                        self.mine[zz].astype(F32) + self.theirs[zz].astype(F32)
                    ).astype(BF16)
                for way in range(1, p.depth):
                    self.along(unit, way).start()
                self.keep(unit).start()
            else:
                for zz in range(p.depth):
                    self.over(unit, zz).wait_send()
                for way in range(1, p.depth):
                    self.along(unit, way).wait_send()
                self.keep(unit).wait()

    def tick(self, time):
        self.stage(2, time - 1 - (self.SLOTS - 1))
        self.stage(0, time)
        self.stage(1, time - 1)

    def latency(self):
        return 1 + self.SLOTS

    def finish(self):
        def unit_end(unit, _):
            for way in range(1, self.place.depth):
                self.along(unit, way).wait_recv()
            return 0

        lax.fori_loop(0, self.units, unit_end, 0)


def feed_kernel(cfg, *refs):
    (
        b_ref,
        cot_ref,
        g_ref,
        grads_ref,
        x_in,
        z_in,
        kept,
        out_ref,
        db_ref,
        acc_out,
        acc_db,
        weights,
        grad_buf,
        hidden,
        dgu,
        part,
        half_in,
        half,
        far_in,
        total,
        back,
        sum_sends,
        sum_recvs,
        weight_sem,
        grad_sem,
        local_sem,
        *scatter_refs,
    ) = refs
    depth, first_unit, chunks, pace, scatter_units = cfg
    place = Place(depth)
    token_count, width = b_ref.shape
    rows = x_in.shape[2]
    blocks = token_count // ROWS
    tall = 2 * ROWS
    scatter = Scatter(place, rows, scatter_units, (grads_ref, x_in, z_in, kept, *scatter_refs))
    summer = TensorSum(place, part, (half_in, half, far_in, total, back), (sum_sends, sum_recvs))

    def load(chunk, matrix):
        slot = lax.rem(chunk, 2)
        return pltpu.make_async_copy(
            g_ref.at[first_unit + 3 * chunk + matrix],
            weights.at[slot, matrix],
            weight_sem.at[slot, matrix],
        )

    def save(chunk, matrix):
        slot = lax.rem(chunk, 2)
        return pltpu.make_async_copy(
            grad_buf.at[slot, matrix],
            grads_ref.at[3 * chunk + matrix],
            grad_sem.at[slot, matrix],
        )

    for matrix in range(3):
        load(0, matrix).start()
    place.enter()

    def clear(blk, _):
        rows_at = pl.ds(pl.multiple_of(blk * ROWS, ROWS), ROWS)
        acc_out[rows_at, :] = jnp.zeros((ROWS, width), F32)
        acc_db[rows_at, :] = jnp.zeros((ROWS, width), F32)
        return 0

    lax.fori_loop(0, blocks, clear, 0)

    def compute(chunk, slot):
        def hidden_rows(blk, _):
            rows_at = pl.ds(pl.multiple_of(blk * tall, tall), tall)
            stream, cot = b_ref[rows_at, :], cot_ref[rows_at, :]
            gate = dot(stream, weights[slot, 0])
            upper = dot(stream, weights[slot, 1])
            grad_hidden = dot(cot, weights[slot, 2])
            sigmoid = jax.nn.sigmoid(gate)
            silu = gate * sigmoid
            hid = (silu * upper).astype(BF16)
            grad_gate = (grad_hidden * upper * sigmoid * (1.0 + gate * (1.0 - sigmoid))).astype(
                BF16
            )
            grad_up = (grad_hidden * silu).astype(BF16)
            hidden[rows_at, :] = hid
            dgu[rows_at, :UNIT] = grad_gate
            dgu[rows_at, UNIT:] = grad_up

            def spread(piece, _):
                cols = pl.ds(pl.multiple_of(piece * tall, tall), tall)
                acc_out[rows_at, cols] += dot_nt(hidden[rows_at, :], weights[slot, 2, cols, :])
                acc_db[rows_at, cols] += dot_nt(
                    dgu[rows_at, :UNIT], weights[slot, 0, cols, :]
                ) + dot_nt(dgu[rows_at, UNIT:], weights[slot, 1, cols, :])
                return 0

            lax.fori_loop(0, width // tall, spread, 0)
            return 0

        lax.fori_loop(0, token_count // tall, hidden_rows, 0)

        def grad_rows(blk, _):
            cols = pl.ds(pl.multiple_of(blk * ROWS, ROWS), ROWS)
            both = dot_tn(b_ref[:, cols], dgu[...])
            grad_buf[slot, 0, cols, :] = both[:, :UNIT].astype(BF16)
            grad_buf[slot, 1, cols, :] = both[:, UNIT:].astype(BF16)
            grad_buf[slot, 2, cols, :] = dot_tn(cot_ref[:, cols], hidden[...]).astype(BF16)
            return 0

        lax.fori_loop(0, width // ROWS, grad_rows, 0)

    def step(chunk, _):
        slot = lax.rem(chunk, 2)
        for matrix in range(3):
            load(chunk, matrix).wait()

        @pl.when(chunk + 1 < chunks)
        def _():
            for matrix in range(3):
                load(chunk + 1, matrix).start()

        compute(chunk, slot)
        for matrix in range(3):
            save(chunk, matrix).start()
        for matrix in range(3):
            save(chunk, matrix).wait()
        for number in range(pace):
            scatter.tick(chunk * pace + number)
        return 0

    lax.fori_loop(0, chunks, step, 0)
    time = chunks * pace
    length = scatter_units + scatter.latency()
    for blk in range(blocks):
        rows_at = slice(blk * ROWS, (blk + 1) * ROWS)
        part[blk] = acc_out[rows_at, :].astype(BF16)
        copy = pltpu.make_async_copy(part.at[blk], out_ref.at[pl.ds(blk * ROWS, ROWS)], local_sem)
        copy.start()
        copy.wait()
        part[blk] = acc_db[rows_at, :].astype(BF16)
        summer.begin(blk)
    schedule = []
    for blk in range(blocks):
        schedule.append((blk, functools.partial(summer.middle, blk)))
        schedule.append((blk + 2, functools.partial(summer.late, blk)))

        def finish(blk=blk):
            copies = []
            for (row, values), sem in zip(summer.end(blk), (0, 1)):
                copies.append(
                    pltpu.make_async_copy(
                        values.at[blk], db_ref.at[pl.ds(row, ROWS // 2)], grad_sem.at[sem, 0]
                    )
                )
                copies[-1].start()
            for copy in copies:
                copy.wait()

        schedule.append((blk + 3, finish))
    schedule.sort(key=lambda item: item[0])

    def tail(now, _):
        scatter.tick(time + now)
        for when, work in schedule:
            pl.when(now == when)(work)
        return 0

    lax.fori_loop(0, max(length - time, blocks + 3), tail, 0)
    scatter.finish()
    for blk in range(blocks):
        summer.drain(blk)


def feed(b, cotangent, gathered, depth, first_unit, chunks, pace, scatter_units):
    token_count, width = b.shape
    rows = width // (depth * FOLD)
    blocks, half = token_count // ROWS, ROWS // 2
    sum_bufs, sum_sems = TensorSum.scratch(blocks, half, width)
    full = jax.ShapeDtypeStruct((token_count, width), BF16)
    return pl.pallas_call(
        functools.partial(feed_kernel, (depth, first_unit, chunks, pace, scatter_units)),
        out_shape=(
            jax.ShapeDtypeStruct((3 * chunks, width, UNIT), BF16),
            *Scatter.outputs(scatter_units, depth, rows),
            full,
            full,
        ),
        in_specs=[VMEM_SPEC, VMEM_SPEC, HBM_SPEC],
        out_specs=[HBM_SPEC] * 6,
        scratch_shapes=[
            VMEM((token_count, width), F32),
            VMEM((token_count, width), F32),
            VMEM((2, 3, width, UNIT), BF16),
            VMEM((2, 3, width, UNIT), BF16),
            VMEM((token_count, UNIT), BF16),
            VMEM((token_count, 2 * UNIT), BF16),
            VMEM((blocks, ROWS, width), BF16),
            *sum_bufs,
            *sum_sems,
            DMA((2, 3)),
            DMA((2, 3)),
            DMA,
            *Scatter.scratch(scatter_units, depth, rows),
        ],
        compiler_params=pltpu.CompilerParams(
            collective_id=1, has_side_effects=True, vmem_limit_bytes=63 << 20
        ),
        name="feed",
    )(b, cotangent, gathered)


def tensor_sum(partial):
    rows = partial.shape[0] // 2
    core = lax.axis_index("tensor") % 2
    count = lax.axis_size("tensor")
    flip_core = [(i, i ^ 1) for i in range(count)]
    flip_y = [(i, i ^ 2) for i in range(count)]
    mine = lax.dynamic_slice_in_dim(partial, core * rows, rows, axis=0)
    other = lax.dynamic_slice_in_dim(partial, (1 - core) * rows, rows, axis=0)
    received = lax.ppermute(other, "tensor", flip_core)
    chip = (mine.astype(F32) + received.astype(F32)).astype(BF16)
    across = lax.ppermute(chip, "tensor", flip_y)
    total = (chip.astype(F32) + across.astype(F32)).astype(BF16)
    back = lax.ppermute(total, "tensor", flip_core)
    return jnp.where(
        core == 0,
        jnp.concatenate([total, back], axis=0),
        jnp.concatenate([back, total], axis=0),
    )


def norm_parts(stream):
    inverse = lax.rsqrt(jnp.mean(stream * stream, axis=-1, keepdims=True) + EPS_NORM)
    return (stream * inverse, inverse)


def norm_back(grad_normed, gain, normalized_input, inverse):
    scaled = grad_normed * gain[None, :]
    return inverse * (
        scaled - normalized_input * jnp.mean(scaled * normalized_input, axis=-1, keepdims=True)
    )


def rotate_back(value_vectors, cosine, sine):
    half = value_vectors.shape[-1] // 2
    first = value_vectors[..., :half]
    second = value_vectors[..., half:]
    return jnp.concatenate(
        [first * cosine + second * sine, second * cosine - first * sine], axis=-1
    )


def attention_backward(query_vectors, key_vectors, value_vectors, grad_out, allowed):
    token_positions = query_vectors.shape[0]
    rows = 512
    grad_queries = []
    grad_keys = jnp.zeros(key_vectors.shape, F32)
    grad_values = jnp.zeros(value_vectors.shape, F32)
    for begin_row in range(0, token_positions, rows):
        query_block = query_vectors[begin_row : begin_row + rows]
        grad_block = grad_out[begin_row : begin_row + rows]
        scores = jnp.einsum(
            "qkgd,skd->kgqs", query_block, key_vectors, preferred_element_type=F32
        ) * HEAD_SIZE ** (-0.5)
        scores = jnp.where(allowed[begin_row : begin_row + rows][None, None], scores, NEG_FILL)
        probs = jax.nn.softmax(scores, axis=-1)
        grad_probs = jnp.einsum(
            "qkgd,skd->kgqs", grad_block, value_vectors, preferred_element_type=F32
        )
        centre = jnp.sum(probs * grad_probs, axis=-1, keepdims=True)
        grad_scores = (probs * (grad_probs - centre)).astype(BF16)
        grad_queries.append(
            jnp.einsum("kgqs,skd->qkgd", grad_scores, key_vectors, preferred_element_type=F32)
            * HEAD_SIZE ** (-0.5)
        )
        grad_keys = grad_keys + jnp.einsum(
            "kgqs,qkgd->skd", grad_scores, query_block, preferred_element_type=F32
        ) * HEAD_SIZE ** (-0.5)
        grad_values = grad_values + jnp.einsum(
            "kgqs,qkgd->skd", probs.astype(BF16), grad_block, preferred_element_type=F32
        )
    return (jnp.concatenate(grad_queries, axis=0), grad_keys, grad_values)


def gathered_units(mine, arrived):
    total = mine.astype(F32)
    for step in range(1, arrived.shape[1]):
        total = total + arrived[:, step].astype(F32)
    return total


def shards(
    depth,
    tokens,
    attention_gain,
    query_matrix,
    key_matrix,
    value_matrix,
    output_weight,
    feed_gain,
    gate_weight,
    up_weight,
    down_weight,
    sequence_lengths,
    block_mask,
    cotangent,
):
    token_count, width = tokens.shape
    rows, q_width = query_matrix.shape
    kv_width = key_matrix.shape[1]
    heads_kv = kv_width // HEAD_SIZE
    groups = q_width // kv_width
    feed_width = gate_weight.shape[1]
    chunks = feed_width // UNIT
    q_units = q_width // UNIT

    def pair(cols):
        return cols.reshape(-1, heads_kv, groups, HEAD_SIZE).swapaxes(1, 2).reshape(-1, q_width)

    def unpair(cols):
        return cols.reshape(-1, groups, heads_kv, HEAD_SIZE).swapaxes(1, 2).reshape(-1, q_width)

    def split(cols):
        return cols.reshape(rows, -1, UNIT).swapaxes(0, 1)

    feed_units = jnp.stack(
        [split(gate_weight), split(up_weight), split(down_weight.T)], axis=1
    ).reshape(3 * chunks, rows, UNIT)
    own = jnp.concatenate(
        [
            split(pair(query_matrix)),
            split(jnp.concatenate([key_matrix, value_matrix], axis=1)),
            split(pair(output_weight.T)),
            feed_units,
        ],
        axis=0,
    )
    sequence, position, valid = token_layout(sequence_lengths[0], token_count, BLOCK)
    allowed = allowed_pairs(sequence, position, valid, block_mask, BLOCK)
    cosine, sine = rope_tables(position, HEAD_SIZE)
    wide_cos = jnp.concatenate([cosine] * 4, axis=1)
    wide_sin = jnp.concatenate([-sine, sine] * 2, axis=1)
    gain_rows = jnp.concatenate(
        [
            attention_gain.astype(F32)[None],
            feed_gain.astype(F32)[None],
            jnp.zeros((6, rows), F32),
        ],
        axis=0,
    )
    first_unit = 2 * q_units + 1
    gathered, a, q, k, v, att, att_sum, b = attend(
        tokens, own, gain_rows, allowed.astype(F32), wide_cos, wide_sin, depth, q_units, q_units
    )
    grads, _, z_in, kept, out_part, db = feed(
        b, cotangent, gathered, depth, first_unit, chunks, PACE, 3 * chunks
    )
    stream = tokens.astype(F32)
    middle = stream + att_sum.astype(F32)
    block_output = (middle + tensor_sum(out_part).astype(F32)).astype(BF16)
    gain_one = lax.all_gather(attention_gain, "dp", axis=0, tiled=True).astype(F32)
    gain_two = lax.all_gather(feed_gain, "dp", axis=0, tiled=True).astype(F32)
    normed_two, inverse_two = norm_parts(middle)
    grad_normed_two = db.astype(F32)
    feed_gain_full = jnp.sum(grad_normed_two * normed_two, axis=0)
    grad_middle = cotangent.astype(F32) + norm_back(
        grad_normed_two, gain_two, normed_two, inverse_two
    )
    grad_middle_low = grad_middle.astype(BF16)
    out_t = jnp.concatenate([gathered[q_units + 1 + i] for i in range(q_units)], axis=1)
    query_full = jnp.concatenate([gathered[i] for i in range(q_units)], axis=1)
    kv_full = gathered[q_units]
    output_grad = dot_tn(att, grad_middle_low)
    grad_attended = dot(grad_middle_low, out_t).astype(BF16)

    def heads(cols):
        return unpair(cols).reshape(token_count, heads_kv, groups, HEAD_SIZE)

    grad_q, grad_k, grad_v = attention_backward(
        heads(q),
        k.reshape(token_count, heads_kv, HEAD_SIZE),
        v.reshape(token_count, heads_kv, HEAD_SIZE),
        heads(grad_attended),
        allowed,
    )
    grad_q = pair(
        rotate_back(grad_q, cosine[:, None, None, :], sine[:, None, None, :])
        .astype(BF16)
        .reshape(token_count, q_width)
    )
    grad_k = (
        rotate_back(grad_k, cosine[:, None, :], sine[:, None, :])
        .astype(BF16)
        .reshape(token_count, kv_width)
    )
    grad_v = grad_v.astype(BF16).reshape(token_count, kv_width)
    grad_kv = jnp.concatenate([grad_k, grad_v], axis=1)
    query_grad = dot_tn(a, grad_q)
    kv_grad = dot_tn(a, grad_kv)
    da = dot_nt(grad_q, query_full) + dot_nt(grad_kv, kv_full)
    da = tensor_sum(da.astype(BF16)).astype(F32)
    normed_one, inverse_one = norm_parts(stream)
    attention_gain_full = jnp.sum(da * normed_one, axis=0)
    input_grad = grad_middle + norm_back(da, gain_one, normed_one, inverse_one)
    packed = jnp.concatenate([query_grad, kv_grad], axis=1).astype(BF16)
    packed = lax.psum_scatter(packed, "dp", scatter_dimension=0, tiled=True).astype(F32)
    out_grad = lax.psum_scatter(
        output_grad.astype(BF16), "dp", scatter_dimension=1, tiled=True
    ).astype(F32)
    gain_grads = lax.psum_scatter(
        jnp.stack([attention_gain_full, feed_gain_full]).astype(F32),
        "dp",
        scatter_dimension=1,
        tiled=True,
    )
    feed_grads = gathered_units(kept, z_in).reshape(chunks, 3, rows, UNIT)

    def join(which):
        return feed_grads[:, which].swapaxes(0, 1).reshape(rows, feed_width)

    out_grad = out_grad.reshape(groups, heads_kv, HEAD_SIZE, rows).swapaxes(0, 1)
    return (
        block_output,
        input_grad,
        gain_grads[0],
        unpair(packed[:, :q_width]),
        packed[:, q_width : q_width + kv_width],
        packed[:, q_width + kv_width :],
        out_grad.reshape(q_width, rows),
        gain_grads[1],
        join(0),
        join(1),
        join(2).T,
    )


PACE = 3


def solution(mesh):
    in_specs = (
        P("dp", None),
        P("dp"),
        P("dp", "tensor"),
        P("dp", "tensor"),
        P("dp", "tensor"),
        P("tensor", "dp"),
        P("dp"),
        P("dp", "tensor"),
        P("dp", "tensor"),
        P("tensor", "dp"),
        P("dp", None),
        P("dp", None),
        P("dp", None),
    )
    out_specs = (
        P("dp", None),
        P("dp", None),
        P("dp"),
        P("dp", "tensor"),
        P("dp", "tensor"),
        P("dp", "tensor"),
        P("tensor", "dp"),
        P("dp"),
        P("dp", "tensor"),
        P("dp", "tensor"),
        P("tensor", "dp"),
    )
    return jax.shard_map(
        functools.partial(shards, mesh.shape["dp"] // FOLD),
        mesh=mesh,
        in_specs=in_specs,
        out_specs=out_specs,
        check_vma=False,
    )
```

time: 1720 us -> 1120 us (0.65)
  waiting for transfers between devices: 1190 us -> 151 us
  Pallas kernels: 0 us -> 665 us
  matrix products: 258 us -> 87.5 us
  blocking collectives: 128 us -> 50.6 us
  local copies, waits for them, and re-layouts: 9.64 us -> 47.9 us
  other arithmetic: 112 us -> 88.8 us
    pallas_call x0 -> x2, Pallas kernels: none -> 665 us  [the longest x1 348 us: feed(): pl.pallas_call(functools.partial(feed_kernel, (depth, first_unit, chunks,...]
    reduce_scatter x7 -> x2, waiting for transfers between devices: 545 us -> 36.6 us  [the longest x1 36.5 us: shards(): lax.psum_scatter(packed, 'dp', scatter_dimension=0, tiled=True).astype(F32)]
    all_gather x5 -> x0, waiting for transfers between devices: 337 us -> none  [the longest x1 116 us: shards(): lax.all_gather(up_weight, 'dp', axis=0, tiled=True)]
    psum x3 -> x0, waiting for transfers between devices: 302 us -> none  [the longest x1 153 us: shards(): lax.psum(feed_part.astype(jnp.bfloat16), 'tensor').astype(jnp.float32)]
    dot_general x27 -> x8, matrix products: 217 us -> 36.6 us  [the longest x2 18 us: attention_backward(): jnp.einsum('kgqs,qkgd->skd', probs.astype(BF16), grad_block, preferred_el...]
    ppermute x0 -> x6, waiting for transfers between devices: none -> 60.5 us  [the longest x2 56.5 us: tensor_sum(): across = lax.ppermute(chip, 'tensor', flip_y)]
    all_gather x4 -> x2, blocking collectives: 105 us -> 50.6 us  [the longest x1 25.8 us: shards(): lax.all_gather(attention_gain, 'dp', axis=0, tiled=True).astype(F32)]
    unnamed x15 -> x4, waiting for transfers between devices: 3.12 us -> 54.2 us
  transfers between devices with their start and end apart: 15 -> 9, of which waited for: 12 -> 5; matrix products, arithmetic and copies ran while one was open for 15% -> 9% of each run, Pallas kernels for 0% -> 0%
where the time goes in v2:
time: 1120 us; the launch traced here: 1110 us
  Pallas kernels  665 us (59%)
  waiting for transfers between devices  151 us (13%)
  other arithmetic  88.8 us (8%)
  matrix products  87.5 us (8%)
  blocking collectives  50.6 us (5%)
  local copies, waits for them, and re-layouts  47.9 us (4%)
  between operations  14.7 us (1%)
    pallas_call x1, Pallas kernels, feed(): pl.pallas_call(functools.partial(feed_kernel, (depth, first_unit, chunks,...  348 us
    pallas_call x1, Pallas kernels, attend(): pl.pallas_call(functools.partial(attend_kernel, (depth, units, q_units, o...  316 us
    ppermute x2, waiting for transfers between devices, tensor_sum(): across = lax.ppermute(chip, 'tensor', flip_y)  56.5 us
    unnamed x4, waiting for transfers between devices  54.2 us
    reduce_scatter x1, waiting for transfers between devices, shards(): lax.psum_scatter(packed, 'dp', scatter_dimension=0, tiled=True).astype(F32)  36.5 us
    all_gather x1, blocking collectives, shards(): lax.all_gather(attention_gain, 'dp', axis=0, tiled=True).astype(F32)  25.8 us
    all_gather x1, blocking collectives, shards(): gain_two = lax.all_gather(feed_gain, 'dp', axis=0, tiled=True).astype(F32)  24.8 us
    convert_element_type x2, other arithmetic, attention_backward(): grad_scores = (probs * (grad_probs - centre)).astype(BF16)  23.2 us
  transfers between devices with their start and end apart: 9, of which 5 were waited for; matrix products, arithmetic and copies ran while one was open for 9% of the time, Pallas kernels for 0%

profile of v2, /device:TPU:0, one launch (start us, length us, event | category | flops | bytes accessed | tf_op | source)
XLA Modules:
  0.0 1109.1 jit_solution(4917198237120665737)
XLA Ops:
  14.9 3.1 bitcast_bitcast_fusion
  23.1 3.8 fusion.112
  30.7 316.4 %attend.1 = (bf16[29,2048,256]{2,1,0:T(8,128)(2,1)}, bf16[1024,2048]{1,0:T(8,128)(2,1)}, bf16[1024,512]{1,0:T(8,128)(2,1)}, bf16[1024,128]{1,0:T(8,128)(2,1)}, b...) custom-call(bf16[1024,2048]{1,0:T(8,128)(2,1)} %refs_0_.1, ...), custom_call_target="tpu_custom_call" | custom-call | tf_op jit(solution)/shard_map/attend/pallas_call | solution.py:527
  347.2 348.3 %feed.1 = (bf16[24,2048,256]{2,1,0:T(8,128)(2,1)}, bf16[24,4,256,256]{3,2,1,0:T(8,128)(2,1)}, bf16[24,4,256,256]{3,2,1,0:T(8,128)(2,1)}, bf16[24,256,256]{2,1,0:...) custom-call(bf16[1024,2048]{1,0:T(8,128)(2,1)} %get-tuple-element.24.refs_0_, ...), custom_call_target="tpu_custom_call" | custom-call | tf_op jit(solution)/shard_map/feed/pallas_call | solution.py:874
  695.4 3.2 constant_dynamic-slice_fusion
  700.2 4.0 collective-permute-done
  707.2 3.6 multiply_reduce_fusion
  710.9 24.8 %all-gather = bf16[8,1,256]{2,1,0:T(2,128)(2,1)S(1)} all-gather(bf16[1,1,256]{2,1,0:T(2,128)(2,1)S(1)} %reshape.320), channel_id=1, replica_groups=mesh['dp'=8,'tensor'=4] {'dp'}, dimensions={0}, use_global_device_ids=true | all-gather | bytes 4608 | tf_op jit(solution)/shard_map/all_gather | solution.py:1056
  735.7 4.2 slice_bitcast_fusion.7
  740.0 5.1 fusion.21
  745.1 9.5 collective-permute-done.1
  769.4 10.6 fusion.117
  780.0 10.6 fusion.122
  790.5 10.9 fusion.20
  801.4 4.4 fusion.53
  806.0 9.6 fusion.60
  815.6 10.7 fusion.5
  826.3 10.7 fusion.2
  836.9 11.5 %fusion.4 = bf16[2,4,512,1024]{2,3,1,0:T(8,128)(2,1)S(1)} fusion(f32[2,1024,512,4]{2,1,3,0:T(8,128)} %get-tuple-element.139, f32[2,4,512]{2,1,0:T(4,128)S(1)} %get-tuple-element.138, f32[2,4,512,1024]{2,3,1,0:T(8,128)} %get-tuple-element.137, f32[2,4,512]{2,1,0:T(4,128)S(1)} %copy-done.22), kind=kLoop, calls=%fused_computation.6 | loop fusion | flops 16777216 | bytes 41975808 | tf_op jit(solution)/shard_map/convert_element_type | solution.py:965
  852.7 11.7 %fusion.7 = bf16[2,4,512,1024]{2,3,1,0:T(8,128)(2,1)S(1)} fusion(f32[2,1024,512,4]{2,1,3,0:T(8,128)} %get-tuple-element.143, f32[2,4,512]{2,1,0:T(4,128)S(1)} %get-tuple-element.142, f32[2,4,512,1024]{2,3,1,0:T(8,128)} %get-tuple-element.141, f32[2,4,512]{2,1,0:T(4,128)S(1)} %copy-done.23), kind=kLoop, calls=%fused_computation.12 | loop fusion | flops 16777216 | bytes 41975808 | tf_op jit(solution)/shard_map/convert_element_type | solution.py:965
  870.1 3.7 convolution_convert_fusion.1
  873.9 4.1 fusion.43
  878.1 8.4 fusion.72
  886.6 2.7 add_convert_fusion
  900.2 47.0 %collective-permute-done.4 = bf16[512,2048]{1,0:T(8,128)(2,1)S(1)} collective-permute-done((bf16[512,2048]{1,0:T(8,128)(2,1)S(1)}, bf16[512,2048]{1,0:T(8,128)(2,1)S(1)}, u32[]{:S(2)}, u32[]{:S(2)}) %collective-permute-start.4) | collective-permute-done | bytes 2097184 | tf_op jit(solution)/shard_map/ppermute | solution.py:916
  948.3 25.8 %all-gather.1 = bf16[8,1,256]{2,1,0:T(2,128)(2,1)S(1)} all-gather(bf16[1,1,256]{2,1,0:T(2,128)(2,1)S(1)} %reshape.322), channel_id=1, replica_groups=mesh['dp'=8,'tensor'=4] {'dp'}, dimensions={0}, use_global_device_ids=true | all-gather | bytes 4608 | tf_op jit(solution)/shard_map/all_gather | solution.py:1055
  974.0 4.7 convert_add_fusion.1
  983.9 2.9 copy.238
  988.7 36.5 %reduce-scatter.6.cloned.1.call-done = bf16[256,768]{0,1:T(8,128)(2,1)} async-done(((bf16[2048,768]{0,1:T(8,128)(2,1)}), bf16[256,768]{0,1:T(8,128)(2,1)}) %reduce-scatter.6.cloned.1.call-update) | async-done | bytes 393232 | tf_op jit(solution)/shard_map/reduce_scatter | solution.py:1100
  1029.7 5.3 fusion.23
  1036.4 9.4 fusion.17
  1045.8 54.2 %reduce-scatter.10.cloned.1.call-done = f32[256,2]{1,0:T(8,128)} async-done(((f32[2048,2]{1,0:T(8,128)}), f32[256,2]{1,0:T(8,128)}) %reduce-scatter.10.cloned.1.call-update) | async-done | bytes 2064
  (152 shorter events, 73.1 us)
Async XLA Ops:
  7.2 10.8 copy-start.18
  7.2 10.8 copy-start.19
  7.2 979.6 %reduce-scatter.8.cloned.1.call-start = ((), (), s32[]{:S(2)}) async-start(), calls=%async_computation.4 | async-start | bytes 2359296 | tf_op jit(solution)/shard_map/reduce_scatter | solution.py:1101
  20.0 6.9 copy-start.5
  698.6 5.6 collective-permute-start
  700.2 7.0 copy-start
  700.2 10.6 copy-start.26
  706.6 48.0 %collective-permute-start.1 = (bf16[512,2048]{1,0:T(8,128)(2,1)S(1)}, bf16[512,2048]{1,0:T(8,128)(2,1)S(1)}, u32[]{:S(2)}, u32[]{:S(2)}) collective-permute-start(bf16[512,2048]{1,0:T(8,128)(2,1)S(1)} %add_convert_fusion.5), channel_id=1, source_target_pairs={{0,2},{1,3},{2,0},{3,1},{4,6},{5,7},{6,4},{7,5},{8,10},{9,11},{10,... | collective-permute-start | bytes 6291464 | tf_op jit(solution)/shard_map/ppermute | solution.py:916
  710.8 29.1 %copy-start.2 = (bf16[1024,2048]{1,0:T(8,128)(2,1)S(1)}, bf16[1024,2048]{1,0:T(8,128)(2,1)}, u32[]{:S(2)}) copy-start(bf16[1024,2048]{1,0:T(8,128)(2,1)} %get-tuple-element.23) | copy-start | bytes 12582916
  710.8 29.1 %copy-start.4 = (bf16[1024,2048]{1,0:T(8,128)(2,1)S(1)}, bf16[1024,2048]{1,0:T(8,128)(2,1)}, u32[]{:S(2)}) copy-start(bf16[1024,2048]{1,0:T(8,128)(2,1)} %get-tuple-element.27) | copy-start | bytes 12582916
  745.1 10.4 copy-start.6
  745.1 13.5 %copy-start.16 = (bf16[1024,128]{1,0:T(8,128)(2,1)S(1)}, bf16[1024,128]{1,0:T(8,128)(2,1)}, u32[]{:S(2)}) copy-start(bf16[1024,128]{1,0:T(8,128)(2,1)} %get-tuple-element.28) | copy-start | bytes 786436
  755.4 35.2 %collective-permute-start.2 = (bf16[512,2048]{1,0:T(8,128)(2,1)S(1)}, bf16[512,2048]{1,0:T(8,128)(2,1)}, u32[]{:S(2)}, u32[]{:S(2)}) collective-permute-start(bf16[512,2048]{1,0:T(8,128)(2,1)S(1)} %add_convert_fusion.4), channel_id=1, source_target_pairs={{0,1},{1,0},{2,3},{3,2},{4,5},{5,4},{6,7},{7,6},{8,9},{9,8},{10,11... | collective-permute-start | bytes 6291464 | tf_op jit(solution)/shard_map/ppermute | solution.py:918
  780.0 10.6 copy-start.24
  790.5 10.9 copy-start.15
  801.4 68.6 %copy-start.1 = (f32[1024,2048]{1,0:T(8,128)}, f32[1024,2048]{1,0:T(8,128)S(1)}, u32[]{:S(2)}) copy-start(f32[1024,2048]{1,0:T(8,128)S(1)} %get-tuple-element.116) | copy-start | bytes 25165828
  801.4 4.5 copy-start.23
  805.9 20.3 %copy-start.10 = (bf16[1024,4,2,64]{0,3,1,2:T(8,128)(2,1)}, bf16[1024,4,2,64]{0,3,1,2:T(8,128)(2,1)S(1)}, u32[]{:S(2)}) copy-start(bf16[1024,4,2,64]{0,3,1,2:T(8,128)(2,1)S(1)} %copy.271) | copy-start | bytes 3145732
  806.0 9.6 copy-start.17
  815.6 10.7 copy-start.22
  873.8 151.4 %reduce-scatter.6.cloned.1.call-start = ((), (), s32[]{:S(2)}) async-start(), calls=%async_computation.3 | async-start | bytes 3538944 | tf_op jit(solution)/shard_map/reduce_scatter | solution.py:1100
  873.9 4.2 copy-start.11
  886.6 4.9 copy-start.25
  889.3 5.8 copy-start.3
  890.9 6.1 collective-permute-start.3
  897.0 51.3 %copy-start.27 = (bf16[256]{0:T(256)(128)(2,1)S(1)}, bf16[256]{0:T(256)(128)(2,1)}, u32[]{:S(2)}) copy-start(bf16[256]{0:T(256)(128)(2,1)} %param.14) | copy-start | bytes 1540
  897.0 203.0 %reduce-scatter.10.cloned.1.call-start = ((), (), s32[]{:S(2)}) async-start(), calls=%async_computation.5 | async-start | bytes 1179648
  897.0 77.0 %copy-start.7 = (bf16[24,256,256]{2,1,0:T(8,128)(2,1)S(1)}, bf16[24,256,256]{2,1,0:T(8,128)(2,1)}, u32[]{:S(2)}) copy-start(bf16[24,256,256]{2,1,0:T(8,128)(2,1)} %get-tuple-element.33) | copy-start | bytes 9437188
  899.6 47.7 %collective-permute-start.4 = (bf16[512,2048]{1,0:T(8,128)(2,1)S(1)}, bf16[512,2048]{1,0:T(8,128)(2,1)S(1)}, u32[]{:S(2)}, u32[]{:S(2)}) collective-permute-start(bf16[512,2048]{1,0:T(8,128)(2,1)S(1)} %add_convert_fusion.3), channel_id=1, source_target_pairs={{0,2},{1,3},{2,0},{3,1},{4,6},{5,7},{6,4},{7,5},{8,10},{9,11},{10,... | collective-permute-start | bytes 6291464 | tf_op jit(solution)/shard_map/ppermute | solution.py:916
  948.2 81.5 %collective-permute-start.5 = (bf16[512,2048]{1,0:T(8,128)(2,1)S(1)}, bf16[512,2048]{1,0:T(8,128)(2,1)}, u32[]{:S(2)}, u32[]{:S(2)}) collective-permute-start(bf16[512,2048]{1,0:T(8,128)(2,1)S(1)} %add_convert_fusion.2), channel_id=1, source_target_pairs={{0,1},{1,0},{2,3},{3,2},{4,5},{5,4},{6,7},{7,6},{8,9},{9,8},{10,11... | collective-permute-start | bytes 6291464 | tf_op jit(solution)/shard_map/ppermute | solution.py:918
  980.7 6.1 copy-start.21
  988.7 46.3 %copy-start.20 = (f32[2048]{0:T(1024)S(1)}, f32[2048]{0:T(1024)}, u32[]{:S(2)}) copy-start(f32[2048]{0:T(1024)} %get-tuple-element.101) | copy-start | bytes 24580
  (6 other events, 20.8 us)
Sparse Core Ops, SparseCore 0:
  874.0 73.4 reduce-scatter.7
  951.1 74.0 reduce-scatter.5
  1036.5 63.3 reduce-scatter.9

commit v3 on v2

--- a/solution.py
+++ b/solution.py
@@ -344,8 +344,8 @@
         att_ref,
         sum_ref,
         b_ref,
+        gains,
         gain_in,
-        gains,
         weights,
         part,
         half_in,
@@ -535,12 +535,12 @@
             out(token_count, q_width),
             out(token_count, width),
             out(token_count, width),
+            jax.ShapeDtypeStruct((8, width), F32),
         ),
         in_specs=[VMEM_SPEC] * 6,
-        out_specs=[HBM_SPEC] + [VMEM_SPEC] * 7,
+        out_specs=[HBM_SPEC] + [VMEM_SPEC] * 8,
         scratch_shapes=[
             VMEM((count, 8, rows), F32),
-            VMEM((8, width), F32),
             VMEM((q_units + 1 + o_units, width, cols), BF16),
             VMEM((blocks, ROWS, width), BF16),
             *sum_bufs,
@@ -559,6 +559,7 @@
 
 class Scatter:
     SLOTS = 4
+    LAG = 2
 
     def __init__(self, place, rows, units, refs, first=0):
         self.place, self.rows, self.units, self.first = place, rows, units, first
@@ -679,12 +680,12 @@
                 self.keep(unit).wait()
 
     def tick(self, time):
-        self.stage(2, time - 1 - (self.SLOTS - 1))
+        self.stage(2, time - self.LAG - (self.SLOTS - 1))
         self.stage(0, time)
-        self.stage(1, time - 1)
+        self.stage(1, time - self.LAG)
 
     def latency(self):
-        return 1 + self.SLOTS
+        return self.LAG + self.SLOTS
 
     def finish(self):
         def unit_end(unit, _):
@@ -865,7 +866,7 @@
         summer.drain(blk)
 
 
-def feed(b, cotangent, gathered, depth, first_unit, chunks, pace, scatter_units):
+def feed(b, cotangent, gathered, depth, first_unit, chunks, pace, scatter_units, grad_units):
     token_count, width = b.shape
     rows = width // (depth * FOLD)
     blocks, half = token_count // ROWS, ROWS // 2
@@ -874,7 +875,7 @@
     return pl.pallas_call(
         functools.partial(feed_kernel, (depth, first_unit, chunks, pace, scatter_units)),
         out_shape=(
-            jax.ShapeDtypeStruct((3 * chunks, width, UNIT), BF16),
+            jax.ShapeDtypeStruct((grad_units, width, UNIT), BF16),
             *Scatter.outputs(scatter_units, depth, rows),
             full,
             full,
@@ -903,77 +904,378 @@
     )(b, cotangent, gathered)
 
 
-def tensor_sum(partial):
-    rows = partial.shape[0] // 2
-    core = lax.axis_index("tensor") % 2
-    count = lax.axis_size("tensor")
-    flip_core = [(i, i ^ 1) for i in range(count)]
-    flip_y = [(i, i ^ 2) for i in range(count)]
-    mine = lax.dynamic_slice_in_dim(partial, core * rows, rows, axis=0)
-    other = lax.dynamic_slice_in_dim(partial, (1 - core) * rows, rows, axis=0)
-    received = lax.ppermute(other, "tensor", flip_core)
-    chip = (mine.astype(F32) + received.astype(F32)).astype(BF16)
-    across = lax.ppermute(chip, "tensor", flip_y)
-    total = (chip.astype(F32) + across.astype(F32)).astype(BF16)
-    back = lax.ppermute(total, "tensor", flip_core)
-    return jnp.where(
-        core == 0,
-        jnp.concatenate([total, back], axis=0),
-        jnp.concatenate([back, total], axis=0),
+def back_kernel(cfg, *refs):
+    (
+        x_ref,
+        q_ref,
+        k_ref,
+        v_ref,
+        att_ref,
+        mask_ref,
+        cos_ref,
+        sin_ref,
+        gains,
+        cot_ref,
+        att_sum_ref,
+        db_ref,
+        part_out_ref,
+        a_ref,
+        g_ref,
+        _,
+        grads_ref,
+        x_in,
+        z_in,
+        kept,
+        dx_ref,
+        sum_ref,
+        gain_ref,
+        dx2,
+        low,
+        weights,
+        do,
+        dq,
+        dkv,
+        dk,
+        dv,
+        part,
+        half_in,
+        half,
+        far_in,
+        total,
+        back,
+        far_first,
+        piece,
+        grad_buf,
+        gain_acc,
+        gain_blocks,
+        gain_land,
+        sum_sends,
+        sum_recvs,
+        first_sends,
+        first_recvs,
+        gain_send,
+        gain_recv,
+        load_sem,
+        *scatter_refs,
+    ) = refs
+    depth, first_grad, scatter_units, q_units, o_units = cfg
+    place = Place(depth)
+    count = depth * FOLD
+    token_count, width = x_ref.shape
+    rows = x_in.shape[2]
+    kv_width = k_ref.shape[1]
+    blocks, short = token_count // ROWS, ROWS // 2
+    scatter = Scatter(
+        place, rows, scatter_units, (grads_ref, x_in, z_in, kept, *scatter_refs), first_grad
     )
-
-
-def norm_parts(stream):
-    inverse = lax.rsqrt(jnp.mean(stream * stream, axis=-1, keepdims=True) + EPS_NORM)
-    return (stream * inverse, inverse)
-
-
-def norm_back(grad_normed, gain, normalized_input, inverse):
-    scaled = grad_normed * gain[None, :]
-    return inverse * (
-        scaled - normalized_input * jnp.mean(scaled * normalized_input, axis=-1, keepdims=True)
+    feed_left = scatter_units - o_units - q_units - 1
+    own_grads = first_grad + feed_left
+    summer = TensorSum(place, part, (half_in, half, far_in, total, back), (sum_sends, sum_recvs))
+    stored = StoredSum(
+        place,
+        part_out_ref,
+        (half_in, half, far_first, total, back),
+        (first_sends, first_recvs),
+        piece,
+        load_sem.at[0],
     )
-
-
-def rotate_back(value_vectors, cosine, sine):
-    half = value_vectors.shape[-1] // 2
-    first = value_vectors[..., :half]
-    second = value_vectors[..., half:]
-    return jnp.concatenate(
-        [first * cosine + second * sine, second * cosine - first * sine], axis=-1
+    lane = lax.broadcasted_iota(jnp.int32, (1, LANES), 1)
+    low_half = lane < HEAD_SIZE
+
+    def fetch(pairs):
+        copies = [
+            pltpu.make_async_copy(src, dst, load_sem.at[number])
+            for number, (src, dst) in enumerate(pairs)
+        ]
+        for copy in copies:
+            copy.start()
+        for copy in copies:
+            copy.wait()
+
+    gain_acc[...] = jnp.zeros_like(gain_acc)
+    dk[...] = jnp.zeros_like(dk)
+    dv[...] = jnp.zeros_like(dv)
+    place.enter()
+
+    def middle_grad(blk):
+        at = slice(blk * ROWS, (blk + 1) * ROWS)
+        fetch(
+            (
+                (cot_ref.at[pl.ds(blk * ROWS, ROWS)], part.at[0]),
+                (att_sum_ref.at[pl.ds(blk * ROWS, ROWS)], part.at[1]),
+                (db_ref.at[pl.ds(blk * ROWS, ROWS)], part.at[2]),
+            )
+        )
+        middle = x_ref[at, :].astype(F32) + part[1].astype(F32)
+        inverse = lax.rsqrt(jnp.mean(middle * middle, axis=-1, keepdims=True) + EPS_NORM)
+        normal = middle * inverse
+        grad = part[2].astype(F32)
+        gain_acc[1:2, :] += jnp.sum(grad * normal, axis=0, keepdims=True)
+        scaled = grad * gains[1:2, :]
+        centre = jnp.mean(scaled * normal, axis=-1, keepdims=True)
+        result = part[0].astype(F32) + inverse * (scaled - normal * centre)
+        dx2[at, :] = result
+        low[at, :] = result.astype(BF16)
+
+    def attended_grad():
+        fetch([(g_ref.at[q_units + 1 + unit], weights.at[unit]) for unit in range(o_units)])
+
+        def block(blk, _):
+            at = pl.ds(pl.multiple_of(blk * ROWS, ROWS), ROWS)
+            for unit in range(o_units):
+                do[at, unit * UNIT : (unit + 1) * UNIT] = dot(low[at, :], weights[unit]).astype(
+                    BF16
+                )
+            return 0
+
+        lax.fori_loop(0, blocks, block, 0)
+
+    def save_grad(slot, number, left, right, start):
+        def block(blk, _):
+            cols = pl.ds(pl.multiple_of(blk * ROWS, ROWS), ROWS)
+            grad_buf[slot, cols, :] = dot_tn(
+                left[:, cols], right[:, start : start + UNIT]
+            ).astype(BF16)
+            return 0
+
+        lax.fori_loop(0, width // ROWS, block, 0)
+        fetch([(grad_buf.at[slot], grads_ref.at[own_grads + number])])
+
+    def second_weights():
+        fetch(
+            [(a_ref, low)]
+            + [(g_ref.at[unit], weights.at[unit]) for unit in range(q_units + 1)]
+        )
+
+    def attention_pairs(blk, first, last):
+        start, stop = blk * ROWS, (blk + 1) * ROWS
+
+        def pair(index, _):
+            lanes = pl.ds(pl.multiple_of(index * LANES, LANES), LANES)
+            query, grad = q_ref[start:stop, lanes], do[start:stop, lanes]
+            outs = []
+            for one in (True, False):
+                keep = low_half if one else jnp.logical_not(low_half)
+                query_one = jnp.where(keep, query, jnp.zeros_like(query))
+                grad_one = jnp.where(keep, grad, jnp.zeros_like(grad))
+                scores = dot_nt(k_ref[:stop, :], query_one) * HEAD_SIZE ** (-0.5)
+                allowed = mask_ref[:stop, start:stop].astype(F32) > 0
+                scores = jnp.where(allowed, scores, NEG_FILL)
+                expo = jnp.exp(scores - jnp.max(scores, axis=0, keepdims=True))
+                probs = expo * (1.0 / jnp.sum(expo, axis=0, keepdims=True))
+                grad_probs = dot_nt(v_ref[:stop, :], grad_one)
+                centre = jnp.sum(probs * grad_probs, axis=0, keepdims=True)
+                grad_scores = (probs * (grad_probs - centre)).astype(BF16)
+                dv[:stop, :] += dot(probs.astype(BF16), grad_one)
+                dk[:stop, :] += dot(grad_scores, query_one)
+                outs.append(dot_tn(grad_scores, k_ref[:stop, :]))
+            joined = jnp.where(low_half, outs[0], outs[1]) * HEAD_SIZE ** (-0.5)
+            dq[start:stop, lanes] = turn(
+                joined, cos_ref[start:stop, :], sin_ref[start:stop, :], True
+            ).astype(BF16)
+            return 0
+
+        lax.fori_loop(first, last, pair, 0)
+
+    def input_part(blk):
+        at = slice(blk * ROWS, (blk + 1) * ROWS)
+        dkv[at, :kv_width] = turn(
+            dk[at, :] * HEAD_SIZE ** (-0.5), cos_ref[at, :], sin_ref[at, :], True
+        ).astype(BF16)
+        dkv[at, kv_width:] = dv[at, :].astype(BF16)
+        out = dot_nt(dkv[at, :], weights[q_units])
+        for unit in range(q_units):
+            out = out + dot_nt(dq[at, unit * UNIT : (unit + 1) * UNIT], weights[unit])
+        part[blk] = out.astype(BF16)
+        summer.begin(blk)
+
+    def finish(blk):
+        for row, values in summer.end(blk):
+            at = pl.ds(row, short)
+            grad = values[blk].astype(F32)
+            stream = x_ref[at, :].astype(F32)
+            inverse = lax.rsqrt(jnp.mean(stream * stream, axis=-1, keepdims=True) + EPS_NORM)
+            normal = stream * inverse
+            gain_acc[0:1, :] += jnp.sum(grad * normal, axis=0, keepdims=True)
+            scaled = grad * gains[0:1, :]
+            centre = jnp.mean(scaled * normal, axis=-1, keepdims=True)
+            dx2[at, :] += inverse * (scaled - normal * centre)
+        fetch([(dx2.at[pl.ds(blk * ROWS, ROWS)], dx_ref.at[pl.ds(blk * ROWS, ROWS)])])
+
+    def stored_end(blk):
+        fetch(
+            [
+                (values.at[blk], sum_ref.at[pl.ds(row, short)])
+                for row, values in stored.end(blk)
+            ]
+        )
+        stored.drain(blk)
+
+    pairs = q_ref.shape[1] // LANES
+    schedule = []
+
+    def add(when, work, *args):
+        schedule.append((when, functools.partial(work, *args)))
+
+    for blk in range(blocks):
+        add(blk // 2, middle_grad, blk)
+        add(blk, stored.begin, blk)
+        add(blk + 1, stored.middle, blk)
+        add(blk + 3, stored.late, blk)
+        add(blk + 4, stored_end, blk)
+    now = blocks // 2
+    add(now, attended_grad)
+    for unit in range(o_units):
+        add(now + 1 + unit, save_grad, unit % 2, unit, low, att_ref, unit * UNIT)
+    now += o_units
+    add(now, second_weights)
+    now += 1
+    for blk in reversed(range(blocks)):
+        steps = max(1, (blk * 2 + 2) // 3)
+        each = -(-pairs // steps)
+        for first in range(0, pairs, each):
+            add(now, attention_pairs, blk, first, min(pairs, first + each))
+            now += 1
+        begin = max(now - 1, blk + 5)
+        add(begin, input_part, blk)
+        add(begin + 1, summer.middle, blk)
+        add(begin + 3, summer.late, blk)
+        add(begin + 4, finish, blk)
+    length = now + 5
+    for unit in range(q_units):
+        add(now, save_grad, unit % 2, o_units + unit, low, dq, unit * UNIT)
+    add(now, save_grad, q_units % 2, o_units + q_units, low, dkv, 0)
+    early = now - (feed_left + o_units)
+    schedule.sort(key=lambda item: item[0])
+    hold = max(0, early + 1)
+    length = max(length, scatter_units + hold + scatter.latency())
+
+    def body(time, _):
+        for when, work in schedule:
+            pl.when(time == when)(work)
+        scatter.tick(time - hold)
+        return 0
+
+    lax.fori_loop(0, length, body, 0)
+    for source in range(count):
+        gain_blocks[source] = gain_acc[:, source * rows : (source + 1) * rows]
+
+    def gain_copy(step):
+        dest = lax.rem(place.me + step, count)
+        return pltpu.make_async_remote_copy(
+            gain_blocks.at[dest],
+            gain_land.at[place.me],
+            gain_send.at[step],
+            gain_recv.at[place.me],
+            device_id={"dp": dest},
+            device_id_type=MESH,
+        )
+
+    def gain_arrival(source):
+        return pltpu.make_async_remote_copy(
+            gain_blocks.at[0],
+            gain_land.at[source],
+            gain_send.at[0],
+            gain_recv.at[source],
+            device_id={"dp": place.partner},
+            device_id_type=MESH,
+        )
+
+    for step in range(1, count):
+        gain_copy(step).start()
+    summed = gain_blocks[place.me]
+    for step in range(1, count):
+        source = lax.rem(place.me + step, count)
+        gain_arrival(source).wait_recv()
+        summed = summed + gain_land[source]
+    gain_ref[...] = summed
+    for step in range(1, count):
+        gain_copy(step).wait_send()
+    scatter.finish()
+    for blk in range(blocks):
+        summer.drain(blk)
+
+
+class StoredSum(TensorSum):
+    def __init__(self, place, part, bufs, sems, piece, sem):
+        super().__init__(place, part, bufs, sems)
+        self.piece, self.sem = piece, sem
+
+    def rows_of(self, blk, core):
+        short = self.half.shape[1]
+        return pl.ds(pl.multiple_of(blk * 2 * short + core * short, short), short)
+
+    def first(self, blk):
+        src = self.part.at[self.rows_of(blk, 1 - self.place.core)]
+        return self.copy(0, src, self.half_in, blk)
+
+    def middle(self, blk):
+        copy = pltpu.make_async_copy(
+            self.part.at[self.rows_of(blk, self.place.core)], self.piece, self.sem
+        )
+        copy.start()
+        self.first(blk).wait_recv()
+        copy.wait()
+        self.half[blk] = (self.piece[...].astype(F32) + self.half_in[blk].astype(F32)).astype(BF16)
+        self.second(blk).start()
+
+
+def attend_back(
+    tokens, q, k, v, att, mask, cosine, sine, gains, cotangent, att_sum, db, out_part, a,
+    gathered, grads, depth, first_grad, q_units, o_units,
+):
+    token_count, width = tokens.shape
+    rows = width // (depth * FOLD)
+    blocks, half = token_count // ROWS, ROWS // 2
+    q_width, kv_width = q.shape[1], k.shape[1]
+    scatter_units = grads.shape[0] - first_grad
+    sum_bufs, sum_sems = TensorSum.scratch(blocks, half, width)
+    count = depth * FOLD
+    wide = max(q_units + 1, o_units)
+    return pl.pallas_call(
+        functools.partial(back_kernel, (depth, first_grad, scatter_units, q_units, o_units)),
+        out_shape=(
+            jax.ShapeDtypeStruct(grads.shape, BF16),
+            *Scatter.outputs(scatter_units, depth, rows),
+            jax.ShapeDtypeStruct((token_count, width), F32),
+            jax.ShapeDtypeStruct((token_count, width), BF16),
+            jax.ShapeDtypeStruct((8, rows), F32),
+        ),
+        in_specs=[VMEM_SPEC] * 9 + [HBM_SPEC] * 7,
+        out_specs=[HBM_SPEC] * 6 + [VMEM_SPEC],
+        scratch_shapes=[
+            VMEM((token_count, width), F32),
+            VMEM((token_count, width), BF16),
+            VMEM((wide, width, UNIT), BF16),
+            VMEM((token_count, q_width), BF16),
+            VMEM((token_count, q_width), BF16),
+            VMEM((token_count, 2 * kv_width), BF16),
+            VMEM((token_count, kv_width), F32),
+            VMEM((token_count, kv_width), F32),
+            VMEM((blocks, ROWS, width), BF16),
+            *sum_bufs,
+            VMEM((blocks, half, width), BF16),
+            VMEM((half, width), BF16),
+            VMEM((2, width, UNIT), BF16),
+            VMEM((8, width), F32),
+            VMEM((count, 8, rows), F32),
+            VMEM((count, 8, rows), F32),
+            *sum_sems,
+            *sum_sems,
+            DMA((count,)),
+            DMA((count,)),
+            DMA((8,)),
+            *Scatter.scratch(scatter_units, depth, rows),
+        ],
+        input_output_aliases={15: 0},
+        compiler_params=pltpu.CompilerParams(
+            collective_id=2, has_side_effects=True, vmem_limit_bytes=63 << 20
+        ),
+        name="attend_back",
+    )(
+        tokens, q, k, v, att, mask, cosine, sine, gains, cotangent, att_sum, db, out_part, a,
+        gathered, grads,
     )
-
-
-def attention_backward(query_vectors, key_vectors, value_vectors, grad_out, allowed):
-    token_positions = query_vectors.shape[0]
-    rows = 512
-    grad_queries = []
-    grad_keys = jnp.zeros(key_vectors.shape, F32)
-    grad_values = jnp.zeros(value_vectors.shape, F32)
-    for begin_row in range(0, token_positions, rows):
-        query_block = query_vectors[begin_row : begin_row + rows]
-        grad_block = grad_out[begin_row : begin_row + rows]
-        scores = jnp.einsum(
-            "qkgd,skd->kgqs", query_block, key_vectors, preferred_element_type=F32
-        ) * HEAD_SIZE ** (-0.5)
-        scores = jnp.where(allowed[begin_row : begin_row + rows][None, None], scores, NEG_FILL)
-        probs = jax.nn.softmax(scores, axis=-1)
-        grad_probs = jnp.einsum(
-            "qkgd,skd->kgqs", grad_block, value_vectors, preferred_element_type=F32
-        )
-        centre = jnp.sum(probs * grad_probs, axis=-1, keepdims=True)
-        grad_scores = (probs * (grad_probs - centre)).astype(BF16)
-        grad_queries.append(
-            jnp.einsum("kgqs,skd->qkgd", grad_scores, key_vectors, preferred_element_type=F32)
-            * HEAD_SIZE ** (-0.5)
-        )
-        grad_keys = grad_keys + jnp.einsum(
-            "kgqs,qkgd->skd", grad_scores, query_block, preferred_element_type=F32
-        ) * HEAD_SIZE ** (-0.5)
-        grad_values = grad_values + jnp.einsum(
-            "kgqs,qkgd->skd", probs.astype(BF16), grad_block, preferred_element_type=F32
-        )
-    return (jnp.concatenate(grad_queries, axis=0), grad_keys, grad_values)
 
 
 def gathered_units(mine, arrived):
@@ -1043,83 +1345,43 @@
         axis=0,
     )
     first_unit = 2 * q_units + 1
-    gathered, a, q, k, v, att, att_sum, b = attend(
+    gathered, a, q, k, v, att, att_sum, b, gains = attend(
         tokens, own, gain_rows, allowed.astype(F32), wide_cos, wide_sin, depth, q_units, q_units
     )
     grads, _, z_in, kept, out_part, db = feed(
-        b, cotangent, gathered, depth, first_unit, chunks, PACE, 3 * chunks
+        b, cotangent, gathered, depth, first_unit, chunks, PACE, EARLY, own.shape[0]
     )
-    stream = tokens.astype(F32)
-    middle = stream + att_sum.astype(F32)
-    block_output = (middle + tensor_sum(out_part).astype(F32)).astype(BF16)
-    gain_one = lax.all_gather(attention_gain, "dp", axis=0, tiled=True).astype(F32)
-    gain_two = lax.all_gather(feed_gain, "dp", axis=0, tiled=True).astype(F32)
-    normed_two, inverse_two = norm_parts(middle)
-    grad_normed_two = db.astype(F32)
-    feed_gain_full = jnp.sum(grad_normed_two * normed_two, axis=0)
-    grad_middle = cotangent.astype(F32) + norm_back(
-        grad_normed_two, gain_two, normed_two, inverse_two
+    _, _, z_in_late, kept_late, input_grad, out_sum, gain_grads = attend_back(
+        tokens, q, k, v, att, allowed.T.astype(BF16), wide_cos, wide_sin, gains, cotangent,
+        att_sum, db, out_part, a, gathered, grads, depth, EARLY, q_units, q_units,
     )
-    grad_middle_low = grad_middle.astype(BF16)
-    out_t = jnp.concatenate([gathered[q_units + 1 + i] for i in range(q_units)], axis=1)
-    query_full = jnp.concatenate([gathered[i] for i in range(q_units)], axis=1)
-    kv_full = gathered[q_units]
-    output_grad = dot_tn(att, grad_middle_low)
-    grad_attended = dot(grad_middle_low, out_t).astype(BF16)
-
-    def heads(cols):
-        return unpair(cols).reshape(token_count, heads_kv, groups, HEAD_SIZE)
-
-    grad_q, grad_k, grad_v = attention_backward(
-        heads(q),
-        k.reshape(token_count, heads_kv, HEAD_SIZE),
-        v.reshape(token_count, heads_kv, HEAD_SIZE),
-        heads(grad_attended),
-        allowed,
-    )
-    grad_q = pair(
-        rotate_back(grad_q, cosine[:, None, None, :], sine[:, None, None, :])
-        .astype(BF16)
-        .reshape(token_count, q_width)
-    )
-    grad_k = (
-        rotate_back(grad_k, cosine[:, None, :], sine[:, None, :])
-        .astype(BF16)
-        .reshape(token_count, kv_width)
-    )
-    grad_v = grad_v.astype(BF16).reshape(token_count, kv_width)
-    grad_kv = jnp.concatenate([grad_k, grad_v], axis=1)
-    query_grad = dot_tn(a, grad_q)
-    kv_grad = dot_tn(a, grad_kv)
-    da = dot_nt(grad_q, query_full) + dot_nt(grad_kv, kv_full)
-    da = tensor_sum(da.astype(BF16)).astype(F32)
-    normed_one, inverse_one = norm_parts(stream)
-    attention_gain_full = jnp.sum(da * normed_one, axis=0)
-    input_grad = grad_middle + norm_back(da, gain_one, normed_one, inverse_one)
-    packed = jnp.concatenate([query_grad, kv_grad], axis=1).astype(BF16)
-    packed = lax.psum_scatter(packed, "dp", scatter_dimension=0, tiled=True).astype(F32)
-    out_grad = lax.psum_scatter(
-        output_grad.astype(BF16), "dp", scatter_dimension=1, tiled=True
-    ).astype(F32)
-    gain_grads = lax.psum_scatter(
-        jnp.stack([attention_gain_full, feed_gain_full]).astype(F32),
-        "dp",
-        scatter_dimension=1,
-        tiled=True,
-    )
-    feed_grads = gathered_units(kept, z_in).reshape(chunks, 3, rows, UNIT)
+    block_output = (
+        tokens.astype(F32) + att_sum.astype(F32) + out_sum.astype(F32)
+    ).astype(BF16)
+    late = gathered_units(kept_late, z_in_late)
+    feed_late = 3 * chunks - EARLY
+    feed_grads = jnp.concatenate(
+        [gathered_units(kept, z_in), late[:feed_late]], axis=0
+    ).reshape(chunks, 3, rows, UNIT)
+
+    def row_of(units):
+        return units.swapaxes(0, 1).reshape(rows, -1)
+
+    out_grad = row_of(late[feed_late : feed_late + q_units]).T
+    query_grad = row_of(late[feed_late + q_units : feed_late + 2 * q_units])
+    kv_grad = late[feed_late + 2 * q_units]
 
     def join(which):
-        return feed_grads[:, which].swapaxes(0, 1).reshape(rows, feed_width)
+        return row_of(feed_grads[:, which])
 
     out_grad = out_grad.reshape(groups, heads_kv, HEAD_SIZE, rows).swapaxes(0, 1)
     return (
         block_output,
         input_grad,
         gain_grads[0],
-        unpair(packed[:, :q_width]),
-        packed[:, q_width : q_width + kv_width],
-        packed[:, q_width + kv_width :],
+        unpair(query_grad),
+        kv_grad[:, :kv_width],
+        kv_grad[:, kv_width:],
         out_grad.reshape(q_width, rows),
         gain_grads[1],
         join(0),
@@ -1128,7 +1390,8 @@
     )
 
 
-PACE = 3
+PACE = 1
+EARLY = 13
 
 
 def solution(mesh):

time: 1120 us -> 877 us (0.78)
  waiting for transfers between devices: 151 us -> 0 us
  Pallas kernels: 665 us -> 794 us
  matrix products: 87.5 us -> 0 us
  other arithmetic: 88.8 us -> 38.1 us
  blocking collectives: 50.6 us -> 0 us
  between operations: 14.7 us -> 1.05 us
    pallas_call x0 -> x1, Pallas kernels: none -> 247 us  [attend_back(): pl.pallas_call(functools.partial(back_kernel, (depth, first_grad, scatter...]
    pallas_call x1, Pallas kernels: 348 us -> 231 us  [feed(): pl.pallas_call(functools.partial(feed_kernel, (depth, first_unit, chunks,...]
    dot_general x14 -> x0, matrix products: 66.4 us -> none  [the longest x2 21.4 us: attention_backward(): jnp.einsum('qkgd,skd->kgqs', grad_block, value_vectors, preferred_element...]
    ppermute x6 -> x0, waiting for transfers between devices: 60.5 us -> none  [the longest x2 56.5 us: tensor_sum(): across = lax.ppermute(chip, 'tensor', flip_y)]
    unnamed x4 -> x0, waiting for transfers between devices: 54.2 us -> none
    all_gather x2 -> x0, blocking collectives: 50.6 us -> none  [the longest x1 25.8 us: shards(): lax.all_gather(attention_gain, 'dp', axis=0, tiled=True).astype(F32)]
    reduce_scatter x2 -> x0, waiting for transfers between devices: 36.6 us -> none  [the longest x1 36.5 us: shards(): lax.psum_scatter(packed, 'dp', scatter_dimension=0, tiled=True).astype(F32)]
    sub x2 -> x0, matrix products: 21.1 us -> none  [attention_backward(): probs = jax.nn.softmax(scores, axis=-1)]
  transfers between devices with their start and end apart: 9 -> 0, of which waited for: 5 -> 0; matrix products, arithmetic and copies ran while one was open for 9% -> 0% of each run, Pallas kernels for 0% -> 0%
where the time goes in v3:
time: 877 us; the launch traced here: 870 us
  Pallas kernels  794 us (91%)
  other arithmetic  38.1 us (4%)
  local copies, waits for them, and re-layouts  37.3 us (4%)
    pallas_call x1, Pallas kernels, attend(): pl.pallas_call(functools.partial(attend_kernel, (depth, units, q_units, o...  317 us
    pallas_call x1, Pallas kernels, attend_back(): pl.pallas_call(functools.partial(back_kernel, (depth, first_grad, scatter...  247 us
    pallas_call x1, Pallas kernels, feed(): pl.pallas_call(functools.partial(feed_kernel, (depth, first_unit, chunks,...  231 us

profile of v3, /device:TPU:0, one launch (start us, length us, event | category | flops | bytes accessed | tf_op | source)
XLA Modules:
  0.0 870.3 jit_solution(5788569577788595517)
XLA Ops:
  2.4 1.9 fusion.3
  4.3 1.8 pad_maximum_fusion.3
  6.6 3.6 convert_bitcast_fusion
  10.2 2.6 convert_element_type.76
  12.8 5.5 copy.119.refs_3_
  18.3 1.5 bitcast_bitcast_fusion
  19.8 1.3 copy.116
  21.1 2.2 pad_maximum_fusion.2
  23.3 0.8 copy.109
  24.2 1.0 copy.110
  25.2 0.8 copy.111
  26.0 1.0 copy.112
  27.0 0.8 copy.113
  27.9 3.0 pad_maximum_fusion.1.refs_1_
  31.6 316.6 %attend.1 = (bf16[29,2048,256]{2,1,0:T(8,128)(2,1)}, bf16[1024,2048]{1,0:T(8,128)(2,1)}, bf16[1024,512]{1,0:T(8,128)(2,1)}, bf16[1024,128]{1,0:T(8,128)(2,1)}, b...) custom-call(bf16[1024,2048]{1,0:T(8,128)(2,1)} %refs_0_.3, ...), custom_call_target="tpu_custom_call" | custom-call | tf_op jit(solution)/shard_map/attend/pallas_call | solution.py:527
  348.3 230.6 %feed.1 = (bf16[29,2048,256]{2,1,0:T(8,128)(2,1)}, bf16[13,4,256,256]{3,2,1,0:T(8,128)(2,1)}, bf16[13,4,256,256]{3,2,1,0:T(8,128)(2,1)}, bf16[13,256,256]{2,1,0:...) custom-call(bf16[1024,2048]{1,0:T(8,128)(2,1)} %get-tuple-element.36.refs_0_, ...), custom_call_target="tpu_custom_call" | custom-call | tf_op jit(solution)/shard_map/feed/pallas_call | solution.py:875
  578.9 5.7 convert_add_fusion.3
  584.7 246.5 %attend_back.1 = (bf16[29,2048,256]{2,1,0:T(8,128)(2,1)}, bf16[16,4,256,256]{3,2,1,0:T(8,128)(2,1)}, bf16[16,4,256,256]{3,2,1,0:T(8,128)(2,1)}, bf16[16,256,256]...) custom-call(bf16[1024,2048]{1,0:T(8,128)(2,1)} %refs_0_.3, ...), custom_call_target="tpu_custom_call", output_to_operand_aliasing={{0}: (15, {})} | custom-call | tf_op jit(solution)/shard_map/attend_back/pallas_call | solution.py:1235
  831.2 4.0 convert_add_fusion
  835.2 2.0 copy-done
  837.4 1.8 copy-done.1
  839.8 2.4 slice_bitcast_fusion
  842.2 2.9 copy.132
  845.1 3.2 copy.136
  848.3 1.6 copy.137
  849.9 1.3 slice_bitcast_fusion.9
  851.4 1.0 copy.133
  852.6 0.8 copy.126
  853.5 1.0 slice_bitcast_fusion.11
  855.2 10.2 %add_convert_fusion = bf16[1024,2048]{1,0:T(8,128)(2,1)} fusion(bf16[1024,2048]{1,0:T(8,128)(2,1)} %get-tuple-element.42, bf16[1024,2048]{1,0:T(8,128)(2,1)} %get-tuple-element.30.refs_10_, bf16[1024,2048]{1,0:T(8,128)(2,1)} %refs_0_.3), kind=kLoop, calls=%fused_computation | loop fusion | flops 12582912 | bytes 16777216 | tf_op jit(solution)/shard_map/convert_element_type | solution.py:1360
  865.4 1.3 fusion.9
  866.7 3.4 copy.149
  (49 shorter events, 4.9 us)
Async XLA Ops:
  0.6 5.5 copy-start.8
  12.8 5.5 copy-start.3
  12.8 5.5 copy-start.4
  18.3 1.5 copy-start.2
  19.8 3.5 copy-start.5
  21.1 6.7 copy-start.6
  21.1 6.7 copy-start.7
  27.0 3.9 copy-start.9
  27.0 3.9 copy-start.10
  835.2 2.0 copy-start
  837.2 2.0 copy-start.1
  855.2 11.6 %slice-start = ((s8[8388608]{0:T(1024)(128)(4,1)}), s8[4194304]{0:T(1024)(128)(4,1)S(1)}, s32[]{:S(2)}) async-start(s8[8388608]{0:T(1024)(128)(4,1)} %bitcast.129), calls=%async_computation | async-start | bytes 8388608
  855.2 11.6 %slice-start.1 = ((s8[8388608]{0:T(1024)(128)(4,1)}), s8[4194304]{0:T(1024)(128)(4,1)S(1)}, s32[]{:S(2)}) async-start(s8[8388608]{0:T(1024)(128)(4,1)} %bitcast.129), calls=%async_computation.1 | async-start | bytes 8388608

commit v4 on v3

v4 whole, which is shorter than its diff:
```python
import functools

import jax
import jax.numpy as jnp
from jax import lax
from jax.experimental import pallas as pl
from jax.experimental.pallas import tpu as pltpu
from jax.sharding import PartitionSpec as P

HEAD_SIZE = 64
BLOCK = 128
LANES = 128
EPS_NORM = 1e-05
THETA_BASE = 500000.0
NEG_FILL = -1e30
UNIT = 256
ROWS = 256
FOLD = 2
XFIRST = 6
MESH = pl.DeviceIdType.MESH
VMEM = pltpu.VMEM
DMA = pltpu.SemaphoreType.DMA
HBM_SPEC = pl.BlockSpec(memory_space=pl.ANY)
VMEM_SPEC = pl.BlockSpec(memory_space=pltpu.VMEM)
F32 = jnp.float32
BF16 = jnp.bfloat16


EARLY_CHUNKS = 6
EARLY_UNITS = 10
SCATTER_EVERY = 2


def split(depth):
    return 2 if depth <= 8 else 1


def token_layout(lengths_row, total, block):
    blocks_per = (lengths_row + block - 1) // block
    offsets = jnp.cumsum(blocks_per) - blocks_per
    first_token = offsets * block
    indices = jnp.arange(total, dtype=jnp.int32)
    member = (indices[:, None] >= first_token[None, :]) & (blocks_per[None, :] > 0)
    sequence = jnp.sum(member.astype(jnp.int32), axis=1) - 1
    select = sequence[:, None] == jnp.arange(lengths_row.shape[0], dtype=jnp.int32)[None, :]
    begins = jnp.sum(jnp.where(select, first_token[None, :], 0), axis=1)
    limits = jnp.sum(jnp.where(select, lengths_row[None, :], 0), axis=1)
    position = indices - begins
    return (sequence, position, position < limits)


def slot_codes(sequence, valid, mask_blocks, block):
    blocks = mask_blocks.shape[0]
    index = jnp.arange(blocks, dtype=jnp.int32)
    own = jnp.max(jnp.where(index[:, None] == index[None, :], mask_blocks, 0), axis=1)
    live = jnp.broadcast_to(own[:, None] > 0, (blocks, block)).reshape(blocks * block)
    query_code = jnp.where(live, sequence, -1)
    key_code = jnp.where(valid, sequence, -2)
    return query_code, key_code


def rope_tables(position, head_dim):
    freqs = THETA_BASE ** (-jnp.arange(head_dim // 2, dtype=F32) * 2.0 / head_dim)
    angles = position.astype(F32)[:, None] * freqs[None, :]
    return (jnp.cos(angles), jnp.sin(angles))


def dot(left, right):
    return jnp.dot(left, right, preferred_element_type=F32)


def dot_nt(left, right):
    return lax.dot_general(left, right, (((1,), (1,)), ((), ())), preferred_element_type=F32)


def dot_tn(left, right):
    return lax.dot_general(left, right, (((0,), (0,)), ((), ())), preferred_element_type=F32)


class Place:
    def __init__(self, depth):
        self.depth = depth
        self.me = lax.axis_index("dp")
        self.z = self.me // FOLD
        self.x = self.me % FOLD
        self.right = self.me + FOLD
        self.left = self.me - FOLD
        self.partner = self.z * FOLD + (1 - self.x)
        member = lax.axis_index("tensor")
        self.core = member % 2
        row = member // 2
        self.other = row * 2 + (1 - self.core)
        self.across = (1 - row) * 2 + self.core

    def enter(self):
        count = self.depth * FOLD
        barrier = pltpu.get_barrier_semaphore()
        for step in range(1, count):
            pl.semaphore_signal(
                barrier,
                1,
                device_id={"dp": lax.rem(self.me + step, count)},
                device_id_type=MESH,
            )
        for peer in (self.other, self.across):
            pl.semaphore_signal(barrier, 1, device_id={"tensor": peer}, device_id_type=MESH)
        pl.semaphore_wait(barrier, count + 1)


class Gather:
    def __init__(self, place, g_ref, rows, pieces, sems, base=0):
        self.place, self.g, self.rows, self.pieces, self.base = place, g_ref, rows, pieces, base
        self.z_send, self.z_recv, self.x_send, self.x_recv = sems

    @staticmethod
    def scratch(pieces, depth):
        return [
            DMA((pieces, 2, depth, FOLD)),
            DMA((pieces, depth, FOLD)),
            DMA((pieces, depth)),
            DMA((pieces, depth)),
        ]

    def block(self, piece, index):
        whole, parts = piece + self.base, split(self.place.depth)
        size = self.rows // parts
        start = pl.multiple_of(index * self.rows + lax.rem(whole, parts) * size, size)
        return self.g.at[whole // parts, pl.ds(start, size)]

    def along(self, piece, zz, xx, way):
        p = self.place
        ref = self.block(piece, zz * FOLD + xx)
        return pltpu.make_async_remote_copy(
            ref,
            ref,
            self.z_send.at[piece, way, zz, xx],
            self.z_recv.at[piece, zz, xx],
            device_id={"dp": p.left if way else p.right},
            device_id_type=MESH,
        )

    def over(self, piece, zz, incoming=False):
        p = self.place
        ref = self.block(piece, zz * FOLD + (1 - p.x if incoming else p.x))
        return pltpu.make_async_remote_copy(
            ref,
            ref,
            self.x_send.at[piece, zz],
            self.x_recv.at[piece, zz],
            device_id={"dp": p.partner},
            device_id_type=MESH,
        )

    def lanes(self, wide):
        return range(FOLD) if wide else (self.place.x,)

    def send_both(self, piece, zz, wide):
        p, last = self.place, self.place.depth - 1

        @pl.when(p.z < last)
        def _():
            for xx in self.lanes(wide):
                self.along(piece, zz, xx, 0).start()

        @pl.when(p.z > 0)
        def _():
            for xx in self.lanes(wide):
                self.along(piece, zz, xx, 1).start()

    def forward(self, piece, step, wide):
        p, last = self.place, self.place.depth - 1

        @pl.when(p.z >= step)
        def _():
            zz = p.z - step
            for xx in self.lanes(wide):
                self.along(piece, zz, xx, 0).wait_recv()

            @pl.when(p.z < last)
            def _():
                for xx in self.lanes(wide):
                    self.along(piece, zz, xx, 0).start()

            if not wide:
                self.over(piece, zz).start()

        @pl.when(p.z + step <= last)
        def _():
            zz = p.z + step
            for xx in self.lanes(wide):
                self.along(piece, zz, xx, 1).wait_recv()

            @pl.when(p.z > 0)
            def _():
                for xx in self.lanes(wide):
                    self.along(piece, zz, xx, 1).start()

            if not wide:
                self.over(piece, zz).start()

    def drain(self, piece, wide):
        p, last = self.place, self.place.depth - 1
        for zz in range(p.depth):

            @pl.when((p.z >= zz) & (p.z < last))
            def _():
                for xx in self.lanes(wide):
                    self.along(piece, zz, xx, 0).wait_send()

            @pl.when((p.z <= zz) & (p.z > 0))
            def _():
                for xx in self.lanes(wide):
                    self.along(piece, zz, xx, 1).wait_send()

    def stage(self, step, piece):
        p, depth = self.place, self.place.depth

        def slow_first():
            if step == 0:
                self.send_both(piece, p.z, False)
                self.over(piece, p.z).start()
            elif step < depth:
                self.forward(piece, step, False)
            else:
                for zz in range(depth):
                    self.over(piece, zz, True).wait_recv()
                for zz in range(depth):
                    self.over(piece, zz).wait_send()
                self.drain(piece, False)

        def fast_first():
            if step == 0:
                self.over(piece, p.z).start()
            elif step == 1:
                self.over(piece, p.z, True).wait_recv()
                self.send_both(piece, p.z, True)
            else:
                self.forward(piece, step - 1, True)
                if step == depth:
                    self.over(piece, p.z).wait_send()
                    self.drain(piece, True)

        inside = (piece >= 0) & (piece < self.pieces)
        fast = lax.rem(piece + self.base, XFIRST) == XFIRST - 1
        pl.when(inside & jnp.logical_not(fast))(slow_first)
        pl.when(inside & fast)(fast_first)

    def latency(self):
        return self.place.depth + 1

    def tick(self, time):
        depth = self.place.depth
        for step in range(depth):
            self.stage(step, time - step)
        self.stage(depth, time - depth - 1)


class TensorSum:
    def __init__(self, place, part, bufs, sems):
        self.place, self.part = place, part
        self.half_in, self.half, self.far_in, self.total, self.back = bufs
        self.sends, self.recvs = sems

    @staticmethod
    def scratch(blocks, half, width):
        return [VMEM((blocks, half, width), BF16)] * 5, [DMA((3, blocks)), DMA((3, blocks))]

    def copy(self, step, src, dst, blk):
        p = self.place
        return pltpu.make_async_remote_copy(
            src,
            dst.at[blk],
            self.sends.at[step, blk],
            self.recvs.at[step, blk],
            device_id={"tensor": p.across if step == 1 else p.other},
            device_id_type=MESH,
        )

    def first(self, blk):
        half = self.half.shape[1]
        start = pl.multiple_of((1 - self.place.core) * half, half)
        return self.copy(0, self.part.at[blk, pl.ds(start, half)], self.half_in, blk)

    def second(self, blk):
        return self.copy(1, self.half.at[blk], self.far_in, blk)

    def third(self, blk):
        return self.copy(2, self.total.at[blk], self.back, blk)

    def begin(self, blk):
        self.first(blk).start()

    def middle(self, blk):
        half = self.half.shape[1]
        self.first(blk).wait_recv()
        start = pl.multiple_of(self.place.core * half, half)
        mine = self.part[blk, pl.ds(start, half), :].astype(F32)
        self.half[blk] = (mine + self.half_in[blk].astype(F32)).astype(BF16)
        self.second(blk).start()

    def late(self, blk):
        self.second(blk).wait_recv()
        self.total[blk] = (self.half[blk].astype(F32) + self.far_in[blk].astype(F32)).astype(BF16)
        self.third(blk).start()

    def end(self, blk):
        half = self.half.shape[1]
        self.third(blk).wait_recv()
        core = self.place.core
        return (
            (pl.multiple_of(blk * 2 * half + core * half, half), self.total),
            (pl.multiple_of(blk * 2 * half + (1 - core) * half, half), self.back),
        )

    def drain(self, blk):
        self.first(blk).wait_send()
        self.second(blk).wait_send()
        self.third(blk).wait_send()


class StoredSum(TensorSum):
    def __init__(self, place, part, bufs, sems, piece, sem):
        super().__init__(place, part, bufs, sems)
        self.piece, self.sem = piece, sem

    def rows_of(self, blk, core):
        short = self.half.shape[1]
        return pl.ds(pl.multiple_of(blk * 2 * short + core * short, short), short)

    def first(self, blk):
        src = self.part.at[self.rows_of(blk, 1 - self.place.core)]
        return self.copy(0, src, self.half_in, blk)

    def middle(self, blk):
        copy = pltpu.make_async_copy(
            self.part.at[self.rows_of(blk, self.place.core)], self.piece, self.sem
        )
        copy.start()
        self.first(blk).wait_recv()
        copy.wait()
        self.half[blk] = (self.piece[...].astype(F32) + self.half_in[blk].astype(F32)).astype(BF16)
        self.second(blk).start()


def turn(values, cosine, sine, back=False):
    half = HEAD_SIZE // 2
    lane = lax.broadcasted_iota(jnp.int32, (1, LANES), 1)
    low = lax.rem(lane, HEAD_SIZE) < half
    tiles = []
    for start in range(0, values.shape[1], LANES):
        tile = values[:, start : start + LANES]
        swapped = jnp.where(low, pltpu.roll(tile, LANES - half, 1), pltpu.roll(tile, half, 1))
        if back:
            tiles.append(tile * cosine - swapped * sine)
        else:
            tiles.append(tile * cosine + swapped * sine)
    return tiles[0] if len(tiles) == 1 else jnp.concatenate(tiles, axis=1)


def normed(stream):
    return stream * lax.rsqrt(jnp.mean(stream * stream, axis=-1, keepdims=True) + EPS_NORM)


def attend_kernel(cfg, *refs):
    (
        x_ref,
        w_ref,
        gain_ref,
        cols_ref,
        rows_ref,
        cos_ref,
        sin_ref,
        g_ref,
        a_ref,
        q_ref,
        k_ref,
        v_ref,
        att_ref,
        sum_ref,
        b_ref,
        gains,
        gain_in,
        weights,
        mask,
        part,
        half_in,
        half,
        far_in,
        total,
        back,
        sum_sends,
        sum_recvs,
        z_send,
        z_recv,
        x_send,
        x_recv,
        gain_send,
        gain_recv,
        local_sem,
    ) = refs
    depth, pieces, q_units, o_units = cfg
    place = Place(depth)
    count = depth * FOLD
    token_count, width = x_ref.shape
    rows = w_ref.shape[1]
    blocks = token_count // ROWS
    fill = pltpu.make_async_copy(
        w_ref, g_ref.at[:, pl.ds(pl.multiple_of(place.me * rows, rows), rows)], local_sem
    )
    fill.start()
    place.enter()
    fill.wait()
    gather = Gather(place, g_ref, rows, pieces, (z_send, z_recv, x_send, x_recv))
    summer = TensorSum(place, part, (half_in, half, far_in, total, back), (sum_sends, sum_recvs))

    def gain_copy(step):
        return pltpu.make_async_remote_copy(
            gain_ref,
            gain_in.at[place.me],
            gain_send.at[step],
            gain_recv.at[place.me],
            device_id={"dp": lax.rem(place.me + step, count)},
            device_id_type=MESH,
        )

    def gain_arrival(source):
        return pltpu.make_async_remote_copy(
            gain_ref,
            gain_in.at[source],
            gain_send.at[0],
            gain_recv.at[source],
            device_id={"dp": place.partner},
            device_id_type=MESH,
        )

    lane = lax.broadcasted_iota(jnp.int32, (1, LANES), 1)
    low_half = lane < HEAD_SIZE

    def spread_gains():
        gain_in[place.me] = gain_ref[...]
        for step in range(1, count):
            gain_arrival(lax.rem(place.me + step, count)).wait_recv()
        for source in range(count):
            gains[:, source * rows : (source + 1) * rows] = gain_in[source]

    def norm_block(blk):
        rows_at = pl.ds(pl.multiple_of(blk * ROWS, ROWS), ROWS)
        stream = x_ref[rows_at, :].astype(F32)
        a_ref[rows_at, :] = (normed(stream) * gains[0:1, :]).astype(BF16)

    def load(unit):
        copy = pltpu.make_async_copy(g_ref.at[unit], weights.at[unit], local_sem)
        copy.start()
        copy.wait()

    def project(unit):
        load(unit)

        def block(blk, _):
            rows_at = pl.ds(pl.multiple_of(blk * ROWS, ROWS), ROWS)
            cosine, sine = cos_ref[rows_at, :], sin_ref[rows_at, :]
            out = dot(a_ref[rows_at, :], weights[unit])
            if unit < q_units:
                q_ref[rows_at, unit * UNIT : (unit + 1) * UNIT] = turn(out, cosine, sine).astype(
                    BF16
                )
            else:
                kv = k_ref.shape[1]
                k_ref[rows_at, :] = turn(out[:, :kv], cosine, sine).astype(BF16)
                v_ref[rows_at, :] = out[:, kv:].astype(BF16)
            return 0

        lax.fori_loop(0, blocks, block, 0)

    def attend(blk, first, last):
        start, stop = blk * ROWS, (blk + 1) * ROWS
        if first == 0:
            key = lax.broadcasted_iota(jnp.int32, (ROWS, stop), 1)
            query_at = lax.broadcasted_iota(jnp.int32, (ROWS, stop), 0) + start
            same = cols_ref[start:stop, 0:1] == rows_ref[1:2, :stop]
            allowed = (same & (key <= query_at)) | (key == query_at)
            mask[:, :stop] = jnp.where(allowed, 0.0, NEG_FILL)

        def pair(index, _):
            lanes = pl.ds(pl.multiple_of(index * LANES, LANES), LANES)
            query = q_ref[start:stop, lanes]
            outs = []
            for one in (True, False):
                keep = low_half if one else jnp.logical_not(low_half)
                masked = jnp.where(keep, query, jnp.zeros_like(query))
                scores = dot_nt(masked, k_ref[:stop, :]) * HEAD_SIZE ** (-0.5)
                scores = jnp.where(mask[:, :stop] < 0, NEG_FILL, scores)
                expo = jnp.exp(scores - jnp.max(scores, axis=-1, keepdims=True))
                probs = expo * (1.0 / jnp.sum(expo, axis=-1, keepdims=True))
                outs.append(dot(probs.astype(BF16), v_ref[:stop, :]))
            att_ref[start:stop, lanes] = jnp.where(low_half, outs[0], outs[1]).astype(BF16)
            return 0

        lax.fori_loop(first, last, pair, 0)

    def emit(blk):
        first = q_units + 1
        out = None
        for number in range(o_units):
            cols = slice(number * UNIT, (number + 1) * UNIT)
            piece = dot_nt(att_ref[blk * ROWS : (blk + 1) * ROWS, cols], weights[first + number])
            out = piece if out is None else out + piece
        part[blk] = out.astype(BF16)
        summer.begin(blk)

    def finish(blk):
        for row, values in summer.end(blk):
            rows_at = pl.ds(row, ROWS // 2)
            added = values[blk]
            sum_ref[rows_at, :] = added
            stream = x_ref[rows_at, :].astype(F32) + added.astype(F32)
            b_ref[rows_at, :] = (normed(stream) * gains[1:2, :]).astype(BF16)

    def ready(unit):
        return split(depth) * (unit + 1) - 1 + gather.latency()

    pairs = q_ref.shape[1] // LANES
    schedule = []
    for unit in range(q_units + 1):
        schedule.append((ready(unit), functools.partial(project, unit)))
    for unit in range(q_units + 1, q_units + 1 + o_units):
        schedule.append((ready(unit), functools.partial(load, unit)))
    now = ready(q_units) + 1
    sent = ready(q_units + o_units)
    for blk in range(blocks):
        steps = 1 + blk // 2
        each = -(-pairs // steps)
        for first in range(0, pairs, each):
            schedule.append(
                (now, functools.partial(attend, blk, first, min(pairs, first + each)))
            )
            now += 1
        sent = max(sent + 1, now)
        schedule.append((sent, functools.partial(emit, blk)))
        schedule.append((sent + 1, functools.partial(summer.middle, blk)))
        schedule.append((sent + 4, functools.partial(summer.late, blk)))
        schedule.append((sent + 5, functools.partial(finish, blk)))
    schedule.sort(key=lambda item: item[0])
    length = max(pieces + gather.latency() + 1, sent + 6)

    for step in range(1, count):
        gain_copy(step).start()

    def body(time, _):
        gather.tick(time)
        pl.when(time == 0)(spread_gains)

        @pl.when(time < blocks)
        def _():
            norm_block(time)

        for when, work in schedule:
            pl.when(time == when)(work)
        return 0

    lax.fori_loop(0, length, body, 0)
    for blk in range(blocks):
        summer.drain(blk)
    for step in range(1, count):
        gain_copy(step).wait_send()


def attend(tokens, own, gain_rows, cols, rows_of, cosine, sine, depth, pieces, q_units, o_units):
    token_count, width = tokens.shape
    units, rows, _ = own.shape
    blocks, half = token_count // ROWS, ROWS // 2
    q_width = q_units * UNIT
    kv_width = UNIT // 2
    sum_bufs, sum_sems = TensorSum.scratch(blocks, half, width)
    count = depth * FOLD

    def out(*shape):
        return jax.ShapeDtypeStruct(shape, BF16)

    return pl.pallas_call(
        functools.partial(attend_kernel, (depth, pieces, q_units, o_units)),
        out_shape=(
            out(units, width, UNIT),
            out(token_count, width),
            out(token_count, q_width),
            out(token_count, kv_width),
            out(token_count, kv_width),
            out(token_count, q_width),
            out(token_count, width),
            out(token_count, width),
            jax.ShapeDtypeStruct((8, width), F32),
        ),
        in_specs=[VMEM_SPEC] * 7,
        out_specs=[HBM_SPEC] + [VMEM_SPEC] * 8,
        scratch_shapes=[
            VMEM((count, 8, rows), F32),
            VMEM((q_units + 1 + o_units, width, UNIT), BF16),
            VMEM((ROWS, token_count), F32),
            VMEM((blocks, ROWS, width), BF16),
            *sum_bufs,
            *sum_sems,
            *Gather.scratch(pieces, depth),
            DMA((count,)),
            DMA((count,)),
            DMA,
        ],
        compiler_params=pltpu.CompilerParams(
            collective_id=0, has_side_effects=True, vmem_limit_bytes=60 << 20
        ),
        name="attend",
    )(tokens, own, gain_rows, cols, rows_of, cosine, sine)


class Scatter:
    SLOTS = 4

    def __init__(self, place, rows, units, refs, lag, first=0):
        self.lag = lag
        self.place, self.rows, self.units, self.first = place, rows, units, first
        (
            self.grads,
            self.x_in,
            self.z_in,
            self.kept,
            self.mine,
            self.theirs,
            self.summed,
            self.x_send,
            self.x_recv,
            self.z_send,
            self.z_recv,
            self.load_sem,
            self.keep_sem,
        ) = refs

    @staticmethod
    def scratch(units, depth, rows):
        return [
            VMEM((depth, rows, UNIT), BF16),
            VMEM((depth, rows, UNIT), BF16),
            VMEM((Scatter.SLOTS, depth, rows, UNIT), BF16),
            DMA((units, depth)),
            DMA((units, depth)),
            DMA((units, depth)),
            DMA((units, depth)),
            DMA((2, depth)),
            DMA((Scatter.SLOTS,)),
        ]

    @staticmethod
    def outputs(units, everything, depth, rows):
        return (
            jax.ShapeDtypeStruct((units, depth, rows, UNIT), BF16),
            jax.ShapeDtypeStruct((everything, depth - 1, rows, UNIT), BF16),
            jax.ShapeDtypeStruct((everything, rows, UNIT), BF16),
        )

    def block(self, unit, index):
        start = pl.multiple_of(index * self.rows, self.rows)
        return self.grads.at[unit + self.first, pl.ds(start, self.rows)]

    def over(self, unit, zz):
        p = self.place
        return pltpu.make_async_remote_copy(
            self.block(unit, zz * FOLD + 1 - p.x),
            self.x_in.at[unit, zz],
            self.x_send.at[unit, zz],
            self.x_recv.at[unit, zz],
            device_id={"dp": p.partner},
            device_id_type=MESH,
        )

    def along(self, unit, step):
        p = self.place
        dest = lax.rem(p.z + step, p.depth)
        slot = lax.rem(unit, self.SLOTS)
        return pltpu.make_async_remote_copy(
            self.summed.at[slot, dest],
            self.z_in.at[unit + self.first, step - 1],
            self.z_send.at[unit, step],
            self.z_recv.at[unit, step],
            device_id={"dp": dest * FOLD + p.x},
            device_id_type=MESH,
        )

    def keep(self, unit):
        slot = lax.rem(unit, self.SLOTS)
        return pltpu.make_async_copy(
            self.summed.at[slot, self.place.z], self.kept.at[unit + self.first], self.keep_sem.at[slot]
        )

    def stage(self, step, unit):
        p = self.place

        @pl.when((unit >= 0) & (unit < self.units))
        def _():
            if step == 0:
                for zz in range(p.depth):
                    self.over(unit, zz).start()
            elif step == 1:
                loads = []
                for zz in range(p.depth):
                    loads.append(
                        pltpu.make_async_copy(
                            self.block(unit, zz * FOLD + p.x),
                            self.mine.at[zz],
                            self.load_sem.at[0, zz],
                        )
                    )
                    loads[-1].start()
                for zz in range(p.depth):
                    self.over(unit, zz).wait_recv()
                    loads.append(
                        pltpu.make_async_copy(
                            self.x_in.at[unit, zz], self.theirs.at[zz], self.load_sem.at[1, zz]
                        )
                    )
                    loads[-1].start()
                for copy in loads:
                    copy.wait()
                slot = lax.rem(unit, self.SLOTS)
                for zz in range(p.depth):
                    self.summed[slot, zz] = (
                        self.mine[zz].astype(F32) + self.theirs[zz].astype(F32)
                    ).astype(BF16)
                for way in range(1, p.depth):
                    self.along(unit, way).start()
                self.keep(unit).start()
            else:
                for zz in range(p.depth):
                    self.over(unit, zz).wait_send()
                for way in range(1, p.depth):
                    self.along(unit, way).wait_send()
                self.keep(unit).wait()

    def tick(self, time):
        self.stage(2, time - self.lag - 2)
        self.stage(0, time)
        self.stage(1, time - self.lag)

    def latency(self):
        return self.lag + 3

    def finish(self):
        def unit_end(unit, _):
            for way in range(1, self.place.depth):
                self.along(unit, way).wait_recv()
            return 0

        lax.fori_loop(0, self.units, unit_end, 0)


def feed_kernel(cfg, *refs):
    (
        b_ref,
        cot_ref,
        _,
        g_ref,
        grads_ref,
        x_in,
        z_in,
        kept,
        out_ref,
        db_ref,
        acc_out,
        acc_db,
        weights,
        grad_buf,
        hidden,
        dgu,
        part,
        weight_sem,
        grad_sem,
        z_send,
        z_recv,
        x_send,
        x_recv,
        *scatter_refs,
    ) = refs
    depth, first_unit, chunks, early, base, scatter_units, scatter_every = cfg
    place = Place(depth)
    token_count, width = b_ref.shape
    rows = x_in.shape[2]
    blocks = token_count // ROWS
    tall = 2 * ROWS
    scatter = Scatter(place, rows, scatter_units, (grads_ref, x_in, z_in, kept, *scatter_refs), 1)
    pieces = split(depth) * g_ref.shape[0] - base
    gather = Gather(place, g_ref, rows, pieces, (z_send, z_recv, x_send, x_recv), base)

    def load(chunk, matrix):
        slot = lax.rem(chunk, 2)
        return pltpu.make_async_copy(
            g_ref.at[first_unit + 3 * chunk + matrix],
            weights.at[slot, matrix],
            weight_sem.at[slot, matrix],
        )

    def save(chunk, matrix):
        slot = lax.rem(chunk, 2)
        return pltpu.make_async_copy(
            grad_buf.at[slot, matrix],
            grads_ref.at[3 * chunk + matrix],
            grad_sem.at[slot, matrix],
        )

    for matrix in range(3):
        load(0, matrix).start()
    place.enter()

    def clear(blk, _):
        rows_at = pl.ds(pl.multiple_of(blk * ROWS, ROWS), ROWS)
        acc_out[rows_at, :] = jnp.zeros((ROWS, width), F32)
        acc_db[rows_at, :] = jnp.zeros((ROWS, width), F32)
        return 0

    def hidden_rows(chunk, blk):
        slot = lax.rem(chunk, 2)
        rows_at = pl.ds(pl.multiple_of(blk * tall, tall), tall)
        stream, cot = b_ref[rows_at, :], cot_ref[rows_at, :]
        gate = dot(stream, weights[slot, 0])
        upper = dot(stream, weights[slot, 1])
        grad_hidden = dot(cot, weights[slot, 2])
        sigmoid = jax.nn.sigmoid(gate)
        silu = gate * sigmoid
        hid = (silu * upper).astype(BF16)
        grad_gate = (grad_hidden * upper * sigmoid * (1.0 + gate * (1.0 - sigmoid))).astype(BF16)
        grad_up = (grad_hidden * silu).astype(BF16)
        hidden[rows_at, :] = hid
        dgu[rows_at, :UNIT] = grad_gate
        dgu[rows_at, UNIT:] = grad_up

        def spread(piece, _):
            cols = pl.ds(pl.multiple_of(piece * tall, tall), tall)
            acc_out[rows_at, cols] += dot_nt(hidden[rows_at, :], weights[slot, 2, cols, :])
            acc_db[rows_at, cols] += dot_nt(dgu[rows_at, :UNIT], weights[slot, 0, cols, :]) + dot_nt(
                dgu[rows_at, UNIT:], weights[slot, 1, cols, :]
            )
            return 0

        lax.fori_loop(0, width // tall, spread, 0)

    def weight_grads(chunk):
        slot = lax.rem(chunk, 2)

        def grad_rows(blk, _):
            cols = pl.ds(pl.multiple_of(blk * ROWS, ROWS), ROWS)
            both = dot_tn(b_ref[:, cols], dgu[...])
            grad_buf[slot, 0, cols, :] = both[:, :UNIT].astype(BF16)
            grad_buf[slot, 1, cols, :] = both[:, UNIT:].astype(BF16)
            grad_buf[slot, 2, cols, :] = dot_tn(cot_ref[:, cols], hidden[...]).astype(BF16)
            return 0

        lax.fori_loop(0, width // ROWS, grad_rows, 0)
        for matrix in range(3):
            save(chunk, matrix).start()
        for matrix in range(3):
            save(chunk, matrix).wait()

    halves = token_count // tall
    steps = halves + 1
    ready = [3 * split(depth) * (late + 1) + gather.latency() for late in range(chunks - early)]
    start = max(ready[0], steps * early)
    spread_ticks = steps
    while any(start + spread_ticks * late < when for late, when in enumerate(ready)):
        spread_ticks += 1

    def stored_at(chunk):
        return steps * (chunk + 1) - 1 if chunk < early else (
            start + spread_ticks * (chunk - early) + steps - 1
        )

    scatter_from = max(
        stored_at(unit // 3) - scatter_every * unit for unit in range(scatter_units)
    )
    length = start + spread_ticks * (chunks - early - 1) + steps
    full_turns = -(-(length - scatter_from) // scatter_every)
    scatter_time = length + max(0, scatter_units + scatter.latency() - full_turns)

    def body(time, _):
        gather.tick(time)
        soon = time < steps * early
        since = time - start
        chunk = jnp.where(soon, time // steps, early + since // spread_ticks)
        step = jnp.where(soon, lax.rem(time, steps), lax.rem(since, spread_ticks))
        active = soon | ((since >= 0) & (step < steps) & (chunk < chunks))

        @pl.when(time == 0)
        def _():
            lax.fori_loop(0, blocks, clear, 0)

        @pl.when(active & (step == 0))
        def _():
            for matrix in range(3):
                load(chunk, matrix).wait()

        @pl.when(soon & (step == 0) & (chunk + 1 < early))
        def _():
            for matrix in range(3):
                load(chunk + 1, matrix).start()

        coming = since + 1

        @pl.when((coming >= 0) & (lax.rem(coming, spread_ticks) == 0))
        def _():
            later = early + coming // spread_ticks

            @pl.when(later < chunks)
            def _():
                for matrix in range(3):
                    load(later, matrix).start()

        @pl.when(active & (step < halves))
        def _():
            hidden_rows(chunk, step)

        @pl.when(active & (step == halves))
        def _():
            weight_grads(chunk)

        turn_at = time - scatter_from

        over = time - length

        @pl.when((over >= 0) | ((turn_at >= 0) & (lax.rem(turn_at, scatter_every) == 0)))
        def _():
            scatter.tick(jnp.where(over >= 0, full_turns + over, turn_at // scatter_every))

        return 0

    lax.fori_loop(0, max(length, scatter_time), body, 0)
    for which, (acc, target) in enumerate(((acc_db, db_ref), (acc_out, out_ref))):
        copies = []
        for blk in range(blocks):
            slot = blk % 2
            if blk >= 2:
                copies[blk - 2].wait()
            part[slot] = acc[blk * ROWS : (blk + 1) * ROWS, :].astype(BF16)
            copies.append(
                pltpu.make_async_copy(
                    part.at[slot], target.at[pl.ds(blk * ROWS, ROWS)], grad_sem.at[which, slot]
                )
            )
            copies[-1].start()
        for copy in copies[-2:]:
            copy.wait()
    scatter.finish()


def feed(b, cotangent, gathered, depth, cfg):
    first_unit, chunks, early, base, scatter_units, scatter_every = cfg
    token_count, width = b.shape
    everything = gathered.shape[0]
    rows = width // (depth * FOLD)
    full = jax.ShapeDtypeStruct((token_count, width), BF16)
    pieces = split(depth) * everything - base
    return pl.pallas_call(
        functools.partial(feed_kernel, (depth, *cfg)),
        out_shape=(
            jax.ShapeDtypeStruct(gathered.shape, BF16),
            jax.ShapeDtypeStruct((everything, width, UNIT), BF16),
            *Scatter.outputs(scatter_units, everything, depth, rows),
            full,
            full,
        ),
        in_specs=[VMEM_SPEC, VMEM_SPEC, HBM_SPEC],
        out_specs=[HBM_SPEC] * 7,
        scratch_shapes=[
            VMEM((token_count, width), F32),
            VMEM((token_count, width), F32),
            VMEM((2, 3, width, UNIT), BF16),
            VMEM((2, 3, width, UNIT), BF16),
            VMEM((token_count, UNIT), BF16),
            VMEM((token_count, 2 * UNIT), BF16),
            VMEM((2, ROWS, width), BF16),
            DMA((2, 3)),
            DMA((2, 3)),
            *Gather.scratch(pieces, depth),
            *Scatter.scratch(scatter_units, depth, rows),
        ],
        input_output_aliases={2: 0},
        compiler_params=pltpu.CompilerParams(
            collective_id=1, has_side_effects=True, vmem_limit_bytes=63 << 20
        ),
        name="feed",
    )(b, cotangent, gathered)


def back_kernel(cfg, *refs):
    (
        x_ref,
        q_ref,
        k_ref,
        v_ref,
        att_ref,
        cols_ref,
        rows_ref,
        cos_ref,
        sin_ref,
        gains,
        cot_ref,
        att_sum_ref,
        part_db_ref,
        part_out_ref,
        a_ref,
        g_ref,
        _,
        _,
        _,
        grads_ref,
        x_in,
        z_in,
        kept,
        dx_ref,
        sum_ref,
        gain_ref,
        dx2,
        low,
        weights,
        do,
        dq,
        dkv,
        dk,
        dv,
        part,
        half_in,
        half,
        far_in,
        total,
        back,
        far_db,
        far_out,
        piece,
        mask,
        grad_buf,
        right,
        gain_acc,
        gain_blocks,
        gain_land,
        sum_sends,
        sum_recvs,
        db_sends,
        db_recvs,
        out_sends,
        out_recvs,
        gain_send,
        gain_recv,
        load_sem,
        *scatter_refs,
    ) = refs
    depth, first_grad, scatter_units, q_units, o_units = cfg
    place = Place(depth)
    count = depth * FOLD
    token_count, width = x_ref.shape
    rows = x_in.shape[2]
    kv_width = k_ref.shape[1]
    blocks, short = token_count // ROWS, ROWS // 2
    scatter = Scatter(
        place, rows, scatter_units, (grads_ref, x_in, z_in, kept, *scatter_refs), 2, first_grad
    )
    feed_left = scatter_units - o_units - q_units - 1
    own_grads = first_grad + feed_left
    summer = TensorSum(place, part, (half_in, half, far_in, total, back), (sum_sends, sum_recvs))
    db_sum = StoredSum(
        place,
        part_db_ref,
        (half_in, half, far_db, total, back),
        (db_sends, db_recvs),
        piece,
        load_sem.at[0],
    )
    out_sum = StoredSum(
        place,
        part_out_ref,
        (half_in, half, far_out, total, back),
        (out_sends, out_recvs),
        piece,
        load_sem.at[0],
    )
    lane = lax.broadcasted_iota(jnp.int32, (1, LANES), 1)

    def fetch(pairs):
        copies = [
            pltpu.make_async_copy(src, dst, load_sem.at[number])
            for number, (src, dst) in enumerate(pairs)
        ]
        for copy in copies:
            copy.start()
        for copy in copies:
            copy.wait()

    gain_acc[...] = jnp.zeros_like(gain_acc)
    dk[...] = jnp.zeros_like(dk)
    dv[...] = jnp.zeros_like(dv)
    place.enter()

    def span(blk):
        return pl.ds(pl.multiple_of(blk * ROWS, ROWS), ROWS)

    def middle_grad(blk):
        fetch(
            ((cot_ref.at[span(blk)], part.at[0]), (att_sum_ref.at[span(blk)], part.at[1]))
        )
        for (row, values), inner in zip(db_sum.end(blk), (place.core, 1 - place.core)):
            at = pl.ds(row, short)
            inside = pl.ds(pl.multiple_of(inner * short, short), short)
            middle = x_ref[at, :].astype(F32) + part[1, inside, :].astype(F32)
            inverse = lax.rsqrt(jnp.mean(middle * middle, axis=-1, keepdims=True) + EPS_NORM)
            normal = middle * inverse
            grad = values[blk].astype(F32)
            gain_acc[1:2, :] += jnp.sum(grad * normal, axis=0, keepdims=True)
            scaled = grad * gains[1:2, :]
            centre = jnp.mean(scaled * normal, axis=-1, keepdims=True)
            result = part[0, inside, :].astype(F32) + inverse * (scaled - normal * centre)
            dx2[at, :] = result
            low[at, :] = result.astype(BF16)
        db_sum.drain(blk)
        at = span(blk)
        for unit in range(o_units):
            do[at, unit * UNIT : (unit + 1) * UNIT] = dot(low[at, :], weights[unit]).astype(BF16)

    def first_weights():
        fetch([(g_ref.at[q_units + 1 + unit], weights.at[unit]) for unit in range(o_units)])

    def save_grad(number):
        for unit in range(o_units):

            @pl.when(number == unit)
            def _():
                right[...] = att_ref[:, unit * UNIT : (unit + 1) * UNIT]

        for unit in range(q_units):

            @pl.when(number == o_units + unit)
            def _():
                right[...] = dq[:, unit * UNIT : (unit + 1) * UNIT]

        @pl.when(number == o_units + q_units)
        def _():
            right[...] = dkv[...]

        def block(blk, _):
            cols = span(blk)
            grad_buf[cols, :] = dot_tn(low[:, cols], right[...]).astype(BF16)
            return 0

        lax.fori_loop(0, width // ROWS, block, 0)
        fetch([(grad_buf, grads_ref.at[own_grads + number])])

    def second_weights():
        fetch(
            [(a_ref, low)]
            + [(g_ref.at[unit], weights.at[unit]) for unit in range(q_units + 1)]
        )

    def attention_heads(blk, first, last, stop):
        at = span(blk)

        @pl.when(first == 0)
        def _():
            key = lax.broadcasted_iota(jnp.int32, (stop, ROWS), 0)
            query_at = lax.broadcasted_iota(jnp.int32, (stop, ROWS), 1) + blk * ROWS
            same = cols_ref[:stop, 1:2] == rows_ref[0:1, at]
            allowed = (same & (key <= query_at)) | (key == query_at)
            mask[:stop, :] = jnp.where(allowed, 0.0, NEG_FILL)

        def head(index, _):
            lanes = pl.ds(pl.multiple_of(index // 2 * LANES, LANES), LANES)
            keep = lane // HEAD_SIZE == lax.rem(index, 2)
            query, grad = q_ref[at, lanes], do[at, lanes]
            query = jnp.where(keep, query, jnp.zeros_like(query))
            grad = jnp.where(keep, grad, jnp.zeros_like(grad))
            scores = dot_nt(k_ref[:stop, :], query) * HEAD_SIZE ** (-0.5)
            scores = jnp.where(mask[:stop, :] < 0, NEG_FILL, scores)
            expo = jnp.exp(scores - jnp.max(scores, axis=0, keepdims=True))
            probs = expo * (1.0 / jnp.sum(expo, axis=0, keepdims=True))
            grad_probs = dot_nt(v_ref[:stop, :], grad)
            centre = jnp.sum(probs * grad_probs, axis=0, keepdims=True)
            grad_scores = (probs * (grad_probs - centre)).astype(BF16)
            dv[:stop, :] += dot(probs.astype(BF16), grad)
            dk[:stop, :] += dot(grad_scores, query)
            out = dot_tn(grad_scores, k_ref[:stop, :]) * HEAD_SIZE ** (-0.5)
            out = turn(out, cos_ref[at, :], sin_ref[at, :], True).astype(BF16)
            dq[at, lanes] = jnp.where(keep, out, dq[at, lanes])
            return 0

        lax.fori_loop(first, last, head, 0)

    def input_part(blk):
        at = span(blk)
        dkv[at, :kv_width] = turn(
            dk[at, :] * HEAD_SIZE ** (-0.5), cos_ref[at, :], sin_ref[at, :], True
        ).astype(BF16)
        dkv[at, kv_width:] = dv[at, :].astype(BF16)
        out = dot_nt(dkv[at, :], weights[q_units])
        for unit in range(q_units):
            out = out + dot_nt(dq[at, unit * UNIT : (unit + 1) * UNIT], weights[unit])
        part[blk] = out.astype(BF16)
        summer.begin(blk)

    def finish(blk):
        for row, values in summer.end(blk):
            at = pl.ds(row, short)
            grad = values[blk].astype(F32)
            stream = x_ref[at, :].astype(F32)
            inverse = lax.rsqrt(jnp.mean(stream * stream, axis=-1, keepdims=True) + EPS_NORM)
            normal = stream * inverse
            gain_acc[0:1, :] += jnp.sum(grad * normal, axis=0, keepdims=True)
            scaled = grad * gains[0:1, :]
            centre = jnp.mean(scaled * normal, axis=-1, keepdims=True)
            dx2[at, :] += inverse * (scaled - normal * centre)
        summer.drain(blk)
        part[blk] = dx2[span(blk), :].astype(BF16)
        fetch([(part.at[blk], dx_ref.at[span(blk)])])

    def out_end(blk):
        fetch([(att_sum_ref.at[span(blk)], part.at[blk])])
        for (row, values), inner in zip(out_sum.end(blk), (place.core, 1 - place.core)):
            inside = pl.ds(pl.multiple_of(inner * short, short), short)
            part[blk, inside, :] = (
                x_ref[pl.ds(row, short), :].astype(F32)
                + part[blk, inside, :].astype(F32)
                + values[blk].astype(F32)
            ).astype(BF16)
        out_sum.drain(blk)
        fetch([(part.at[blk], sum_ref.at[span(blk)])])

    heads = q_ref.shape[1] // HEAD_SIZE
    swapped = 1 + blocks + o_units
    attention_at = 3
    parts_at = max(2 + blocks + attention_at - 1, swapped, 7)
    second_at = attention_at + 2 * blocks
    kv_at = max(second_at + q_units, parts_at + blocks)
    hold = max(
        0,
        swapped + 1 - feed_left,
        second_at + 1 - (feed_left + o_units),
        kv_at + 1 - (scatter_units - 1),
    )
    gains_at = parts_at + blocks + 4
    length = max(gains_at + 1, scatter_units + hold + scatter.latency())

    def each_block(work):
        def step(number, _):
            work(blocks - 1 - number)
            return 0

        lax.fori_loop(0, blocks, step, 0)

    def open_sums():
        each_block(db_sum.begin)
        first_weights()
        each_block(db_sum.middle)

    def attention_step(time):
        index = time - attention_at
        blk = blocks - 1 - index // 2
        first = lax.rem(index, 2) * (heads // 2)
        half_way = blocks // 2

        @pl.when(blk >= half_way)
        def _():
            attention_heads(blk, first, first + heads // 2, token_count)

        @pl.when(blk < half_way)
        def _():
            attention_heads(blk, first, first + heads // 2, token_count // 2)

    def steps(time):
        def blockwise(start, work):
            @pl.when((time >= start) & (time < start + blocks))
            def _():
                work(blocks - 1 - (time - start))

        pl.when(time == 0)(open_sums)
        blockwise(1, db_sum.late)
        blockwise(2, middle_grad)
        blockwise(3, out_sum.begin)
        blockwise(4, out_sum.middle)
        blockwise(6, out_sum.late)
        blockwise(7, out_end)

        @pl.when((time >= attention_at) & (time < second_at))
        def _():
            attention_step(time)

        o_at = swapped - o_units + 1
        number = jnp.where(
            time < second_at,
            time - o_at,
            jnp.where(time < second_at + q_units, time - second_at + o_units, o_units + q_units),
        )

        @pl.when(
            ((time >= o_at) & (time < o_at + o_units))
            | ((time >= second_at) & (time < second_at + q_units))
            | (time == kv_at)
        )
        def _():
            save_grad(number)

        pl.when(time == swapped)(second_weights)
        blockwise(parts_at, input_part)
        blockwise(parts_at + 1, summer.middle)
        blockwise(parts_at + 3, summer.late)
        blockwise(parts_at + 4, finish)

    def gain_copy(step):
        dest = lax.rem(place.me + step, count)
        return pltpu.make_async_remote_copy(
            gain_blocks.at[dest],
            gain_land.at[place.me],
            gain_send.at[step],
            gain_recv.at[place.me],
            device_id={"dp": dest},
            device_id_type=MESH,
        )

    def gain_arrival(source):
        return pltpu.make_async_remote_copy(
            gain_blocks.at[0],
            gain_land.at[source],
            gain_send.at[0],
            gain_recv.at[source],
            device_id={"dp": place.partner},
            device_id_type=MESH,
        )

    def send_gains():
        for source in range(count):
            gain_blocks[source] = gain_acc[:, source * rows : (source + 1) * rows]
        for step in range(1, count):
            gain_copy(step).start()

    def body(time, _):
        scatter.tick(time - hold)
        steps(time)
        pl.when(time == gains_at)(send_gains)
        return 0

    lax.fori_loop(0, length, body, 0)
    summed = gain_blocks[place.me]
    for step in range(1, count):
        source = lax.rem(place.me + step, count)
        gain_arrival(source).wait_recv()
        summed = summed + gain_land[source]
    gain_ref[...] = summed
    for step in range(1, count):
        gain_copy(step).wait_send()
    scatter.finish()


def attend_back(
    tokens, q, k, v, att, cols, rows_of, cosine, sine, gains, cotangent, att_sum, part_db,
    part_out, a, gathered, grads, z_in, kept, depth, first_grad, q_units, o_units,
):
    token_count, width = tokens.shape
    rows = width // (depth * FOLD)
    blocks, half = token_count // ROWS, ROWS // 2
    q_width, kv_width = q.shape[1], k.shape[1]
    scatter_units = grads.shape[0] - first_grad
    sum_bufs, sum_sems = TensorSum.scratch(blocks, half, width)
    count = depth * FOLD
    wide = max(q_units + 1, o_units)
    return pl.pallas_call(
        functools.partial(back_kernel, (depth, first_grad, scatter_units, q_units, o_units)),
        out_shape=(
            jax.ShapeDtypeStruct(grads.shape, BF16),
            *Scatter.outputs(scatter_units, grads.shape[0], depth, rows),
            jax.ShapeDtypeStruct((token_count, width), BF16),
            jax.ShapeDtypeStruct((token_count, width), BF16),
            jax.ShapeDtypeStruct((8, rows), F32),
        ),
        in_specs=[VMEM_SPEC] * 10 + [HBM_SPEC] * 9,
        out_specs=[HBM_SPEC] * 6 + [VMEM_SPEC],
        scratch_shapes=[
            VMEM((token_count, width), F32),
            VMEM((token_count, width), BF16),
            VMEM((wide, width, UNIT), BF16),
            VMEM((token_count, q_width), BF16),
            VMEM((token_count, q_width), BF16),
            VMEM((token_count, 2 * kv_width), BF16),
            VMEM((token_count, kv_width), F32),
            VMEM((token_count, kv_width), F32),
            VMEM((blocks, ROWS, width), BF16),
            *sum_bufs,
            VMEM((blocks, half, width), BF16),
            VMEM((blocks, half, width), BF16),
            VMEM((half, width), BF16),
            VMEM((token_count, ROWS), F32),
            VMEM((width, UNIT), BF16),
            VMEM((token_count, UNIT), BF16),
            VMEM((8, width), F32),
            VMEM((count, 8, rows), F32),
            VMEM((count, 8, rows), F32),
            *sum_sems,
            *sum_sems,
            *sum_sems,
            DMA((count,)),
            DMA((count,)),
            DMA((8,)),
            *Scatter.scratch(scatter_units, depth, rows),
        ],
        input_output_aliases={16: 0, 17: 2, 18: 3},
        compiler_params=pltpu.CompilerParams(
            collective_id=2, has_side_effects=True, vmem_limit_bytes=63 << 20
        ),
        name="attend_back",
    )(
        tokens, q, k, v, att, cols, rows_of, cosine, sine, gains, cotangent, att_sum, part_db,
        part_out, a, gathered, grads, z_in, kept,
    )


def settle_kernel(kept_ref, z_ref, gate_ref, up_ref, down_ref):
    steps = z_ref.shape[1]
    for number, out_ref in enumerate((gate_ref, up_ref, down_ref)):
        total = kept_ref[number].astype(F32)
        for step in range(steps):
            total = total + z_ref[number, step].astype(F32)
        out_ref[...] = total if number < 2 else total.T


def settle(kept, z_in, chunks):
    _, rows, cols = kept.shape
    steps = z_in.shape[1]
    wide = pl.BlockSpec((rows, cols), lambda i: (0, i))
    return pl.pallas_call(
        settle_kernel,
        grid=(chunks,),
        out_shape=(
            jax.ShapeDtypeStruct((rows, chunks * cols), F32),
            jax.ShapeDtypeStruct((rows, chunks * cols), F32),
            jax.ShapeDtypeStruct((chunks * cols, rows), F32),
        ),
        in_specs=[
            pl.BlockSpec((3, rows, cols), lambda i: (i, 0, 0)),
            pl.BlockSpec((3, steps, rows, cols), lambda i: (i, 0, 0, 0)),
        ],
        out_specs=[wide, wide, pl.BlockSpec((cols, rows), lambda i: (i, 0))],
        name="settle",
    )(kept, z_in)


def shards(
    depth,
    tokens,
    attention_gain,
    query_matrix,
    key_matrix,
    value_matrix,
    output_weight,
    feed_gain,
    gate_weight,
    up_weight,
    down_weight,
    sequence_lengths,
    block_mask,
    cotangent,
):
    token_count, width = tokens.shape
    rows, q_width = query_matrix.shape
    kv_width = key_matrix.shape[1]
    heads_kv = kv_width // HEAD_SIZE
    groups = q_width // kv_width
    feed_width = gate_weight.shape[1]
    chunks = feed_width // UNIT
    q_units = q_width // UNIT

    def pair(cols):
        return cols.reshape(-1, heads_kv, groups, HEAD_SIZE).swapaxes(1, 2).reshape(-1, q_width)

    def unpair(cols):
        return cols.reshape(-1, groups, heads_kv, HEAD_SIZE).swapaxes(1, 2).reshape(-1, q_width)

    def units_of(cols):
        return cols.reshape(rows, -1, UNIT).swapaxes(0, 1)

    feed_units = jnp.stack(
        [units_of(gate_weight), units_of(up_weight), units_of(down_weight.T)], axis=1
    ).reshape(3 * chunks, rows, UNIT)
    own = jnp.concatenate(
        [
            units_of(pair(query_matrix)),
            units_of(jnp.concatenate([key_matrix, value_matrix], axis=1)),
            units_of(pair(output_weight.T)),
            feed_units,
        ],
        axis=0,
    )
    sequence, position, valid = token_layout(sequence_lengths[0], token_count, BLOCK)
    query_code, key_code = slot_codes(sequence, valid, block_mask, BLOCK)
    cols = jnp.stack([query_code, key_code], axis=1)
    rows_of = jnp.stack([query_code, key_code], axis=0)
    cosine, sine = rope_tables(position, HEAD_SIZE)
    wide_cos = jnp.concatenate([cosine] * 4, axis=1)
    wide_sin = jnp.concatenate([-sine, sine] * 2, axis=1)
    gain_rows = jnp.concatenate(
        [
            attention_gain.astype(F32)[None],
            feed_gain.astype(F32)[None],
            jnp.zeros((6, rows), F32),
        ],
        axis=0,
    )
    first_unit = 2 * q_units + 1
    pieces = split(depth) * (first_unit + 3 * EARLY_CHUNKS)
    gathered, a, q, k, v, att, att_sum, b, gains = attend(
        tokens, own, gain_rows, cols, rows_of, wide_cos, wide_sin, depth, pieces, q_units, q_units
    )
    gathered, grads, _, z_in, kept, part_out, part_db = feed(
        b,
        cotangent,
        gathered,
        depth,
        (first_unit, chunks, EARLY_CHUNKS, pieces, EARLY_UNITS, SCATTER_EVERY),
    )
    _, _, z_in, kept, input_grad, block_output, gain_grads = attend_back(
        tokens, q, k, v, att, cols, rows_of, wide_cos, wide_sin, gains, cotangent, att_sum,
        part_db, part_out, a, gathered, grads, z_in, kept, depth, EARLY_UNITS, q_units, q_units,
    )
    gate_grad, up_grad, down_grad = settle(kept, z_in, chunks)
    late = kept[3 * chunks :].astype(F32) + jnp.sum(z_in[3 * chunks :].astype(F32), axis=1)

    def row_of(units):
        return units.swapaxes(0, 1).reshape(rows, -1)

    out_grad = row_of(late[:q_units]).T
    kv_grad = late[2 * q_units]
    out_grad = out_grad.reshape(groups, heads_kv, HEAD_SIZE, rows).swapaxes(0, 1)
    return (
        block_output,
        input_grad.astype(F32),
        gain_grads[0],
        unpair(row_of(late[q_units : 2 * q_units])),
        kv_grad[:, :kv_width],
        kv_grad[:, kv_width:],
        out_grad.reshape(q_width, rows),
        gain_grads[1],
        gate_grad,
        up_grad,
        down_grad,
    )


def solution(mesh):
    in_specs = (
        P("dp", None),
        P("dp"),
        P("dp", "tensor"),
        P("dp", "tensor"),
        P("dp", "tensor"),
        P("tensor", "dp"),
        P("dp"),
        P("dp", "tensor"),
        P("dp", "tensor"),
        P("tensor", "dp"),
        P("dp", None),
        P("dp", None),
        P("dp", None),
    )
    out_specs = (
        P("dp", None),
        P("dp", None),
        P("dp"),
        P("dp", "tensor"),
        P("dp", "tensor"),
        P("dp", "tensor"),
        P("tensor", "dp"),
        P("dp"),
        P("dp", "tensor"),
        P("dp", "tensor"),
        P("tensor", "dp"),
    )
    return jax.shard_map(
        functools.partial(shards, mesh.shape["dp"] // FOLD),
        mesh=mesh,
        in_specs=in_specs,
        out_specs=out_specs,
        check_vma=False,
    )
```

time: 877 us -> 810 us (0.924)
  Pallas kernels: 794 us -> 768 us
  local copies, waits for them, and re-layouts: 37.3 us -> 12 us
  other arithmetic: 38.1 us -> 22.2 us
    pallas_call x2 -> x3, Pallas kernels: 547 us -> 504 us  [the longest x1 279 us: attend(): pl.pallas_call(functools.partial(attend_kernel, (depth, pieces, q_units,...]
    pallas_call x1, Pallas kernels: 247 us -> 264 us  [attend_back(): pl.pallas_call(functools.partial(back_kernel, (depth, first_grad, scatter...]
    convert_element_type x3 -> x1, other arithmetic: 16.4 us -> 6.8 us  [shards(): input_grad.astype(F32)]
where the time goes in v4:
time: 810 us; the launch traced here: 803 us
  Pallas kernels  768 us (95%)
  other arithmetic  22.2 us (3%)
  local copies, waits for them, and re-layouts  12 us (1%)
    pallas_call x1, Pallas kernels, attend(): pl.pallas_call(functools.partial(attend_kernel, (depth, pieces, q_units,...  279 us
    pallas_call x1, Pallas kernels, attend_back(): pl.pallas_call(functools.partial(back_kernel, (depth, first_grad, scatter...  264 us
    pallas_call x1, Pallas kernels, feed(): pl.pallas_call(functools.partial(feed_kernel, (depth, *cfg)), out_shape=(...  216 us

profile of v4, /device:TPU:0, one launch (start us, length us, event | category | flops | bytes accessed | tf_op | source)
XLA Modules:
  0.0 803.2 jit_solution(10037772406595774174)
XLA Ops:
  0.7 0.9 select_reduce_fusion.2
  1.7 0.7 broadcast_in_dim.72
  2.4 0.7 broadcast_in_dim.73
  3.0 0.7 compare_bitcast_fusion
  4.0 0.7 maximum_maximum_fusion.refs_2_
  4.7 0.7 select_reduce_fusion.1
  5.5 0.6 pad_add_fusion.1.refs_4_.refs_6_
  6.1 0.9 maximum_bitcast_fusion
  7.0 1.1 copy.95
  8.2 1.0 copy.98
  9.2 0.8 copy.99
  10.1 1.0 copy.104.refs_3_.refs_5_
  11.1 0.5 copy.102
  11.6 1.9 fusion
  13.5 1.8 pad_maximum_fusion.2
  15.4 0.2 bitcast_bitcast_fusion
  15.6 0.3 pad_maximum_fusion.1
  16.0 0.6 copy-done.4
  16.6 2.0 pad_maximum_fusion.refs_1_
  18.6 278.6 %attend.1 = (bf16[29,2048,256]{2,1,0:T(8,128)(2,1)}, bf16[1024,2048]{1,0:T(8,128)(2,1)}, bf16[1024,512]{1,0:T(8,128)(2,1)}, bf16[1024,128]{1,0:T(8,128)(2,1)}, b...) custom-call(bf16[1024,2048]{1,0:T(8,128)(2,1)} %refs_0_.3, ...), custom_call_target="tpu_custom_call" | custom-call | tf_op jit(solution)/shard_map/attend/pallas_call | solution.py:580
  297.2 215.7 %feed.1 = (bf16[29,2048,256]{2,1,0:T(8,128)(2,1)}, bf16[29,2048,256]{2,1,0:T(8,128)(2,1)}, bf16[10,4,256,256]{3,2,1,0:T(8,128)(2,1)}, bf16[29,3,256,256]{3,2,1,0...) custom-call(bf16[1024,2048]{1,0:T(8,128)(2,1)} %get-tuple-element.40, ...), custom_call_target="tpu_custom_call", output_to_operand_aliasing={{0}: (2, {})} | custom-call | tf_op jit(solution)/shard_map/feed/pallas_call | solution.py:956
  512.9 264.2 %attend_back.1 = (bf16[29,2048,256]{2,1,0:T(8,128)(2,1)}, bf16[19,4,256,256]{3,2,1,0:T(8,128)(2,1)}, bf16[29,3,256,256]{3,2,1,0:T(8,128)(2,1)}, bf16[29,256,256]...) custom-call(bf16[1024,2048]{1,0:T(8,128)(2,1)} %refs_0_.3, ...), custom_call_target="tpu_custom_call", output_to_operand_aliasing={{0}: (16, {}), {2}: (17, {}), {3}: (18, {})} | custom-call | tf_op jit(solution)/shard_map/attend_back/pallas_call | solution.py:1364
  777.1 1.3 fusion.3
  778.4 2.0 convert_reduce_fusion
  780.4 9.5 %settle.1 = (f32[256,2048]{1,0:T(8,128)}, f32[256,2048]{1,0:T(8,128)}, f32[2048,256]{1,0:T(8,128)}) custom-call(bf16[29,256,256]{2,1,0:T(8,128)(2,1)} %get-tuple-element.52.kept_ref, bf16[29,3,256,256]{3,2,1,0:T(8,128)(2,1)} %get-tuple-element.53.z_ref), custom_call_target="tpu_custom_call" | custom-call | tf_op jit(solution)/shard_map/settle/pallas_call | solution.py:1427
  789.9 1.2 convert_add_fusion
  791.2 0.2 copy.108
  791.4 0.8 copy.109
  792.3 0.7 fusion.2
  793.2 1.0 copy.110
  794.2 6.8 convert_element_type.23
  801.0 2.0 copy.124
  (28 shorter events, 1.0 us)
Async XLA Ops:
  0.6 10.5 %copy-start.1 = (bf16[2048,256]{1,0:T(8,128)(2,1)S(1)}, bf16[2048,256]{1,0:T(8,128)(2,1)}, u32[]{:S(2)}) copy-start(bf16[2048,256]{1,0:T(8,128)(2,1)} %param.22) | copy-start | bytes 3145732
  9.2 6.2 copy-start.2
  11.6 3.8 copy-start.3
  15.6 1.0 copy-start.4
  794.2 6.8 copy-start

commit v5 on v4

--- a/solution.py
+++ b/solution.py
@@ -26,8 +26,9 @@
 BF16 = jnp.bfloat16
 
 
-EARLY_CHUNKS = 6
+EARLY_CHUNKS = 7
 EARLY_UNITS = 10
+ATTENTION_STEPS = 3
 SCATTER_EVERY = 2
 
 
@@ -1227,8 +1228,8 @@
     heads = q_ref.shape[1] // HEAD_SIZE
     swapped = 1 + blocks + o_units
     attention_at = 3
-    parts_at = max(2 + blocks + attention_at - 1, swapped, 7)
-    second_at = attention_at + 2 * blocks
+    parts_at = max(attention_at + (ATTENTION_STEPS - 1) * blocks, swapped, 7)
+    second_at = attention_at + ATTENTION_STEPS * blocks
     kv_at = max(second_at + q_units, parts_at + blocks)
     hold = max(
         0,
@@ -1253,17 +1254,19 @@
 
     def attention_step(time):
         index = time - attention_at
-        blk = blocks - 1 - index // 2
-        first = lax.rem(index, 2) * (heads // 2)
+        blk = blocks - 1 - index // ATTENTION_STEPS
+        some = -(-heads // ATTENTION_STEPS)
+        first = lax.rem(index, ATTENTION_STEPS) * some
+        last = jnp.minimum(first + some, heads)
         half_way = blocks // 2
 
         @pl.when(blk >= half_way)
         def _():
-            attention_heads(blk, first, first + heads // 2, token_count)
+            attention_heads(blk, first, last, token_count)
 
         @pl.when(blk < half_way)
         def _():
-            attention_heads(blk, first, first + heads // 2, token_count // 2)
+            attention_heads(blk, first, last, token_count // 2)
 
     def steps(time):
         def blockwise(start, work):

time: 810 us -> 801 us (0.989)
    pallas_call x1, Pallas kernels: 216 us -> 184 us  [feed(): pl.pallas_call(functools.partial(feed_kernel, (depth, *cfg)), out_shape=(...]
    pallas_call x1, Pallas kernels: 279 us -> 310 us  [attend(): pl.pallas_call(functools.partial(attend_kernel, (depth, pieces, q_units,...]
where the time goes in v5:
time: 801 us; the launch traced here: 795 us
  Pallas kernels  760 us (95%)
  other arithmetic  22.2 us (3%)
  local copies, waits for them, and re-layouts  12 us (1%)
    pallas_call x1, Pallas kernels, attend(): pl.pallas_call(functools.partial(attend_kernel, (depth, pieces, q_units,...  310 us
    pallas_call x1, Pallas kernels, attend_back(): pl.pallas_call(functools.partial(back_kernel, (depth, first_grad, scatter...  257 us
    pallas_call x1, Pallas kernels, feed(): pl.pallas_call(functools.partial(feed_kernel, (depth, *cfg)), out_shape=(...  184 us

profile of v5, /device:TPU:0, one launch (start us, length us, event | category | flops | bytes accessed | tf_op | source)
XLA Modules:
  0.0 794.9 jit_solution(2579485566772365114)
XLA Ops:
  0.7 0.9 select_reduce_fusion.2
  1.7 0.7 broadcast_in_dim.72
  2.4 0.7 broadcast_in_dim.73
  3.0 0.7 compare_bitcast_fusion
  4.0 0.7 maximum_maximum_fusion.refs_2_
  4.7 0.7 select_reduce_fusion.1
  5.5 0.6 pad_add_fusion.1.refs_4_.refs_6_
  6.1 0.9 maximum_bitcast_fusion
  7.0 1.1 copy.95
  8.2 1.0 copy.98
  9.2 0.8 copy.99
  10.1 1.0 copy.104.refs_3_.refs_5_
  11.1 0.5 copy.102
  11.6 1.9 fusion
  13.5 1.8 pad_maximum_fusion.2
  15.4 0.2 bitcast_bitcast_fusion
  15.6 0.3 pad_maximum_fusion.1
  16.0 0.6 copy-done.4
  16.6 2.0 pad_maximum_fusion.refs_1_
  18.6 309.8 %attend.1 = (bf16[29,2048,256]{2,1,0:T(8,128)(2,1)}, bf16[1024,2048]{1,0:T(8,128)(2,1)}, bf16[1024,512]{1,0:T(8,128)(2,1)}, bf16[1024,128]{1,0:T(8,128)(2,1)}, b...) custom-call(bf16[1024,2048]{1,0:T(8,128)(2,1)} %refs_0_.3, ...), custom_call_target="tpu_custom_call" | custom-call | tf_op jit(solution)/shard_map/attend/pallas_call | solution.py:581
  328.4 183.5 %feed.1 = (bf16[29,2048,256]{2,1,0:T(8,128)(2,1)}, bf16[29,2048,256]{2,1,0:T(8,128)(2,1)}, bf16[10,4,256,256]{3,2,1,0:T(8,128)(2,1)}, bf16[29,3,256,256]{3,2,1,0...) custom-call(bf16[1024,2048]{1,0:T(8,128)(2,1)} %get-tuple-element.40, ...), custom_call_target="tpu_custom_call", output_to_operand_aliasing={{0}: (2, {})} | custom-call | tf_op jit(solution)/shard_map/feed/pallas_call | solution.py:957
  511.9 256.8 %attend_back.1 = (bf16[29,2048,256]{2,1,0:T(8,128)(2,1)}, bf16[19,4,256,256]{3,2,1,0:T(8,128)(2,1)}, bf16[29,3,256,256]{3,2,1,0:T(8,128)(2,1)}, bf16[29,256,256]...) custom-call(bf16[1024,2048]{1,0:T(8,128)(2,1)} %refs_0_.3, ...), custom_call_target="tpu_custom_call", output_to_operand_aliasing={{0}: (16, {}), {2}: (17, {}), {3}: (18, {})} | custom-call | tf_op jit(solution)/shard_map/attend_back/pallas_call | solution.py:1367
  768.7 1.3 fusion.3
  770.1 2.0 convert_reduce_fusion
  772.1 9.5 %settle.1 = (f32[256,2048]{1,0:T(8,128)}, f32[256,2048]{1,0:T(8,128)}, f32[2048,256]{1,0:T(8,128)}) custom-call(bf16[29,256,256]{2,1,0:T(8,128)(2,1)} %get-tuple-element.52.kept_ref, bf16[29,3,256,256]{3,2,1,0:T(8,128)(2,1)} %get-tuple-element.53.z_ref), custom_call_target="tpu_custom_call" | custom-call | tf_op jit(solution)/shard_map/settle/pallas_call | solution.py:1430
  781.5 1.2 convert_add_fusion
  782.8 0.2 copy.108
  783.1 0.8 copy.109
  783.9 0.7 fusion.2
  784.9 1.0 copy.110
  785.9 6.8 convert_element_type.23
  792.7 2.0 copy.124
  (28 shorter events, 1.0 us)
Async XLA Ops:
  0.6 10.5 %copy-start.1 = (bf16[2048,256]{1,0:T(8,128)(2,1)S(1)}, bf16[2048,256]{1,0:T(8,128)(2,1)}, u32[]{:S(2)}) copy-start(bf16[2048,256]{1,0:T(8,128)(2,1)} %param.22) | copy-start | bytes 3145732
  9.2 6.2 copy-start.2
  11.6 3.8 copy-start.3
  15.6 1.0 copy-start.4
  785.9 6.8 copy-start
